TPU v7x, 128 devices: a whole 4x4x4 slice. The times are simulated.
128 devices in a mesh: gx: 16 (over y, z_lo, core), gy: 8 (over x, z_hi).
Axes of the slice: x: 4, y: 4, z: 4 (z_hi: 2, z_lo: 2; z = z_hi * 2 + z_lo), core: 2. Of those that a mesh axis runs over, the one named last changes fastest.
Arguments:
- density: float32 [512, 512, 128], P('gx', 'gy'), may hold values from 0 to 1
- transfer_table: int32 [4, 128], replicated, may hold values from 0 to 255
- shear_x: int32 [2, 512], P(None, 'gx'), may hold values from -16 to 15, as said below
- shear_y: int32 [2, 512], P(None, 'gy'), may hold values from -16 to 15, as said below
- direction: int32 [2, 2], replicated, may hold values from 0 to 1
Outputs:
- image_x: float32 [2, 4, 512, 128], P(None, None, ('gy', 'gx'))
- image_y: float32 [2, 4, 512, 128], P(None, None, ('gx', 'gy'))
Inputs may be any that keep to these rules, and one draw needn't show every extreme that they name: `shear_x`: the shift along z of a slice in a view. `shear_y`: the shift along z of a slice in a view.
All inputs are finite; a program needn't handle non-finite values.
Results may differ from a plain program's by a relative error of at most 0.0003.
Values sent between devices are 32-bit elements; how exact they have to be, the bound alone decides.
No kernel may reach another device: no remote copies, remote signals or barrier semaphores. Data moves between devices by JAX's collectives and lax.ppermute only.
A program may use at most 192 MiB of HBM per device.

v0:
```python
import functools

import jax
import jax.numpy as jnp
from jax import lax
from jax.experimental import pallas as pl
from jax.experimental.pallas import tpu as pltpu
from jax.sharding import PartitionSpec as P


SHEAR = 16
ROWS = 8
PIECE = 4
LOG2E = 1.4426950408889634
PACK = 1024.0
ROUNDER = 12582912.0
GROUP_X, GROUP_Y = 4, 2
UNROLL_C, UNROLL_X, UNROLL_Y = 4, 2, 8

SMEM = pl.BlockSpec(memory_space=pltpu.SMEM)
VMEM = pl.BlockSpec(memory_space=pltpu.VMEM)
HBM = pl.BlockSpec(memory_space=pltpu.HBM)
STAGES = ((1, 2, 4, 8), (1, 2, 4))


def slot_of(i, count):
    piece = i // PIECE
    return (piece % 2) * (count // 2) + (piece // 2) * PIECE + i % PIECE


def lane_take(values, index):
    numbers = lax.GatherDimensionNumbers(
        offset_dims=(), collapsed_slice_dims=(1,), start_index_map=(1,),
        operand_batching_dims=(0,), start_indices_batching_dims=(0,))
    return lax.gather(values, index[..., None], numbers, slice_sizes=(1, 1),
                      mode=lax.GatherScatterMode.PROMISE_IN_BOUNDS)


def load_kernel(stages, turn_ref, spot_ref, table_ref, density_ref, cells_ref, face_xa_ref,
                face_xb_ref, face_ya_ref, face_yb_ref, lut_ref, index_ref, mask_ref, ahead_ref,
                levels_ref, sem, table_sem):
    count_x, count_y, cells_z = density_ref.shape
    inner = cells_ref.at[pl.ds(1, count_x), pl.ds(ROWS, count_y), :]
    copy = pltpu.make_async_copy(density_ref, inner, sem)
    copy.start()
    table_copy = pltpu.make_async_copy(table_ref, levels_ref, table_sem)
    table_copy.start()

    lane = lax.broadcasted_iota(jnp.int32, (ROWS, cells_z), 1)
    row = lax.broadcasted_iota(jnp.int32, (ROWS, cells_z), 0)
    stage = 0
    for family, masks in enumerate(stages):
        turned = jnp.where(row < PIECE, turn_ref[family, 0], turn_ref[family, 1])
        for mask in masks:
            upper = jnp.where((spot_ref[family] & mask) != 0, 1, 0)
            ahead_ref[stage] = jnp.where(turned == upper, 1.0, 0.0)
            stage += 1

    def shifted(s, carry):
        source = lane - (s - SHEAR)
        kept = (source & -cells_z) == 0
        index_ref[s] = source & (cells_z - 1)
        mask_ref[s] = jnp.where(kept, -1.0, 0.0)
        mask_ref[s + 2 * SHEAR] = jnp.where(kept, 1.0, 0.0)
        return carry

    lax.fori_loop(0, 2 * SHEAR, shifted, 0, unroll=4)
    table_copy.wait()
    levels = levels_ref[...].astype(jnp.float32)
    for c in range(4):
        level = jnp.broadcast_to(levels[c:c + 1], (ROWS, cells_z))
        rise = jnp.where(lane == cells_z - 1, 0.0, pltpu.roll(level, cells_z - 1, 1) - level)
        lut_ref[c] = level + rise * (1.0 / PACK)
    copy.wait()

    odd_x, odd_y = (spot_ref[0] & 1) != 0, (spot_ref[1] & 1) != 0
    first, last = cells_ref[1, pl.ds(ROWS, count_y), :], cells_ref[count_x, pl.ds(ROWS, count_y), :]
    face_xa_ref[...] = jnp.where(odd_x, last, first)
    face_xb_ref[...] = jnp.where(odd_x, first, last)
    first, last = (cells_ref[pl.ds(1, count_x), ROWS, :],
                   cells_ref[pl.ds(1, count_x), ROWS + count_y - 1, :])
    face_ya_ref[...] = jnp.where(odd_y, last, first)
    face_yb_ref[...] = jnp.where(odd_y, first, last)


def classify_kernel(step_len, cells_ref, lut_ref, field_ref):
    count_x, cells_z = cells_ref.shape[0] - 2, cells_ref.shape[2]
    count_y = cells_ref.shape[1] - 2 * ROWS
    pitch = field_ref.shape[1] // count_x

    def body(i, carry):
        slot = slot_of(i, count_x) * pitch
        for base in range(0, count_y, ROWS):
            scaled = cells_ref[i + 1, pl.ds(ROWS + base, ROWS), :] * (cells_z - 1.0)
            knot = scaled.astype(jnp.int32)
            part = (scaled - knot.astype(jnp.float32)) * PACK - 1.0
            classed = []
            for c in range(4):
                packed = lane_take(lut_ref[c], knot)
                level = (packed + ROUNDER) - ROUNDER
                classed.append(packed + (packed - level) * part)
            optical = classed[3] * (2.0 * step_len * LOG2E / 255.0)
            opacity = (1.0 - jnp.exp2(-optical)) * (1.0 / 255.0)
            values = [classed[c] * opacity for c in range(3)] + [optical]
            for c in range(4):
                field_ref[c, pl.ds(slot + base, ROWS), :] = values[c]
        return carry

    lax.fori_loop(0, count_x, body, 0, unroll=UNROLL_C)


def march(fields, shift, turned, index_ref, mask_ref, states):
    place = shift + SHEAR
    index = index_ref[place]
    mask = mask_ref[place + jnp.where(turned, 2 * SHEAR, 0)]
    out = []
    for (red, green, blue, optical), state in zip(fields, states):
        depth = lane_take(optical, index) * mask
        after = state[0] + depth
        seen = jnp.exp2(jnp.where(turned, after, state[0])) * mask
        out.append((after, state[1] + seen * lane_take(red, index),
                    state[2] + seen * lane_take(green, index),
                    state[3] + seen * lane_take(blue, index)))
    return tuple(out)


def settle(turned, state):
    sign = jnp.where(turned, 1.0, -1.0)
    total = state[0] * sign
    fade = jnp.exp2(jnp.where(turned, -total, 0.0)) * sign
    return [state[1] * fade, state[2] * fade, state[3] * fade, total]


def x_kernel(group, turn_ref, spot_ref, shear_ref, face_xa_ref, face_xb_ref, face_ya_ref,
             face_yb_ref, field_ref, index_ref, mask_ref, _, keep_ref, give_ref, emit_ref,
             cells_ref):
    count_x, cells_z = cells_ref.shape[0] - 2, cells_ref.shape[2]
    count_y = cells_ref.shape[1] - 2 * ROWS
    pitch = field_ref.shape[1] // count_x
    pad = ROWS
    lane = lax.broadcasted_iota(jnp.int32, (ROWS, cells_z), 1)

    odd_x, odd_y = (spot_ref[0] & 1) != 0, (spot_ref[1] & 1) != 0
    cells_ref[0, pl.ds(pad, count_y), :] = jnp.where(odd_x, face_xb_ref[...], face_xa_ref[...])
    cells_ref[count_x + 1, pl.ds(pad, count_y), :] = jnp.where(odd_x, face_xa_ref[...],
                                                               face_xb_ref[...])
    low_y = jnp.where(odd_y, face_yb_ref[...], face_ya_ref[...])
    high_y = jnp.where(odd_y, face_ya_ref[...], face_yb_ref[...])
    for i in range(count_x):
        cells_ref[i + 1, pl.ds(pad - 1, 1), :] = low_y[i:i + 1]
        cells_ref[i + 1, pl.ds(pad + count_y, 1), :] = high_y[i:i + 1]

    turned = [turn_ref[0, v] != 0 for v in range(2)]
    zeros = jnp.zeros((ROWS, cells_z), jnp.float32)
    up, down = (lane + 1) & (cells_z - 1), (lane - 1) & (cells_z - 1)

    def shade(i, base):
        here = cells_ref[i + 1, pl.ds(base + pad, ROWS), :]
        diff_x = (cells_ref[i + 2, pl.ds(base + pad, ROWS), :]
                  - cells_ref[i, pl.ds(base + pad, ROWS), :])
        diff_y = (cells_ref[i + 1, pl.ds(base + pad + 1, ROWS), :]
                  - cells_ref[i + 1, pl.ds(base + pad - 1, ROWS), :])
        above = jnp.where(lane == cells_z - 1, 0.0, lane_take(here, up))
        below = jnp.where(lane == 0, 0.0, lane_take(here, down))
        diff_z = above - below
        side = diff_y + diff_z
        facing = jnp.abs(diff_x + (side + side))
        norm = diff_x * diff_x + diff_y * diff_y + diff_z * diff_z + 0.04
        return 0.3 + (0.7 / 3.0) * facing * lax.rsqrt(norm)

    def block_of(block, carry):
        base = pl.multiple_of(block * (ROWS * group), ROWS)

        def body(i, states):
            fields = []
            slot = slot_of(i, count_x) * pitch
            for g in range(group):
                shaded = shade(i, base + g * ROWS)
                row = slot + base + g * ROWS
                colours = [field_ref[c, pl.ds(row, ROWS), :] * shaded for c in range(3)]
                for c in range(3):
                    emit_ref[c, pl.ds(row, ROWS), :] = colours[c]
                fields.append((*colours, field_ref[3, pl.ds(row, ROWS), :]))
            return tuple(march(fields, shear_ref[v, i], turned[v], index_ref, mask_ref,
                               states[v]) for v in range(2))

        states = lax.fori_loop(0, count_x, body, (((zeros,) * 4,) * group,) * 2, unroll=UNROLL_X)
        for v in range(2):
            for g in range(group):
                for c, value in enumerate(settle(turned[v], states[v][g])):
                    even, odd = value[:PIECE], value[PIECE:]
                    spot, rows = block * group + g, pl.ds(PIECE * v, PIECE)
                    keep_ref[spot, c, rows, :] = jnp.where(odd_x, odd, even)
                    give_ref[spot, c, rows, :] = jnp.where(odd_x, even, odd)
        return carry

    lax.fori_loop(0, count_y // (ROWS * group), block_of, 0)


def y_kernel(group, kept, pitch, turn_ref, spot_ref, shear_ref, emit_ref, field_ref, index_ref, mask_ref,
             out_ref):
    cells_z = emit_ref.shape[-1]
    count_y = shear_ref.shape[1]
    size = out_ref.shape[0] * PIECE
    first = ((spot_ref[1] & 1) ^ (1 - kept)) * size
    turned = [turn_ref[1, v] != 0 for v in range(2)]
    zeros = jnp.zeros((ROWS, cells_z), jnp.float32)

    def block_of(block, carry):
        def body(j, states):
            fields = []
            for g in range(group):
                start = (first + (block * group + g) * ROWS) * pitch
                rows = pl.ds(start + j, ROWS, stride=pitch)
                fields.append((emit_ref[0, rows, :], emit_ref[1, rows, :], emit_ref[2, rows, :],
                               field_ref[3, rows, :]))
            return tuple(march(fields, shear_ref[v, j], turned[v], index_ref, mask_ref,
                               states[v]) for v in range(2))

        states = lax.fori_loop(0, count_y, body, (((zeros,) * 4,) * group,) * 2, unroll=UNROLL_Y)
        for v in range(2):
            for g in range(group):
                for c, value in enumerate(settle(turned[v], states[v][g])):
                    for half in range(2):
                        out_ref[2 * (block * group + g) + half, c, pl.ds(PIECE * v, PIECE), :] = (
                            value[PIECE * half:PIECE * (half + 1)])
        return carry

    lax.fori_loop(0, size // (ROWS * group), block_of, 0)


def options(micros, limit=16 << 20):
    return dict(
        compiler_params=pltpu.CompilerParams(vmem_limit_bytes=limit),
        cost_estimate=pl.CostEstimate(flops=0, transcendentals=0,
                                      bytes_accessed=int(micros * 3.5e6)))


def floats(*shape):
    return jax.ShapeDtypeStruct(shape, jnp.float32)


def load(density, transfer_table, direction, spot):
    count_x, count_y, cells_z = density.shape
    return pl.pallas_call(
        functools.partial(load_kernel, STAGES),
        out_shape=(floats(count_x + 2, count_y + 2 * ROWS, cells_z),
                   floats(count_y, cells_z), floats(count_y, cells_z),
                   floats(count_x, cells_z), floats(count_x, cells_z),
                   floats(4, ROWS, cells_z),
                   jax.ShapeDtypeStruct((2 * SHEAR, ROWS, cells_z), jnp.int32),
                   floats(4 * SHEAR, ROWS, cells_z),
                   floats(sum(map(len, STAGES)), ROWS, cells_z)),
        in_specs=[SMEM, SMEM, HBM, HBM],
        out_specs=(VMEM,) * 9,
        scratch_shapes=[pltpu.VMEM(transfer_table.shape, jnp.int32), pltpu.SemaphoreType.DMA,
                        pltpu.SemaphoreType.DMA],
        name="load",
        **options(2),
    )(direction, spot, transfer_table, density)


def classify(cells, lut, step_len):
    count_x, count_y, cells_z = cells.shape[0] - 2, cells.shape[1] - 2 * ROWS, cells.shape[2]
    return pl.pallas_call(
        functools.partial(classify_kernel, step_len),
        out_shape=floats(4, count_x * (count_y + 1), cells_z),
        in_specs=[VMEM, VMEM],
        out_specs=VMEM,
        name="classify",
        **options(3),
    )(cells, lut)


def x_march(cells, halo, field, shifts, shear_x, direction, spot):
    count_y, cells_z = cells.shape[1] - 2 * ROWS, cells.shape[2]
    part = floats(count_y // (2 * PIECE), 4, 2 * PIECE, cells_z)
    keep, give, emitted, _ = pl.pallas_call(
        functools.partial(x_kernel, GROUP_X),
        out_shape=(part, part, floats(3, *field.shape[1:]), floats(*cells.shape)),
        in_specs=[SMEM] * 3 + [VMEM] * 8,
        out_specs=(VMEM,) * 4,
        input_output_aliases={10: 3},
        name="x_march",
        **options(8),
    )(direction, spot, shear_x, *halo, field, *shifts, cells)
    return keep, give, emitted


def y_march(emitted, field, shifts, shear_y, direction, spot, count_x, kept):
    cells_z = field.shape[-1]
    return pl.pallas_call(
        functools.partial(y_kernel, GROUP_Y, kept, field.shape[1] // count_x),
        out_shape=floats(count_x // (2 * PIECE), 4, 2 * PIECE, cells_z),
        in_specs=[SMEM] * 3 + [VMEM] * 4,
        out_specs=VMEM,
        **options(2.5),
    )(direction, spot, shear_y, emitted, field, *shifts)


def neighbours(axis, offset):
    count = lax.axis_size(axis)
    pairs = [(i, i + 1) for i in range(offset, count - 1, 2)]
    return pairs + [(target, source) for source, target in pairs]


def swapped(axis, mask):
    return [(i, i ^ mask) for i in range(lax.axis_size(axis))]


def stage_kernel(family, mask, order, split, spot_ref, keep_ref, got_ref, ahead_ref, *out_refs):
    me = spot_ref[family]
    mine_ahead = ahead_ref[order] > 0.5

    def joined(p):
        mine, theirs = [[ref[p, c] for c in range(4)] for ref in (keep_ref, got_ref)]
        seen = jnp.exp2(-jnp.where(mine_ahead, mine[3], theirs[3]))
        near, far = jnp.where(mine_ahead, 1.0, seen), jnp.where(mine_ahead, seen, 1.0)
        return [mine[c] * near + theirs[c] * far for c in range(3)] + [mine[3] + theirs[3]]

    parts = [joined(p) for p in range(keep_ref.shape[0])]
    if split == "image":
        red, green, blue, total = parts[0]
        for c, value in enumerate((red, green, blue, 1.0 - jnp.exp2(-total))):
            for v in range(2):
                out_refs[0][v, c] = value[PIECE * v:PIECE * (v + 1)]
        return
    pick = lambda flag, a, b: [jnp.where(flag, one, two) for one, two in zip(a, b)]
    if split == "pair":
        high = (me & mask) != 0
        pairs = list(zip(parts[::2], parts[1::2]))
        keep = [pick(high, b, a) for a, b in pairs]
        give = [pick(high, a, b) for a, b in pairs]
    elif split == "ring_first":
        upper = (me & (2 * mask)) != 0
        edge = ((me // mask + me // (2 * mask)) & 1) == 0
        ends, middle = (parts[0], parts[3]), (parts[1], parts[2])
        small, large = [pick(edge, ends[k], middle[k]) for k in range(2)]
        keep = [pick(upper, large, small), pick(upper, small, large)]
        small, large = [pick(edge, middle[k], ends[k]) for k in range(2)]
        give = [pick(upper, large, small), pick(upper, small, large)]
    else:
        keep, give = parts[:1], parts[1:]
    for ref, pieces in zip(out_refs, (keep, give)):
        for p, piece in enumerate(pieces):
            for c in range(4):
                ref[p, c] = piece[c]


class Exchange:
    def __init__(self, family, axis, ahead, spot):
        self.family, self.axis, self.ahead, self.spot = family, axis, ahead, spot
        self.stage = 0

    def send(self, keep, give, mask):
        self.keep, self.stage = keep, self.stage + 1
        self.got = lax.ppermute(give, self.axis, swapped(self.axis, mask))

    def meet(self, split, mask=0):
        count, *rest = self.keep.shape
        if split == "image":
            shape = floats(2, 4, PIECE, rest[-1])
        else:
            shape = (floats(count // 2, *rest),) * 2
        order = self.family * len(STAGES[0]) + self.stage - 1
        return pl.pallas_call(
            functools.partial(stage_kernel, self.family, mask, order, split),
            out_shape=shape,
            in_specs=[SMEM] + [VMEM] * 3,
            out_specs=VMEM if split == "image" else (VMEM, VMEM),
            **options(0.3),
        )(self.spot, self.keep, self.got, self.ahead)


def local(density, transfer_table, shear_x, shear_y, direction):
    count_x = density.shape[0]
    step_len = 1.0 / (count_x * lax.axis_size("gx"))
    spot = jnp.stack([lax.axis_index("gx"), lax.axis_index("gy")]).astype(jnp.int32)
    cells, *faces, lut, index, mask, ahead = load(density, transfer_table, direction, spot)
    shifts = (index, mask)
    halo = [lax.ppermute(face, axis, neighbours(axis, offset)) for face, axis, offset in
            zip(faces, ("gx", "gx", "gy", "gy"), (1, 0, 1, 0))]
    field = classify(cells, lut, step_len)
    keep_x, give_x, emitted = x_march(cells, halo, field, shifts, shear_x, direction, spot)

    x, y = Exchange(0, "gx", ahead, spot), Exchange(1, "gy", ahead, spot)
    x.send(keep_x, give_x, 1)
    given = y_march(emitted, field, shifts, shear_y, direction, spot, count_x, 0)
    kept = y_march(emitted, field, shifts, shear_y, direction, spot, count_x, 1)
    x.send(*x.meet("pair", 2), 2)
    y.send(kept, given, 1)
    x.send(*x.meet("ring_first", 4), 4)
    x.send(*x.meet("ring_second"), 12)
    y.send(*y.meet("ring_first", 2), 2)
    image_x = x.meet("image")
    y.send(*y.meet("ring_second"), 6)
    return image_x, y.meet("image")


def solution(mesh):
    placed = (P("gx", "gy", None), P(), P(None, "gx"), P(None, "gy"), P())
    return jax.shard_map(
        local,
        mesh=mesh,
        in_specs=placed,
        out_specs=(P(None, None, ("gy", "gx"), None), P(None, None, ("gx", "gy"), None)),
        check_vma=False,
    )
```

profile of v0, /device:TPU:24, one launch (start us, length us, event | category | flops | bytes accessed | tf_op | source)
XLA Modules:
  0.0 51.7 jit_solution(13714790772636157727)
XLA Ops:
  0.6 0.1 pad_add_fusion.spot_ref
  0.7 0.0 copy-start
  0.7 1.2 %copy-done = f32[32,64,128]{2,1,0:T(8,128)S(1)} copy-done((f32[32,64,128]{2,1,0:T(8,128)S(1)}, f32[32,64,128]{2,1,0:T(8,128)}, u32[]{:S(2)}) %copy-start) | copy-done | bytes 1048600
  1.9 0.0 copy-start.1
  1.9 0.7 %copy-done.1 = s32[2,2]{1,0:T(2,128)S(1)} copy-done((s32[2,2]{1,0:T(2,128)S(1)}, s32[2,2]{1,0:T(2,128)}, u32[]{:S(2)}) %copy-start.1) | copy-done | bytes 40
  2.6 0.0 copy-start.3
  2.6 0.7 %copy-done.3 = s32[4,128]{1,0:T(4,128)S(1)} copy-done((s32[4,128]{1,0:T(4,128)S(1)}, s32[4,128]{1,0:T(4,128)}, u32[]{:S(2)}) %copy-start.3) | copy-done | bytes 2072
  3.3 0.0 copy-start.4
  3.3 0.8 %load.1 = (f32[34,80,128]{2,1,0:T(8,128)S(1)}, f32[64,128]{1,0:T(8,128)S(1)}, f32[64,128]{1,0:T(8,128)S(1)}, f32[32,128]{1,0:T(8,128)S(1)}, f32[32,128]{1,0:T(8,...) custom-call(s32[2,2]{1,0:T(2,128)S(1)} %copy-done.1, ...), custom_call_target="tpu_custom_call" | custom-call | bytes 7000000 | tf_op jit(solution)/shard_map/load/pallas_call | solution.py:245
  4.1 3.4 %collective-permute-start = (f32[64,128]{1,0:T(8,128)S(1)}, f32[64,128]{1,0:T(8,128)S(1)}, u32[]{:S(2)}, u32[]{:S(2)}) collective-permute-start(f32[64,128]{1,0:T(8,128)S(1)} %get-tuple-element.24), channel_id=1, source_target_pairs={{8,16},{24,32},{40,48},{56,64},{72,80},{88,96},{104,112},{16,8},{3... | collective-permute-start | bytes 98312 | tf_op jit(solution)/shard_map/ppermute | solution.py:381
  7.6 0.6 %collective-permute-start.1 = (f32[64,128]{1,0:T(8,128)S(1)}, f32[64,128]{1,0:T(8,128)S(1)}, u32[]{:S(2)}, u32[]{:S(2)}) collective-permute-start(f32[64,128]{1,0:T(8,128)S(1)} %get-tuple-element.25), channel_id=1, source_target_pairs={{0,8},{16,24},{32,40},{48,56},{64,72},{80,88},{96,104},{112,120},{... | collective-permute-start | bytes 98312 | tf_op jit(solution)/shard_map/ppermute | solution.py:381
  8.2 0.7 %collective-permute-start.2 = (f32[32,128]{1,0:T(8,128)S(1)}, f32[32,128]{1,0:T(8,128)S(1)}, u32[]{:S(2)}, u32[]{:S(2)}) collective-permute-start(f32[32,128]{1,0:T(8,128)S(1)} %get-tuple-element.26), channel_id=1, source_target_pairs={{1,2},{3,4},{5,6},{2,1},{4,3},{6,5},{9,10},{11,12},{13,14},{10,9},... | collective-permute-start | bytes 49160 | tf_op jit(solution)/shard_map/ppermute | solution.py:381
  8.8 5.8 %collective-permute-start.3 = (f32[32,128]{1,0:T(8,128)S(1)}, f32[32,128]{1,0:T(8,128)S(1)}, u32[]{:S(2)}, u32[]{:S(2)}) collective-permute-start(f32[32,128]{1,0:T(8,128)S(1)} %get-tuple-element.27), channel_id=1, source_target_pairs={{0,1},{2,3},{4,5},{6,7},{1,0},{3,2},{5,4},{7,6},{8,9},{10,11},{12,... | collective-permute-start | bytes 49160 | tf_op jit(solution)/shard_map/ppermute | solution.py:381
  14.6 2.6 %classify.1.field_ref = f32[4,2080,128]{2,1,0:T(8,128)S(1)} custom-call(f32[34,80,128]{2,1,0:T(8,128)S(1)} %get-tuple-element.28.cells_ref._, f32[4,8,128]{2,1,0:T(8,128)S(1)} %get-tuple-element.29.lut_ref), custom_call_target="tpu_custom_call" | custom-call | bytes 10500000 | tf_op jit(solution)/shard_map/classify/pallas_call | solution.py:265
  17.2 0.0 copy-start.2
  17.2 0.0 collective-permute-done.2.face_ya_ref
  17.2 0.0 collective-permute-done.3.face_yb_ref
  17.2 0.0 collective-permute-done.face_xa_ref
  17.2 0.0 collective-permute-done.1.face_xb_ref
  17.2 0.0 copy-done.4
  17.2 8.4 %x_march.1 = (f32[8,4,8,128]{3,2,1,0:T(8,128)S(1)}, f32[8,4,8,128]{3,2,1,0:T(8,128)S(1)}, f32[3,2080,128]{2,1,0:T(8,128)S(1)}, f32[34,80,128]{2,1,0:T(8,128)S(1)}) custom-call(s32[2,2]{1,0:T(2,128)S(1)} %copy-done.1, s32[2]{0:T(128)S(1)} %pad_add_fusion.spot_ref, s32[2,32]{1,0:T(2,128)S(1)} %copy-done.4, ...), custom_call_target="tpu_custom_call", output_to_operand_aliasing={{3}: (10, {})} | custom-call | bytes 28000000 | tf_op jit(solution)/shard_map/x_march/pallas_call | solution.py:278
  25.6 0.1 collective-permute-start.4
  25.7 0.0 copy-done.2
  25.7 2.7 %shard_map.73 = f32[4,4,8,128]{3,2,1,0:T(8,128)S(1)} custom-call(s32[2,2]{1,0:T(2,128)S(1)} %copy-done.1, s32[2]{0:T(128)S(1)} %pad_add_fusion.spot_ref, s32[2,64]{1,0:T(2,128)S(1)} %copy-done.2, f32[3,2080,128]{2,1,0:T(8,128)S(1)} %get-tuple-element.41.emit_ref, f32[4,2080,128]{2,1,0:T(8,128)S(1)} %classify.1.field_ref, ...), custom_call_target="tpu_custom_call" | custom-call | bytes 8750000 | tf_op jit(solution)/shard_map/pallas_call | solution.py:292
  28.4 2.8 %collective-permute-start.8 = (f32[4,4,8,128]{3,2,1,0:T(8,128)S(1)}, f32[4,4,8,128]{3,2,1,0:T(8,128)S(1)}, u32[]{:S(2)}, u32[]{:S(2)}) collective-permute-start(f32[4,4,8,128]{3,2,1,0:T(8,128)S(1)} %shard_map.73), channel_id=1, source_target_pairs={{0,1},{1,0},{2,3},{3,2},{4,5},{5,4},{6,7},{7,6},{8,9},{9,8},{10,11... | collective-permute-start | bytes 196616 | tf_op jit(solution)/shard_map/ppermute | solution.py:357
  31.2 0.0 collective-permute-done.4.got_ref
  31.2 0.6 %shard_map.68 = (f32[4,4,8,128]{3,2,1,0:T(8,128)S(1)}, f32[4,4,8,128]{3,2,1,0:T(8,128)S(1)}) custom-call(s32[2]{0:T(128)S(1)} %pad_add_fusion.spot_ref, f32[8,4,8,128]{3,2,1,0:T(8,128)S(1)} %get-tuple-element.32.keep_ref, f32[8,4,8,128]{3,2,1,0:T(8,128)S(1)} %collective-permute-done.4.got_ref, f32[7,8,128]{2,1,0:T(8,128)S(1)} %get-tuple-element.34.ahead_ref), custom_call_target="tpu_custom_call" | custom-call | bytes 1050000 | tf_op jit(solution)/shard_map/pallas_call | solution.py:366
  31.8 0.1 collective-permute-start.5
  31.9 2.7 %shard_map.72.keep_ref = f32[4,4,8,128]{3,2,1,0:T(8,128)S(1)} custom-call(s32[2,2]{1,0:T(2,128)S(1)} %copy-done.1, s32[2]{0:T(128)S(1)} %pad_add_fusion.spot_ref, s32[2,64]{1,0:T(2,128)S(1)} %copy-done.2, f32[3,2080,128]{2,1,0:T(8,128)S(1)} %get-tuple-element.41.emit_ref, f32[4,2080,128]{2,1,0:T(8,128)S(1)} %classify.1.field_ref, ...), custom_call_target="tpu_custom_call" | custom-call | bytes 8750000 | tf_op jit(solution)/shard_map/pallas_call | solution.py:292
  34.6 0.4 collective-permute-done.8.got_ref
  35.0 0.6 %shard_map.74 = (f32[2,4,8,128]{3,2,1,0:T(8,128)S(1)}, f32[2,4,8,128]{3,2,1,0:T(8,128)S(1)}) custom-call(s32[2]{0:T(128)S(1)} %pad_add_fusion.spot_ref, f32[4,4,8,128]{3,2,1,0:T(8,128)S(1)} %shard_map.72.keep_ref, f32[4,4,8,128]{3,2,1,0:T(8,128)S(1)} %collective-permute-done.8.got_ref, f32[7,8,128]{2,1,0:T(8,128)S(1)} %get-tuple-element.34.ahead_ref), custom_call_target="tpu_custom_call" | custom-call | bytes 1050000 | tf_op jit(solution)/shard_map/pallas_call | solution.py:366
  35.6 3.3 %collective-permute-start.9 = (f32[2,4,8,128]{3,2,1,0:T(8,128)S(1)}, f32[2,4,8,128]{3,2,1,0:T(8,128)S(1)}, u32[]{:S(2)}, u32[]{:S(2)}) collective-permute-start(f32[2,4,8,128]{3,2,1,0:T(8,128)S(1)} %get-tuple-element.43), channel_id=1, source_target_pairs={{0,2},{1,3},{2,0},{3,1},{4,6},{5,7},{6,4},{7,5},{8,10},{9,11},{10,... | collective-permute-start | bytes 98312 | tf_op jit(solution)/shard_map/ppermute | solution.py:357
  38.9 0.0 collective-permute-done.5.got_ref
  38.9 0.6 %shard_map.69 = (f32[2,4,8,128]{3,2,1,0:T(8,128)S(1)}, f32[2,4,8,128]{3,2,1,0:T(8,128)S(1)}) custom-call(s32[2]{0:T(128)S(1)} %pad_add_fusion.spot_ref, f32[4,4,8,128]{3,2,1,0:T(8,128)S(1)} %get-tuple-element.35.keep_ref, f32[4,4,8,128]{3,2,1,0:T(8,128)S(1)} %collective-permute-done.5.got_ref, f32[7,8,128]{2,1,0:T(8,128)S(1)} %get-tuple-element.34.ahead_ref), custom_call_target="tpu_custom_call" | custom-call | bytes 1050000 | tf_op jit(solution)/shard_map/pallas_call | solution.py:366
  39.4 0.3 collective-permute-start.6
  39.8 1.0 %collective-permute-done.9.got_ref = f32[2,4,8,128]{3,2,1,0:T(8,128)S(1)} collective-permute-done((f32[2,4,8,128]{3,2,1,0:T(8,128)S(1)}, f32[2,4,8,128]{3,2,1,0:T(8,128)S(1)}, u32[]{:S(2)}, u32[]{:S(2)}) %collective-permute-start.9) | collective-permute-done | bytes 32800 | tf_op jit(solution)/shard_map/ppermute | solution.py:357
  40.7 0.6 %shard_map.75 = (f32[1,4,8,128]{3,2,1,0:T(8,128)S(1)}, f32[1,4,8,128]{3,2,1,0:T(8,128)S(1)}) custom-call(s32[2]{0:T(128)S(1)} %pad_add_fusion.spot_ref, f32[2,4,8,128]{3,2,1,0:T(8,128)S(1)} %get-tuple-element.42.keep_ref, f32[2,4,8,128]{3,2,1,0:T(8,128)S(1)} %collective-permute-done.9.got_ref, f32[7,8,128]{2,1,0:T(8,128)S(1)} %get-tuple-element.34.ahead_ref), custom_call_target="tpu_custom_call" | custom-call | bytes 1050000 | tf_op jit(solution)/shard_map/pallas_call | solution.py:366
  41.3 3.7 %collective-permute-start.10 = (f32[1,4,8,128]{3,2,1,0:T(8,128)S(1)}, f32[1,4,8,128]{3,2,1,0:T(8,128)S(1)}, u32[]{:S(2)}, u32[]{:S(2)}) collective-permute-start(f32[1,4,8,128]{3,2,1,0:T(8,128)S(1)} %get-tuple-element.45), channel_id=1, source_target_pairs={{0,6},{1,7},{2,4},{3,5},{4,2},{5,3},{6,0},{7,1},{8,14},{9,15},{10,... | collective-permute-start | bytes 49160 | tf_op jit(solution)/shard_map/ppermute | solution.py:357
  45.0 0.0 collective-permute-done.6.got_ref
  45.0 0.6 %shard_map.70 = (f32[1,4,8,128]{3,2,1,0:T(8,128)S(1)}, f32[1,4,8,128]{3,2,1,0:T(8,128)S(1)}) custom-call(s32[2]{0:T(128)S(1)} %pad_add_fusion.spot_ref, f32[2,4,8,128]{3,2,1,0:T(8,128)S(1)} %get-tuple-element.37.keep_ref, f32[2,4,8,128]{3,2,1,0:T(8,128)S(1)} %collective-permute-done.6.got_ref, f32[7,8,128]{2,1,0:T(8,128)S(1)} %get-tuple-element.34.ahead_ref), custom_call_target="tpu_custom_call" | custom-call | bytes 1050000 | tf_op jit(solution)/shard_map/pallas_call | solution.py:366
  45.5 0.1 collective-permute-start.7
  45.6 1.1 %collective-permute-done.10.got_ref = f32[1,4,8,128]{3,2,1,0:T(8,128)S(1)} collective-permute-done((f32[1,4,8,128]{3,2,1,0:T(8,128)S(1)}, f32[1,4,8,128]{3,2,1,0:T(8,128)S(1)}, u32[]{:S(2)}, u32[]{:S(2)}) %collective-permute-start.10) | collective-permute-done | bytes 16416 | tf_op jit(solution)/shard_map/ppermute | solution.py:357
  46.7 1.2 %shard_map.76 = f32[2,4,4,128]{3,2,1,0:T(4,128)} custom-call(s32[2]{0:T(128)S(1)} %pad_add_fusion.spot_ref, f32[1,4,8,128]{3,2,1,0:T(8,128)S(1)} %get-tuple-element.44.keep_ref, f32[1,4,8,128]{3,2,1,0:T(8,128)S(1)} %collective-permute-done.10.got_ref, f32[7,8,128]{2,1,0:T(8,128)S(1)} %get-tuple-element.34.ahead_ref), custom_call_target="tpu_custom_call" | custom-call | bytes 1050000 | tf_op jit(solution)/shard_map/pallas_call | solution.py:366
  47.8 2.7 %collective-permute-done.7.got_ref = f32[1,4,8,128]{3,2,1,0:T(8,128)S(1)} collective-permute-done((f32[1,4,8,128]{3,2,1,0:T(8,128)S(1)}, f32[1,4,8,128]{3,2,1,0:T(8,128)S(1)}, u32[]{:S(2)}, u32[]{:S(2)}) %collective-permute-start.7) | collective-permute-done | bytes 16416 | tf_op jit(solution)/shard_map/ppermute | solution.py:357
  50.6 1.2 %shard_map.71 = f32[2,4,4,128]{3,2,1,0:T(4,128)} custom-call(s32[2]{0:T(128)S(1)} %pad_add_fusion.spot_ref, f32[1,4,8,128]{3,2,1,0:T(8,128)S(1)} %get-tuple-element.39.keep_ref, f32[1,4,8,128]{3,2,1,0:T(8,128)S(1)} %collective-permute-done.7.got_ref, f32[7,8,128]{2,1,0:T(8,128)S(1)} %get-tuple-element.34.ahead_ref), custom_call_target="tpu_custom_call" | custom-call | bytes 1050000 | tf_op jit(solution)/shard_map/pallas_call | solution.py:366
Async XLA Ops:
  0.7 1.2 %copy-start = (f32[32,64,128]{2,1,0:T(8,128)S(1)}, f32[32,64,128]{2,1,0:T(8,128)}, u32[]{:S(2)}) copy-start(f32[32,64,128]{2,1,0:T(8,128)} %density_ref.1) | copy-start | bytes 3145732
  1.9 0.7 %copy-start.1 = (s32[2,2]{1,0:T(2,128)S(1)}, s32[2,2]{1,0:T(2,128)}, u32[]{:S(2)}) copy-start(s32[2,2]{1,0:T(2,128)} %turn_ref.7) | copy-start | bytes 52
  2.6 0.7 %copy-start.3 = (s32[4,128]{1,0:T(4,128)S(1)}, s32[4,128]{1,0:T(4,128)}, u32[]{:S(2)}) copy-start(s32[4,128]{1,0:T(4,128)} %table_ref.1) | copy-start | bytes 6148
  3.3 13.9 %copy-start.4 = (s32[2,32]{1,0:T(2,128)S(1)}, s32[2,32]{1,0:T(2,128)}, u32[]{:S(2)}) copy-start(s32[2,32]{1,0:T(2,128)} %shear_ref.3) | copy-start | bytes 772
  4.1 13.1 %collective-permute-start = (f32[64,128]{1,0:T(8,128)S(1)}, f32[64,128]{1,0:T(8,128)S(1)}, u32[]{:S(2)}, u32[]{:S(2)}) collective-permute-start(f32[64,128]{1,0:T(8,128)S(1)} %get-tuple-element.24), channel_id=1, source_target_pairs={{8,16},{24,32},{40,48},{56,64},{72,80},{88,96},{104,112},{16,8},{3... | collective-permute-start | bytes 98312 | tf_op jit(solution)/shard_map/ppermute | solution.py:381
  7.6 9.6 %collective-permute-start.1 = (f32[64,128]{1,0:T(8,128)S(1)}, f32[64,128]{1,0:T(8,128)S(1)}, u32[]{:S(2)}, u32[]{:S(2)}) collective-permute-start(f32[64,128]{1,0:T(8,128)S(1)} %get-tuple-element.25), channel_id=1, source_target_pairs={{0,8},{16,24},{32,40},{48,56},{64,72},{80,88},{96,104},{112,120},{... | collective-permute-start | bytes 98312 | tf_op jit(solution)/shard_map/ppermute | solution.py:381
  8.2 9.0 %collective-permute-start.2 = (f32[32,128]{1,0:T(8,128)S(1)}, f32[32,128]{1,0:T(8,128)S(1)}, u32[]{:S(2)}, u32[]{:S(2)}) collective-permute-start(f32[32,128]{1,0:T(8,128)S(1)} %get-tuple-element.26), channel_id=1, source_target_pairs={{1,2},{3,4},{5,6},{2,1},{4,3},{6,5},{9,10},{11,12},{13,14},{10,9},... | collective-permute-start | bytes 49160 | tf_op jit(solution)/shard_map/ppermute | solution.py:381
  8.8 8.4 %collective-permute-start.3 = (f32[32,128]{1,0:T(8,128)S(1)}, f32[32,128]{1,0:T(8,128)S(1)}, u32[]{:S(2)}, u32[]{:S(2)}) collective-permute-start(f32[32,128]{1,0:T(8,128)S(1)} %get-tuple-element.27), channel_id=1, source_target_pairs={{0,1},{2,3},{4,5},{6,7},{1,0},{3,2},{5,4},{7,6},{8,9},{10,11},{12,... | collective-permute-start | bytes 49160 | tf_op jit(solution)/shard_map/ppermute | solution.py:381
  17.2 8.5 %copy-start.2 = (s32[2,64]{1,0:T(2,128)S(1)}, s32[2,64]{1,0:T(2,128)}, u32[]{:S(2)}) copy-start(s32[2,64]{1,0:T(2,128)} %shear_ref.5) | copy-start | bytes 1540
  25.6 5.6 %collective-permute-start.4 = (f32[8,4,8,128]{3,2,1,0:T(8,128)S(1)}, f32[8,4,8,128]{3,2,1,0:T(8,128)S(1)}, u32[]{:S(2)}, u32[]{:S(2)}) collective-permute-start(f32[8,4,8,128]{3,2,1,0:T(8,128)S(1)} %get-tuple-element.33), channel_id=1, source_target_pairs={{0,8},{8,0},{16,24},{24,16},{32,40},{40,32},{48,56},{56,48},{64,72... | collective-permute-start | bytes 393224 | tf_op jit(solution)/shard_map/ppermute | solution.py:357
  28.4 6.6 %collective-permute-start.8 = (f32[4,4,8,128]{3,2,1,0:T(8,128)S(1)}, f32[4,4,8,128]{3,2,1,0:T(8,128)S(1)}, u32[]{:S(2)}, u32[]{:S(2)}) collective-permute-start(f32[4,4,8,128]{3,2,1,0:T(8,128)S(1)} %shard_map.73), channel_id=1, source_target_pairs={{0,1},{1,0},{2,3},{3,2},{4,5},{5,4},{6,7},{7,6},{8,9},{9,8},{10,11... | collective-permute-start | bytes 196616 | tf_op jit(solution)/shard_map/ppermute | solution.py:357
  31.8 7.0 %collective-permute-start.5 = (f32[4,4,8,128]{3,2,1,0:T(8,128)S(1)}, f32[4,4,8,128]{3,2,1,0:T(8,128)S(1)}, u32[]{:S(2)}, u32[]{:S(2)}) collective-permute-start(f32[4,4,8,128]{3,2,1,0:T(8,128)S(1)} %get-tuple-element.36), channel_id=1, source_target_pairs={{0,16},{8,24},{16,0},{24,8},{32,48},{40,56},{48,32},{56,40},{64,80... | collective-permute-start | bytes 196616 | tf_op jit(solution)/shard_map/ppermute | solution.py:357
  35.6 5.2 %collective-permute-start.9 = (f32[2,4,8,128]{3,2,1,0:T(8,128)S(1)}, f32[2,4,8,128]{3,2,1,0:T(8,128)S(1)}, u32[]{:S(2)}, u32[]{:S(2)}) collective-permute-start(f32[2,4,8,128]{3,2,1,0:T(8,128)S(1)} %get-tuple-element.43), channel_id=1, source_target_pairs={{0,2},{1,3},{2,0},{3,1},{4,6},{5,7},{6,4},{7,5},{8,10},{9,11},{10,... | collective-permute-start | bytes 98312 | tf_op jit(solution)/shard_map/ppermute | solution.py:357
  39.4 5.5 %collective-permute-start.6 = (f32[2,4,8,128]{3,2,1,0:T(8,128)S(1)}, f32[2,4,8,128]{3,2,1,0:T(8,128)S(1)}, u32[]{:S(2)}, u32[]{:S(2)}) collective-permute-start(f32[2,4,8,128]{3,2,1,0:T(8,128)S(1)} %get-tuple-element.38), channel_id=1, source_target_pairs={{0,32},{8,40},{16,48},{24,56},{32,0},{40,8},{48,16},{56,24},{64,96... | collective-permute-start | bytes 98312 | tf_op jit(solution)/shard_map/ppermute | solution.py:357
  41.3 5.4 %collective-permute-start.10 = (f32[1,4,8,128]{3,2,1,0:T(8,128)S(1)}, f32[1,4,8,128]{3,2,1,0:T(8,128)S(1)}, u32[]{:S(2)}, u32[]{:S(2)}) collective-permute-start(f32[1,4,8,128]{3,2,1,0:T(8,128)S(1)} %get-tuple-element.45), channel_id=1, source_target_pairs={{0,6},{1,7},{2,4},{3,5},{4,2},{5,3},{6,0},{7,1},{8,14},{9,15},{10,... | collective-permute-start | bytes 49160 | tf_op jit(solution)/shard_map/ppermute | solution.py:357
  45.5 5.0 %collective-permute-start.7 = (f32[1,4,8,128]{3,2,1,0:T(8,128)S(1)}, f32[1,4,8,128]{3,2,1,0:T(8,128)S(1)}, u32[]{:S(2)}, u32[]{:S(2)}) collective-permute-start(f32[1,4,8,128]{3,2,1,0:T(8,128)S(1)} %get-tuple-element.40), channel_id=1, source_target_pairs={{0,96},{8,104},{16,112},{24,120},{32,64},{40,72},{48,80},{56,88},{... | collective-permute-start | bytes 49160 | tf_op jit(solution)/shard_map/ppermute | solution.py:357
where the time goes:
time: 51.9 us; the launch traced here: 51.7 us
  Pallas kernels  22.3 us (43%)
  starting transfers between devices  20.8 us (40%)
  waiting for transfers between devices  5.16 us (10%)
  local copies, waits for them, and re-layouts  2.59 us (5%)
  between operations  0.81 us (2%)
    ppermute x4, starting transfers between devices, local(): lax.ppermute(face, axis, neighbours(axis, offset))  10.5 us
    ppermute x7, starting transfers between devices, send(): self.got = lax.ppermute(give, self.axis, swapped(self.axis, mask))  10.3 us
    pallas_call x1, Pallas kernels, x_march(): pl.pallas_call(functools.partial(x_kernel, GROUP_X), out_shape=(part, par...  8.37 us
    pallas_call x2, Pallas kernels, y_march(): pl.pallas_call(functools.partial(y_kernel, GROUP_Y, kept, field.shape[1]...  5.4 us
    ppermute x7, waiting for transfers between devices, send(): self.got = lax.ppermute(give, self.axis, swapped(self.axis, mask))  5.15 us
    pallas_call x7, Pallas kernels, meet(): pl.pallas_call(functools.partial(stage_kernel, self.family, mask, order,...  5.11 us
    unnamed x10, local copies, waits for them, and re-layouts  2.59 us
    pallas_call x1, Pallas kernels, classify(): pl.pallas_call(functools.partial(classify_kernel, step_len), out_shape=fl...  2.57 us
  transfers between devices with their start and end apart: 11, of which 4 were waited for; matrix products, arithmetic and copies ran while one was open for 0% of the time, Pallas kernels for 23%

commit v1 on v0

--- a/solution.py
+++ b/solution.py
@@ -12,15 +12,20 @@
 ROWS = 8
 PIECE = 4
 LOG2E = 1.4426950408889634
+LOAD_COST = 2
 PACK = 1024.0
 ROUNDER = 12582912.0
 GROUP_X, GROUP_Y = 4, 2
-UNROLL_C, UNROLL_X, UNROLL_Y = 4, 2, 8
+UNROLL_C, UNROLL_E, UNROLL_X, UNROLL_Y = 32, 32, 32, 64
 
 SMEM = pl.BlockSpec(memory_space=pltpu.SMEM)
 VMEM = pl.BlockSpec(memory_space=pltpu.VMEM)
 HBM = pl.BlockSpec(memory_space=pltpu.HBM)
-STAGES = ((1, 2, 4, 8), (1, 2, 4))
+STAGES = (("gx", (1, 2, 4, 8)), ("gy", (1, 2, 4)))
+
+
+def is_set(axis, mask):
+    return (lax.axis_index(axis) & mask) != 0
 
 
 def slot_of(i, count):
@@ -36,25 +41,14 @@
                       mode=lax.GatherScatterMode.PROMISE_IN_BOUNDS)
 
 
-def load_kernel(stages, turn_ref, spot_ref, table_ref, density_ref, cells_ref, face_xa_ref,
-                face_xb_ref, face_ya_ref, face_yb_ref, lut_ref, index_ref, mask_ref, ahead_ref,
-                levels_ref, sem, table_sem):
+def load_kernel(density_ref, cells_ref, face_xa_ref, face_xb_ref, face_ya_ref, face_yb_ref,
+                index_ref, mask_ref, sem):
     count_x, count_y, cells_z = density_ref.shape
     inner = cells_ref.at[pl.ds(1, count_x), pl.ds(ROWS, count_y), :]
     copy = pltpu.make_async_copy(density_ref, inner, sem)
     copy.start()
-    table_copy = pltpu.make_async_copy(table_ref, levels_ref, table_sem)
-    table_copy.start()
 
     lane = lax.broadcasted_iota(jnp.int32, (ROWS, cells_z), 1)
-    row = lax.broadcasted_iota(jnp.int32, (ROWS, cells_z), 0)
-    stage = 0
-    for family, masks in enumerate(stages):
-        turned = jnp.where(row < PIECE, turn_ref[family, 0], turn_ref[family, 1])
-        for mask in masks:
-            upper = jnp.where((spot_ref[family] & mask) != 0, 1, 0)
-            ahead_ref[stage] = jnp.where(turned == upper, 1.0, 0.0)
-            stage += 1
 
     def shifted(s, carry):
         source = lane - (s - SHEAR)
@@ -65,15 +59,9 @@
         return carry
 
     lax.fori_loop(0, 2 * SHEAR, shifted, 0, unroll=4)
-    table_copy.wait()
-    levels = levels_ref[...].astype(jnp.float32)
-    for c in range(4):
-        level = jnp.broadcast_to(levels[c:c + 1], (ROWS, cells_z))
-        rise = jnp.where(lane == cells_z - 1, 0.0, pltpu.roll(level, cells_z - 1, 1) - level)
-        lut_ref[c] = level + rise * (1.0 / PACK)
     copy.wait()
 
-    odd_x, odd_y = (spot_ref[0] & 1) != 0, (spot_ref[1] & 1) != 0
+    odd_x, odd_y = is_set("gx", 1), is_set("gy", 1)
     first, last = cells_ref[1, pl.ds(ROWS, count_y), :], cells_ref[count_x, pl.ds(ROWS, count_y), :]
     face_xa_ref[...] = jnp.where(odd_x, last, first)
     face_xb_ref[...] = jnp.where(odd_x, first, last)
@@ -83,10 +71,16 @@
     face_yb_ref[...] = jnp.where(odd_y, first, last)
 
 
-def classify_kernel(step_len, cells_ref, lut_ref, field_ref):
+def classify_kernel(step_len, cells_ref, table_ref, field_ref, lut_ref):
     count_x, cells_z = cells_ref.shape[0] - 2, cells_ref.shape[2]
     count_y = cells_ref.shape[1] - 2 * ROWS
     pitch = field_ref.shape[1] // count_x
+    lane = lax.broadcasted_iota(jnp.int32, (ROWS, cells_z), 1)
+    levels = table_ref[...].astype(jnp.float32)
+    for c in range(4):
+        level = jnp.broadcast_to(levels[c:c + 1], (ROWS, cells_z))
+        rise = jnp.where(lane == cells_z - 1, 0.0, pltpu.roll(level, cells_z - 1, 1) - level)
+        lut_ref[c] = level + rise * (1.0 / PACK)
 
     def body(i, carry):
         slot = slot_of(i, count_x) * pitch
@@ -131,16 +125,24 @@
     return [state[1] * fade, state[2] * fade, state[3] * fade, total]
 
 
-def x_kernel(group, turn_ref, spot_ref, shear_ref, face_xa_ref, face_xb_ref, face_ya_ref,
+def x_kernel(group, stages, turn_ref, shear_ref, face_xa_ref, face_xb_ref, face_ya_ref,
              face_yb_ref, field_ref, index_ref, mask_ref, _, keep_ref, give_ref, emit_ref,
-             cells_ref):
+             ahead_ref, cells_ref):
     count_x, cells_z = cells_ref.shape[0] - 2, cells_ref.shape[2]
     count_y = cells_ref.shape[1] - 2 * ROWS
     pitch = field_ref.shape[1] // count_x
     pad = ROWS
     lane = lax.broadcasted_iota(jnp.int32, (ROWS, cells_z), 1)
 
-    odd_x, odd_y = (spot_ref[0] & 1) != 0, (spot_ref[1] & 1) != 0
+    row = lax.broadcasted_iota(jnp.int32, (ROWS, cells_z), 0)
+    stage = 0
+    for family, (axis, masks) in enumerate(stages):
+        turned = jnp.where(row < PIECE, turn_ref[family, 0], turn_ref[family, 1])
+        for mask in masks:
+            ahead_ref[stage] = jnp.where(turned == jnp.where(is_set(axis, mask), 1, 0), 1.0, 0.0)
+            stage += 1
+
+    odd_x, odd_y = is_set("gx", 1), is_set("gy", 1)
     cells_ref[0, pl.ds(pad, count_y), :] = jnp.where(odd_x, face_xb_ref[...], face_xa_ref[...])
     cells_ref[count_x + 1, pl.ds(pad, count_y), :] = jnp.where(odd_x, face_xa_ref[...],
                                                                face_xb_ref[...])
@@ -168,6 +170,17 @@
         norm = diff_x * diff_x + diff_y * diff_y + diff_z * diff_z + 0.04
         return 0.3 + (0.7 / 3.0) * facing * lax.rsqrt(norm)
 
+    def emission(i, carry):
+        slot = slot_of(i, count_x) * pitch
+        for base in range(0, count_y, ROWS):
+            shaded = shade(i, base)
+            rows = pl.ds(slot + base, ROWS)
+            for c in range(3):
+                emit_ref[c, rows, :] = field_ref[c, rows, :] * shaded
+        return carry
+
+    lax.fori_loop(0, count_x, emission, 0, unroll=UNROLL_E)
+
     def block_of(block, carry):
         base = pl.multiple_of(block * (ROWS * group), ROWS)
 
@@ -175,12 +188,9 @@
             fields = []
             slot = slot_of(i, count_x) * pitch
             for g in range(group):
-                shaded = shade(i, base + g * ROWS)
-                row = slot + base + g * ROWS
-                colours = [field_ref[c, pl.ds(row, ROWS), :] * shaded for c in range(3)]
-                for c in range(3):
-                    emit_ref[c, pl.ds(row, ROWS), :] = colours[c]
-                fields.append((*colours, field_ref[3, pl.ds(row, ROWS), :]))
+                rows = pl.ds(slot + base + g * ROWS, ROWS)
+                fields.append((emit_ref[0, rows, :], emit_ref[1, rows, :], emit_ref[2, rows, :],
+                               field_ref[3, rows, :]))
             return tuple(march(fields, shear_ref[v, i], turned[v], index_ref, mask_ref,
                                states[v]) for v in range(2))
 
@@ -197,12 +207,12 @@
     lax.fori_loop(0, count_y // (ROWS * group), block_of, 0)
 
 
-def y_kernel(group, kept, pitch, turn_ref, spot_ref, shear_ref, emit_ref, field_ref, index_ref, mask_ref,
+def y_kernel(group, kept, pitch, turn_ref, shear_ref, emit_ref, field_ref, index_ref, mask_ref,
              out_ref):
     cells_z = emit_ref.shape[-1]
     count_y = shear_ref.shape[1]
     size = out_ref.shape[0] * PIECE
-    first = ((spot_ref[1] & 1) ^ (1 - kept)) * size
+    first = jnp.where(is_set("gy", 1) == bool(kept), size, 0)
     turned = [turn_ref[1, v] != 0 for v in range(2)]
     zeros = jnp.zeros((ROWS, cells_z), jnp.float32)
 
@@ -240,62 +250,60 @@
     return jax.ShapeDtypeStruct(shape, jnp.float32)
 
 
-def load(density, transfer_table, direction, spot):
+def load(density):
     count_x, count_y, cells_z = density.shape
     return pl.pallas_call(
-        functools.partial(load_kernel, STAGES),
+        load_kernel,
         out_shape=(floats(count_x + 2, count_y + 2 * ROWS, cells_z),
                    floats(count_y, cells_z), floats(count_y, cells_z),
                    floats(count_x, cells_z), floats(count_x, cells_z),
-                   floats(4, ROWS, cells_z),
                    jax.ShapeDtypeStruct((2 * SHEAR, ROWS, cells_z), jnp.int32),
-                   floats(4 * SHEAR, ROWS, cells_z),
-                   floats(sum(map(len, STAGES)), ROWS, cells_z)),
-        in_specs=[SMEM, SMEM, HBM, HBM],
-        out_specs=(VMEM,) * 9,
-        scratch_shapes=[pltpu.VMEM(transfer_table.shape, jnp.int32), pltpu.SemaphoreType.DMA,
-                        pltpu.SemaphoreType.DMA],
+                   floats(4 * SHEAR, ROWS, cells_z)),
+        in_specs=[HBM],
+        out_specs=(VMEM,) * 7,
+        scratch_shapes=[pltpu.SemaphoreType.DMA],
         name="load",
-        **options(2),
-    )(direction, spot, transfer_table, density)
-
-
-def classify(cells, lut, step_len):
+        **options(LOAD_COST),
+    )(density)
+
+
+def classify(cells, transfer_table, step_len):
     count_x, count_y, cells_z = cells.shape[0] - 2, cells.shape[1] - 2 * ROWS, cells.shape[2]
     return pl.pallas_call(
         functools.partial(classify_kernel, step_len),
         out_shape=floats(4, count_x * (count_y + 1), cells_z),
         in_specs=[VMEM, VMEM],
         out_specs=VMEM,
+        scratch_shapes=[pltpu.VMEM((4, ROWS, cells_z), jnp.float32)],
         name="classify",
         **options(3),
-    )(cells, lut)
-
-
-def x_march(cells, halo, field, shifts, shear_x, direction, spot):
+    )(cells, transfer_table)
+
+
+def x_march(cells, halo, field, shifts, shear_x, direction):
     count_y, cells_z = cells.shape[1] - 2 * ROWS, cells.shape[2]
     part = floats(count_y // (2 * PIECE), 4, 2 * PIECE, cells_z)
-    keep, give, emitted, _ = pl.pallas_call(
-        functools.partial(x_kernel, GROUP_X),
-        out_shape=(part, part, floats(3, *field.shape[1:]), floats(*cells.shape)),
-        in_specs=[SMEM] * 3 + [VMEM] * 8,
-        out_specs=(VMEM,) * 4,
-        input_output_aliases={10: 3},
+    ahead = floats(sum(len(masks) for _, masks in STAGES), ROWS, cells_z)
+    return pl.pallas_call(
+        functools.partial(x_kernel, GROUP_X, STAGES),
+        out_shape=(part, part, floats(3, *field.shape[1:]), ahead, floats(*cells.shape)),
+        in_specs=[SMEM] * 2 + [VMEM] * 8,
+        out_specs=(VMEM,) * 5,
+        input_output_aliases={9: 4},
         name="x_march",
         **options(8),
-    )(direction, spot, shear_x, *halo, field, *shifts, cells)
-    return keep, give, emitted
-
-
-def y_march(emitted, field, shifts, shear_y, direction, spot, count_x, kept):
+    )(direction, shear_x, *halo, field, *shifts, cells)[:4]
+
+
+def y_march(emitted, field, shifts, shear_y, direction, count_x, kept):
     cells_z = field.shape[-1]
     return pl.pallas_call(
         functools.partial(y_kernel, GROUP_Y, kept, field.shape[1] // count_x),
         out_shape=floats(count_x // (2 * PIECE), 4, 2 * PIECE, cells_z),
-        in_specs=[SMEM] * 3 + [VMEM] * 4,
+        in_specs=[SMEM] * 2 + [VMEM] * 4,
         out_specs=VMEM,
         **options(2.5),
-    )(direction, spot, shear_y, emitted, field, *shifts)
+    )(direction, shear_y, emitted, field, *shifts)
 
 
 def neighbours(axis, offset):
@@ -308,8 +316,7 @@
     return [(i, i ^ mask) for i in range(lax.axis_size(axis))]
 
 
-def stage_kernel(family, mask, order, split, spot_ref, keep_ref, got_ref, ahead_ref, *out_refs):
-    me = spot_ref[family]
+def stage_kernel(axis, mask, order, split, keep_ref, got_ref, ahead_ref, *out_refs):
     mine_ahead = ahead_ref[order] > 0.5
 
     def joined(p):
@@ -327,13 +334,13 @@
         return
     pick = lambda flag, a, b: [jnp.where(flag, one, two) for one, two in zip(a, b)]
     if split == "pair":
-        high = (me & mask) != 0
+        high = is_set(axis, mask)
         pairs = list(zip(parts[::2], parts[1::2]))
         keep = [pick(high, b, a) for a, b in pairs]
         give = [pick(high, a, b) for a, b in pairs]
     elif split == "ring_first":
-        upper = (me & (2 * mask)) != 0
-        edge = ((me // mask + me // (2 * mask)) & 1) == 0
+        upper = is_set(axis, 2 * mask)
+        edge = is_set(axis, mask) == upper
         ends, middle = (parts[0], parts[3]), (parts[1], parts[2])
         small, large = [pick(edge, ends[k], middle[k]) for k in range(2)]
         keep = [pick(upper, large, small), pick(upper, small, large)]
@@ -348,8 +355,8 @@
 
 
 class Exchange:
-    def __init__(self, family, axis, ahead, spot):
-        self.family, self.axis, self.ahead, self.spot = family, axis, ahead, spot
+    def __init__(self, axis, first, ahead):
+        self.axis, self.first, self.ahead = axis, first, ahead
         self.stage = 0
 
     def send(self, keep, give, mask):
@@ -362,31 +369,29 @@
             shape = floats(2, 4, PIECE, rest[-1])
         else:
             shape = (floats(count // 2, *rest),) * 2
-        order = self.family * len(STAGES[0]) + self.stage - 1
         return pl.pallas_call(
-            functools.partial(stage_kernel, self.family, mask, order, split),
+            functools.partial(stage_kernel, self.axis, mask, self.first + self.stage - 1, split),
             out_shape=shape,
-            in_specs=[SMEM] + [VMEM] * 3,
+            in_specs=[VMEM] * 3,
             out_specs=VMEM if split == "image" else (VMEM, VMEM),
             **options(0.3),
-        )(self.spot, self.keep, self.got, self.ahead)
+        )(self.keep, self.got, self.ahead)
 
 
 def local(density, transfer_table, shear_x, shear_y, direction):
     count_x = density.shape[0]
     step_len = 1.0 / (count_x * lax.axis_size("gx"))
-    spot = jnp.stack([lax.axis_index("gx"), lax.axis_index("gy")]).astype(jnp.int32)
-    cells, *faces, lut, index, mask, ahead = load(density, transfer_table, direction, spot)
+    cells, *faces, index, mask = load(density)
     shifts = (index, mask)
     halo = [lax.ppermute(face, axis, neighbours(axis, offset)) for face, axis, offset in
             zip(faces, ("gx", "gx", "gy", "gy"), (1, 0, 1, 0))]
-    field = classify(cells, lut, step_len)
-    keep_x, give_x, emitted = x_march(cells, halo, field, shifts, shear_x, direction, spot)
-
-    x, y = Exchange(0, "gx", ahead, spot), Exchange(1, "gy", ahead, spot)
+    field = classify(cells, transfer_table, step_len)
+    keep_x, give_x, emitted, ahead = x_march(cells, halo, field, shifts, shear_x, direction)
+
+    x, y = Exchange("gx", 0, ahead), Exchange("gy", len(STAGES[0][1]), ahead)
     x.send(keep_x, give_x, 1)
-    given = y_march(emitted, field, shifts, shear_y, direction, spot, count_x, 0)
-    kept = y_march(emitted, field, shifts, shear_y, direction, spot, count_x, 1)
+    given = y_march(emitted, field, shifts, shear_y, direction, count_x, 0)
+    kept = y_march(emitted, field, shifts, shear_y, direction, count_x, 1)
     x.send(*x.meet("pair", 2), 2)
     y.send(kept, given, 1)
     x.send(*x.meet("ring_first", 4), 4)

time: 51.9 us -> 43 us (0.83)
  Pallas kernels: 22.3 us -> 12.1 us
  waiting for transfers between devices: 5.16 us -> 7.05 us
  local copies, waits for them, and re-layouts: 2.59 us -> 1.91 us
    pallas_call x9, Pallas kernels: 14.3 us -> 5.81 us  [the longest x1 4.28 us: x_march(): pl.pallas_call(functools.partial(x_kernel, GROUP_X, STAGES), out_shape=(p...]
    ppermute x7, waiting for transfers between devices: 5.15 us -> 7.04 us  [send(): self.got = lax.ppermute(give, self.axis, swapped(self.axis, mask))]
    pallas_call x2, Pallas kernels: 5.4 us -> 4.3 us  [y_march(): pl.pallas_call(functools.partial(y_kernel, GROUP_Y, kept, field.shape[1]...]
    unnamed x10, local copies, waits for them, and re-layouts: 2.59 us -> 1.91 us
    pallas_call x1, Pallas kernels: 2.57 us -> 2.04 us  [classify(): pl.pallas_call(functools.partial(classify_kernel, step_len), out_shape=fl...]
  transfers between devices with their start and end apart: 11 -> 11, of which waited for: 4 -> 4; matrix products, arithmetic and copies ran while one was open for 0% -> 0% of each run, Pallas kernels for 23% -> 17%
where the time goes in v1:
time: 43 us; the launch traced here: 42.8 us
  starting transfers between devices  20.9 us (49%)
  Pallas kernels  12.1 us (28%)
  waiting for transfers between devices  7.05 us (16%)
  local copies, waits for them, and re-layouts  1.91 us (4%)
  between operations  0.8 us (2%)
    ppermute x7, starting transfers between devices, send(): self.got = lax.ppermute(give, self.axis, swapped(self.axis, mask))  10.5 us
    ppermute x4, starting transfers between devices, local(): lax.ppermute(face, axis, neighbours(axis, offset))  10.5 us
    ppermute x7, waiting for transfers between devices, send(): self.got = lax.ppermute(give, self.axis, swapped(self.axis, mask))  7.04 us
    pallas_call x2, Pallas kernels, y_march(): pl.pallas_call(functools.partial(y_kernel, GROUP_Y, kept, field.shape[1]...  4.3 us
    pallas_call x1, Pallas kernels, x_march(): pl.pallas_call(functools.partial(x_kernel, GROUP_X, STAGES), out_shape=(p...  4.28 us
    pallas_call x1, Pallas kernels, classify(): pl.pallas_call(functools.partial(classify_kernel, step_len), out_shape=fl...  2.04 us
    unnamed x10, local copies, waits for them, and re-layouts  1.91 us
    pallas_call x7, Pallas kernels, meet(): pl.pallas_call(functools.partial(stage_kernel, self.axis, mask, self.firs...  1.34 us
  transfers between devices with their start and end apart: 11, of which 4 were waited for; matrix products, arithmetic and copies ran while one was open for 0% of the time, Pallas kernels for 17%

profile of v1, /device:TPU:24, one launch (start us, length us, event | category | flops | bytes accessed | tf_op | source)
XLA Modules:
  0.0 42.8 jit_solution(12170153378605884815)
XLA Ops:
  0.6 0.0 copy-start
  0.6 1.2 %copy-done = f32[32,64,128]{2,1,0:T(8,128)S(1)} copy-done((f32[32,64,128]{2,1,0:T(8,128)S(1)}, f32[32,64,128]{2,1,0:T(8,128)}, u32[]{:S(2)}) %copy-start) | copy-done | bytes 1048600
  1.9 0.0 copy-start.1
  1.9 0.0 copy-start.4
  1.9 0.2 load.1
  2.1 3.4 %collective-permute-start = (f32[64,128]{1,0:T(8,128)S(1)}, f32[64,128]{1,0:T(8,128)S(1)}, u32[]{:S(2)}, u32[]{:S(2)}) collective-permute-start(f32[64,128]{1,0:T(8,128)S(1)} %get-tuple-element.23), channel_id=1, source_target_pairs={{8,16},{24,32},{40,48},{56,64},{72,80},{88,96},{104,112},{16,8},{3... | collective-permute-start | bytes 98312 | tf_op jit(solution)/shard_map/ppermute | solution.py:386
  5.5 0.6 %collective-permute-start.1 = (f32[64,128]{1,0:T(8,128)S(1)}, f32[64,128]{1,0:T(8,128)S(1)}, u32[]{:S(2)}, u32[]{:S(2)}) collective-permute-start(f32[64,128]{1,0:T(8,128)S(1)} %get-tuple-element.24), channel_id=1, source_target_pairs={{0,8},{16,24},{32,40},{48,56},{64,72},{80,88},{96,104},{112,120},{... | collective-permute-start | bytes 98312 | tf_op jit(solution)/shard_map/ppermute | solution.py:386
  6.1 0.7 %collective-permute-start.2 = (f32[32,128]{1,0:T(8,128)S(1)}, f32[32,128]{1,0:T(8,128)S(1)}, u32[]{:S(2)}, u32[]{:S(2)}) collective-permute-start(f32[32,128]{1,0:T(8,128)S(1)} %get-tuple-element.25), channel_id=1, source_target_pairs={{1,2},{3,4},{5,6},{2,1},{4,3},{6,5},{9,10},{11,12},{13,14},{10,9},... | collective-permute-start | bytes 49160 | tf_op jit(solution)/shard_map/ppermute | solution.py:386
  6.7 5.8 %collective-permute-start.3 = (f32[32,128]{1,0:T(8,128)S(1)}, f32[32,128]{1,0:T(8,128)S(1)}, u32[]{:S(2)}, u32[]{:S(2)}) collective-permute-start(f32[32,128]{1,0:T(8,128)S(1)} %get-tuple-element.26), channel_id=1, source_target_pairs={{0,1},{2,3},{4,5},{6,7},{1,0},{3,2},{5,4},{7,6},{8,9},{10,11},{12,... | collective-permute-start | bytes 49160 | tf_op jit(solution)/shard_map/ppermute | solution.py:386
  12.5 0.0 copy-start.3
  12.5 0.7 %copy-done.3 = s32[4,128]{1,0:T(4,128)S(1)} copy-done((s32[4,128]{1,0:T(4,128)S(1)}, s32[4,128]{1,0:T(4,128)}, u32[]{:S(2)}) %copy-start.3) | copy-done | bytes 2072
  13.2 2.0 %classify.1.field_ref = f32[4,2080,128]{2,1,0:T(8,128)S(1)} custom-call(f32[34,80,128]{2,1,0:T(8,128)S(1)} %get-tuple-element.27.cells_ref._, s32[4,128]{1,0:T(4,128)S(1)} %copy-done.3), custom_call_target="tpu_custom_call" | custom-call | bytes 10500000 | tf_op jit(solution)/shard_map/classify/pallas_call | solution.py:272
  15.3 0.0 copy-start.2
  15.3 0.0 collective-permute-done.2.face_ya_ref
  15.3 0.0 collective-permute-done.3.face_yb_ref
  15.3 0.0 collective-permute-done.face_xa_ref
  15.3 0.0 collective-permute-done.1.face_xb_ref
  15.3 0.0 copy-done.1
  15.3 0.0 copy-done.4
  15.3 4.3 %x_march.1 = (f32[8,4,8,128]{3,2,1,0:T(8,128)S(1)}, f32[8,4,8,128]{3,2,1,0:T(8,128)S(1)}, f32[3,2080,128]{2,1,0:T(8,128)S(1)}, f32[7,8,128]{2,1,0:T(8,128)S(1)}, f32[34,80,128]{2,1,0:T(8,128)S(1)}) custom-call(s32[2,2]{1,0:T(2,128)S(1)} %copy-done.1, s32[2,32]{1,0:T(2,128)S(1)} %copy-done.4, ...), custom_call_target="tpu_custom_call", output_to_operand_aliasing={{4}: (9, {})} | custom-call | bytes 28000000 | tf_op jit(solution)/shard_map/x_march/pallas_call | solution.py:287
  19.6 0.1 collective-permute-start.4
  19.7 0.0 copy-done.2
  19.7 2.2 %shard_map.73 = f32[4,4,8,128]{3,2,1,0:T(8,128)S(1)} custom-call(s32[2,2]{1,0:T(2,128)S(1)} %copy-done.1, s32[2,64]{1,0:T(2,128)S(1)} %copy-done.2, f32[3,2080,128]{2,1,0:T(8,128)S(1)} %get-tuple-element.39.emit_ref, f32[4,2080,128]{2,1,0:T(8,128)S(1)} %classify.1.field_ref, s32[32,8,128]{2,1,0:T(8,128)S(1)} %get-tuple-element.28.index_ref, ...), custom_call_target="tpu_custom_call" | custom-call | bytes 8750000 | tf_op jit(solution)/shard_map/pallas_call | solution.py:300
  21.9 2.6 %collective-permute-start.8 = (f32[4,4,8,128]{3,2,1,0:T(8,128)S(1)}, f32[4,4,8,128]{3,2,1,0:T(8,128)S(1)}, u32[]{:S(2)}, u32[]{:S(2)}) collective-permute-start(f32[4,4,8,128]{3,2,1,0:T(8,128)S(1)} %shard_map.73), channel_id=1, source_target_pairs={{0,1},{1,0},{2,3},{3,2},{4,5},{5,4},{6,7},{7,6},{8,9},{9,8},{10,11... | collective-permute-start | bytes 196616 | tf_op jit(solution)/shard_map/ppermute | solution.py:364
  24.5 0.0 collective-permute-done.4.got_ref
  24.6 0.1 collective-permute-start.5
  24.6 2.1 %shard_map.72.keep_ref = f32[4,4,8,128]{3,2,1,0:T(8,128)S(1)} custom-call(s32[2,2]{1,0:T(2,128)S(1)} %copy-done.1, s32[2,64]{1,0:T(2,128)S(1)} %copy-done.2, f32[3,2080,128]{2,1,0:T(8,128)S(1)} %get-tuple-element.39.emit_ref, f32[4,2080,128]{2,1,0:T(8,128)S(1)} %classify.1.field_ref, s32[32,8,128]{2,1,0:T(8,128)S(1)} %get-tuple-element.28.index_ref, ...), custom_call_target="tpu_custom_call" | custom-call | bytes 8750000 | tf_op jit(solution)/shard_map/pallas_call | solution.py:300
  26.8 1.6 %collective-permute-done.8.got_ref = f32[4,4,8,128]{3,2,1,0:T(8,128)S(1)} collective-permute-done((f32[4,4,8,128]{3,2,1,0:T(8,128)S(1)}, f32[4,4,8,128]{3,2,1,0:T(8,128)S(1)}, u32[]{:S(2)}, u32[]{:S(2)}) %collective-permute-start.8) | collective-permute-done | bytes 65568 | tf_op jit(solution)/shard_map/ppermute | solution.py:364
  28.5 3.1 %collective-permute-start.9 = (f32[2,4,8,128]{3,2,1,0:T(8,128)S(1)}, f32[2,4,8,128]{3,2,1,0:T(8,128)S(1)}, u32[]{:S(2)}, u32[]{:S(2)}) collective-permute-start(f32[2,4,8,128]{3,2,1,0:T(8,128)S(1)} %get-tuple-element.41), channel_id=1, source_target_pairs={{0,2},{1,3},{2,0},{3,1},{4,6},{5,7},{6,4},{7,5},{8,10},{9,11},{10,... | collective-permute-start | bytes 98312 | tf_op jit(solution)/shard_map/ppermute | solution.py:364
  31.6 0.0 collective-permute-done.5.got_ref
  31.6 0.8 %collective-permute-start.6 = (f32[2,4,8,128]{3,2,1,0:T(8,128)S(1)}, f32[2,4,8,128]{3,2,1,0:T(8,128)S(1)}, u32[]{:S(2)}, u32[]{:S(2)}) collective-permute-start(f32[2,4,8,128]{3,2,1,0:T(8,128)S(1)} %get-tuple-element.36), channel_id=1, source_target_pairs={{0,32},{8,40},{16,48},{24,56},{32,0},{40,8},{48,16},{56,24},{64,96... | collective-permute-start | bytes 98312 | tf_op jit(solution)/shard_map/ppermute | solution.py:364
  32.4 1.1 %collective-permute-done.9.got_ref = f32[2,4,8,128]{3,2,1,0:T(8,128)S(1)} collective-permute-done((f32[2,4,8,128]{3,2,1,0:T(8,128)S(1)}, f32[2,4,8,128]{3,2,1,0:T(8,128)S(1)}, u32[]{:S(2)}, u32[]{:S(2)}) %collective-permute-start.9) | collective-permute-done | bytes 32800 | tf_op jit(solution)/shard_map/ppermute | solution.py:364
  33.5 3.7 %collective-permute-start.10 = (f32[1,4,8,128]{3,2,1,0:T(8,128)S(1)}, f32[1,4,8,128]{3,2,1,0:T(8,128)S(1)}, u32[]{:S(2)}, u32[]{:S(2)}) collective-permute-start(f32[1,4,8,128]{3,2,1,0:T(8,128)S(1)} %get-tuple-element.43), channel_id=1, source_target_pairs={{0,6},{1,7},{2,4},{3,5},{4,2},{5,3},{6,0},{7,1},{8,14},{9,15},{10,... | collective-permute-start | bytes 49160 | tf_op jit(solution)/shard_map/ppermute | solution.py:364
  37.2 0.0 collective-permute-done.6.got_ref
  37.2 0.1 collective-permute-start.7
  37.3 1.6 %collective-permute-done.10.got_ref = f32[1,4,8,128]{3,2,1,0:T(8,128)S(1)} collective-permute-done((f32[1,4,8,128]{3,2,1,0:T(8,128)S(1)}, f32[1,4,8,128]{3,2,1,0:T(8,128)S(1)}, u32[]{:S(2)}, u32[]{:S(2)}) %collective-permute-start.10) | collective-permute-done | bytes 16416 | tf_op jit(solution)/shard_map/ppermute | solution.py:364
  38.9 0.6 %shard_map.76 = f32[2,4,4,128]{3,2,1,0:T(4,128)} custom-call(f32[1,4,8,128]{3,2,1,0:T(8,128)S(1)} %get-tuple-element.42.keep_ref, f32[1,4,8,128]{3,2,1,0:T(8,128)S(1)} %collective-permute-done.10.got_ref, f32[7,8,128]{2,1,0:T(8,128)S(1)} %get-tuple-element.32.ahead_ref), custom_call_target="tpu_custom_call" | custom-call | bytes 1050000 | tf_op jit(solution)/shard_map/pallas_call | solution.py:372
  39.5 2.7 %collective-permute-done.7.got_ref = f32[1,4,8,128]{3,2,1,0:T(8,128)S(1)} collective-permute-done((f32[1,4,8,128]{3,2,1,0:T(8,128)S(1)}, f32[1,4,8,128]{3,2,1,0:T(8,128)S(1)}, u32[]{:S(2)}, u32[]{:S(2)}) %collective-permute-start.7) | collective-permute-done | bytes 16416 | tf_op jit(solution)/shard_map/ppermute | solution.py:364
  42.2 0.6 %shard_map.71 = f32[2,4,4,128]{3,2,1,0:T(4,128)} custom-call(f32[1,4,8,128]{3,2,1,0:T(8,128)S(1)} %get-tuple-element.37.keep_ref, f32[1,4,8,128]{3,2,1,0:T(8,128)S(1)} %collective-permute-done.7.got_ref, f32[7,8,128]{2,1,0:T(8,128)S(1)} %get-tuple-element.32.ahead_ref), custom_call_target="tpu_custom_call" | custom-call | bytes 1050000 | tf_op jit(solution)/shard_map/pallas_call | solution.py:372
  (5 shorter events, 0.1 us)
Async XLA Ops:
  0.6 1.2 %copy-start = (f32[32,64,128]{2,1,0:T(8,128)S(1)}, f32[32,64,128]{2,1,0:T(8,128)}, u32[]{:S(2)}) copy-start(f32[32,64,128]{2,1,0:T(8,128)} %density_ref.1) | copy-start | bytes 3145732
  1.9 13.5 %copy-start.1 = (s32[2,2]{1,0:T(2,128)S(1)}, s32[2,2]{1,0:T(2,128)}, u32[]{:S(2)}) copy-start(s32[2,2]{1,0:T(2,128)} %turn_ref.5) | copy-start | bytes 52
  1.9 13.5 %copy-start.4 = (s32[2,32]{1,0:T(2,128)S(1)}, s32[2,32]{1,0:T(2,128)}, u32[]{:S(2)}) copy-start(s32[2,32]{1,0:T(2,128)} %shear_ref.3) | copy-start | bytes 772
  2.1 13.2 %collective-permute-start = (f32[64,128]{1,0:T(8,128)S(1)}, f32[64,128]{1,0:T(8,128)S(1)}, u32[]{:S(2)}, u32[]{:S(2)}) collective-permute-start(f32[64,128]{1,0:T(8,128)S(1)} %get-tuple-element.23), channel_id=1, source_target_pairs={{8,16},{24,32},{40,48},{56,64},{72,80},{88,96},{104,112},{16,8},{3... | collective-permute-start | bytes 98312 | tf_op jit(solution)/shard_map/ppermute | solution.py:386
  5.5 9.8 %collective-permute-start.1 = (f32[64,128]{1,0:T(8,128)S(1)}, f32[64,128]{1,0:T(8,128)S(1)}, u32[]{:S(2)}, u32[]{:S(2)}) collective-permute-start(f32[64,128]{1,0:T(8,128)S(1)} %get-tuple-element.24), channel_id=1, source_target_pairs={{0,8},{16,24},{32,40},{48,56},{64,72},{80,88},{96,104},{112,120},{... | collective-permute-start | bytes 98312 | tf_op jit(solution)/shard_map/ppermute | solution.py:386
  6.1 9.2 %collective-permute-start.2 = (f32[32,128]{1,0:T(8,128)S(1)}, f32[32,128]{1,0:T(8,128)S(1)}, u32[]{:S(2)}, u32[]{:S(2)}) collective-permute-start(f32[32,128]{1,0:T(8,128)S(1)} %get-tuple-element.25), channel_id=1, source_target_pairs={{1,2},{3,4},{5,6},{2,1},{4,3},{6,5},{9,10},{11,12},{13,14},{10,9},... | collective-permute-start | bytes 49160 | tf_op jit(solution)/shard_map/ppermute | solution.py:386
  6.7 8.5 %collective-permute-start.3 = (f32[32,128]{1,0:T(8,128)S(1)}, f32[32,128]{1,0:T(8,128)S(1)}, u32[]{:S(2)}, u32[]{:S(2)}) collective-permute-start(f32[32,128]{1,0:T(8,128)S(1)} %get-tuple-element.26), channel_id=1, source_target_pairs={{0,1},{2,3},{4,5},{6,7},{1,0},{3,2},{5,4},{7,6},{8,9},{10,11},{12,... | collective-permute-start | bytes 49160 | tf_op jit(solution)/shard_map/ppermute | solution.py:386
  12.5 0.7 %copy-start.3 = (s32[4,128]{1,0:T(4,128)S(1)}, s32[4,128]{1,0:T(4,128)}, u32[]{:S(2)}) copy-start(s32[4,128]{1,0:T(4,128)} %table_ref.1) | copy-start | bytes 6148
  15.3 4.5 %copy-start.2 = (s32[2,64]{1,0:T(2,128)S(1)}, s32[2,64]{1,0:T(2,128)}, u32[]{:S(2)}) copy-start(s32[2,64]{1,0:T(2,128)} %shear_ref.5) | copy-start | bytes 1540
  19.6 4.9 %collective-permute-start.4 = (f32[8,4,8,128]{3,2,1,0:T(8,128)S(1)}, f32[8,4,8,128]{3,2,1,0:T(8,128)S(1)}, u32[]{:S(2)}, u32[]{:S(2)}) collective-permute-start(f32[8,4,8,128]{3,2,1,0:T(8,128)S(1)} %get-tuple-element.31), channel_id=1, source_target_pairs={{0,8},{8,0},{16,24},{24,16},{32,40},{40,32},{48,56},{56,48},{64,72... | collective-permute-start | bytes 393224 | tf_op jit(solution)/shard_map/ppermute | solution.py:364
  21.9 6.6 %collective-permute-start.8 = (f32[4,4,8,128]{3,2,1,0:T(8,128)S(1)}, f32[4,4,8,128]{3,2,1,0:T(8,128)S(1)}, u32[]{:S(2)}, u32[]{:S(2)}) collective-permute-start(f32[4,4,8,128]{3,2,1,0:T(8,128)S(1)} %shard_map.73), channel_id=1, source_target_pairs={{0,1},{1,0},{2,3},{3,2},{4,5},{5,4},{6,7},{7,6},{8,9},{9,8},{10,11... | collective-permute-start | bytes 196616 | tf_op jit(solution)/shard_map/ppermute | solution.py:364
  24.6 7.0 %collective-permute-start.5 = (f32[4,4,8,128]{3,2,1,0:T(8,128)S(1)}, f32[4,4,8,128]{3,2,1,0:T(8,128)S(1)}, u32[]{:S(2)}, u32[]{:S(2)}) collective-permute-start(f32[4,4,8,128]{3,2,1,0:T(8,128)S(1)} %get-tuple-element.34), channel_id=1, source_target_pairs={{0,16},{8,24},{16,0},{24,8},{32,48},{40,56},{48,32},{56,40},{64,80... | collective-permute-start | bytes 196616 | tf_op jit(solution)/shard_map/ppermute | solution.py:364
  28.5 5.0 %collective-permute-start.9 = (f32[2,4,8,128]{3,2,1,0:T(8,128)S(1)}, f32[2,4,8,128]{3,2,1,0:T(8,128)S(1)}, u32[]{:S(2)}, u32[]{:S(2)}) collective-permute-start(f32[2,4,8,128]{3,2,1,0:T(8,128)S(1)} %get-tuple-element.41), channel_id=1, source_target_pairs={{0,2},{1,3},{2,0},{3,1},{4,6},{5,7},{6,4},{7,5},{8,10},{9,11},{10,... | collective-permute-start | bytes 98312 | tf_op jit(solution)/shard_map/ppermute | solution.py:364
  31.6 5.5 %collective-permute-start.6 = (f32[2,4,8,128]{3,2,1,0:T(8,128)S(1)}, f32[2,4,8,128]{3,2,1,0:T(8,128)S(1)}, u32[]{:S(2)}, u32[]{:S(2)}) collective-permute-start(f32[2,4,8,128]{3,2,1,0:T(8,128)S(1)} %get-tuple-element.36), channel_id=1, source_target_pairs={{0,32},{8,40},{16,48},{24,56},{32,0},{40,8},{48,16},{56,24},{64,96... | collective-permute-start | bytes 98312 | tf_op jit(solution)/shard_map/ppermute | solution.py:364
  33.5 5.4 %collective-permute-start.10 = (f32[1,4,8,128]{3,2,1,0:T(8,128)S(1)}, f32[1,4,8,128]{3,2,1,0:T(8,128)S(1)}, u32[]{:S(2)}, u32[]{:S(2)}) collective-permute-start(f32[1,4,8,128]{3,2,1,0:T(8,128)S(1)} %get-tuple-element.43), channel_id=1, source_target_pairs={{0,6},{1,7},{2,4},{3,5},{4,2},{5,3},{6,0},{7,1},{8,14},{9,15},{10,... | collective-permute-start | bytes 49160 | tf_op jit(solution)/shard_map/ppermute | solution.py:364
  37.2 5.0 %collective-permute-start.7 = (f32[1,4,8,128]{3,2,1,0:T(8,128)S(1)}, f32[1,4,8,128]{3,2,1,0:T(8,128)S(1)}, u32[]{:S(2)}, u32[]{:S(2)}) collective-permute-start(f32[1,4,8,128]{3,2,1,0:T(8,128)S(1)} %get-tuple-element.38), channel_id=1, source_target_pairs={{0,96},{8,104},{16,112},{24,120},{32,64},{40,72},{48,80},{56,88},{... | collective-permute-start | bytes 49160 | tf_op jit(solution)/shard_map/ppermute | solution.py:364

commit v2 on v1

--- a/solution.py
+++ b/solution.py
@@ -8,17 +8,14 @@
 from jax.sharding import PartitionSpec as P
 
 
-SHEAR = 16
 ROWS = 8
 PIECE = 4
 LOG2E = 1.4426950408889634
-LOAD_COST = 2
 PACK = 1024.0
 ROUNDER = 12582912.0
 GROUP_X, GROUP_Y = 4, 2
 UNROLL_C, UNROLL_E, UNROLL_X, UNROLL_Y = 32, 32, 32, 64
 
-SMEM = pl.BlockSpec(memory_space=pltpu.SMEM)
 VMEM = pl.BlockSpec(memory_space=pltpu.VMEM)
 HBM = pl.BlockSpec(memory_space=pltpu.HBM)
 STAGES = (("gx", (1, 2, 4, 8)), ("gy", (1, 2, 4)))
@@ -41,25 +38,52 @@
                       mode=lax.GatherScatterMode.PROMISE_IN_BOUNDS)
 
 
-def load_kernel(density_ref, cells_ref, face_xa_ref, face_xb_ref, face_ya_ref, face_yb_ref,
-                index_ref, mask_ref, sem):
+def load_kernel(stages, density_ref, table_ref, shear_x_ref, shear_y_ref, turn_ref, cells_ref,
+                face_xa_ref, face_xb_ref, face_ya_ref, face_yb_ref, lut_ref, index_ref, mask_ref,
+                turned_ref, ahead_ref, levels_ref, shifts_x_ref, shifts_y_ref, turns_ref, sems):
     count_x, count_y, cells_z = density_ref.shape
     inner = cells_ref.at[pl.ds(1, count_x), pl.ds(ROWS, count_y), :]
-    copy = pltpu.make_async_copy(density_ref, inner, sem)
-    copy.start()
+    copies = [pltpu.make_async_copy(source, target, sems.at[k]) for k, (source, target) in
+              enumerate(((density_ref, inner), (turn_ref, turns_ref), (shear_x_ref, shifts_x_ref),
+                         (shear_y_ref, shifts_y_ref), (table_ref, levels_ref)))]
+    for copy in copies:
+        copy.start()
 
     lane = lax.broadcasted_iota(jnp.int32, (ROWS, cells_z), 1)
-
-    def shifted(s, carry):
-        source = lane - (s - SHEAR)
-        kept = (source & -cells_z) == 0
-        index_ref[s] = source & (cells_z - 1)
-        mask_ref[s] = jnp.where(kept, -1.0, 0.0)
-        mask_ref[s + 2 * SHEAR] = jnp.where(kept, 1.0, 0.0)
-        return carry
-
-    lax.fori_loop(0, 2 * SHEAR, shifted, 0, unroll=4)
-    copy.wait()
+    row = lax.broadcasted_iota(jnp.int32, (ROWS, cells_z), 0)
+    copies[1].wait()
+    stage = 0
+    for family, (axis, masks) in enumerate(stages):
+        turned = jnp.where(row < PIECE, turns_ref[family, 0], turns_ref[family, 1])
+        for mask in masks:
+            ahead_ref[stage] = jnp.where(turned == jnp.where(is_set(axis, mask), 1, 0), 1.0, 0.0)
+            stage += 1
+
+    for family, shifts_ref in enumerate((shifts_x_ref, shifts_y_ref)):
+        copies[2 + family].wait()
+        count = shifts_ref.shape[1]
+        for v in range(2):
+            turned = turns_ref[family, v]
+            turned_ref[2 * family + v] = jnp.full((ROWS, cells_z), turned, jnp.int32)
+            sign = jnp.full((ROWS, cells_z), jnp.where(turned != 0, 1.0, -1.0), jnp.float32)
+            first = 2 * family * count_x + v * count
+
+            def shifted(i, carry):
+                source = lane - shifts_ref[v, i]
+                inside = source & (cells_z - 1)
+                index_ref[first + i] = inside
+                mask_ref[first + i] = jnp.where(inside == source, sign, 0.0)
+                return carry
+
+            lax.fori_loop(0, count, shifted, 0, unroll=8)
+
+    copies[4].wait()
+    levels = levels_ref[...].astype(jnp.float32)
+    for c in range(4):
+        level = jnp.broadcast_to(levels[c:c + 1], (ROWS, cells_z))
+        rise = jnp.where(lane == cells_z - 1, 0.0, pltpu.roll(level, cells_z - 1, 1) - level)
+        lut_ref[c] = level + rise * (1.0 / PACK)
+    copies[0].wait()
 
     odd_x, odd_y = is_set("gx", 1), is_set("gy", 1)
     first, last = cells_ref[1, pl.ds(ROWS, count_y), :], cells_ref[count_x, pl.ds(ROWS, count_y), :]
@@ -71,16 +95,10 @@
     face_yb_ref[...] = jnp.where(odd_y, first, last)
 
 
-def classify_kernel(step_len, cells_ref, table_ref, field_ref, lut_ref):
+def classify_kernel(step_len, cells_ref, lut_ref, field_ref):
     count_x, cells_z = cells_ref.shape[0] - 2, cells_ref.shape[2]
     count_y = cells_ref.shape[1] - 2 * ROWS
     pitch = field_ref.shape[1] // count_x
-    lane = lax.broadcasted_iota(jnp.int32, (ROWS, cells_z), 1)
-    levels = table_ref[...].astype(jnp.float32)
-    for c in range(4):
-        level = jnp.broadcast_to(levels[c:c + 1], (ROWS, cells_z))
-        rise = jnp.where(lane == cells_z - 1, 0.0, pltpu.roll(level, cells_z - 1, 1) - level)
-        lut_ref[c] = level + rise * (1.0 / PACK)
 
     def body(i, carry):
         slot = slot_of(i, count_x) * pitch
@@ -103,10 +121,8 @@
     lax.fori_loop(0, count_x, body, 0, unroll=UNROLL_C)
 
 
-def march(fields, shift, turned, index_ref, mask_ref, states):
-    place = shift + SHEAR
-    index = index_ref[place]
-    mask = mask_ref[place + jnp.where(turned, 2 * SHEAR, 0)]
+def march(fields, place, turned, index_ref, mask_ref, states):
+    index, mask = index_ref[place], mask_ref[place]
     out = []
     for (red, green, blue, optical), state in zip(fields, states):
         depth = lane_take(optical, index) * mask
@@ -125,22 +141,13 @@
     return [state[1] * fade, state[2] * fade, state[3] * fade, total]
 
 
-def x_kernel(group, stages, turn_ref, shear_ref, face_xa_ref, face_xb_ref, face_ya_ref,
-             face_yb_ref, field_ref, index_ref, mask_ref, _, keep_ref, give_ref, emit_ref,
-             ahead_ref, cells_ref):
+def x_kernel(group, face_xa_ref, face_xb_ref, face_ya_ref, face_yb_ref, field_ref, index_ref,
+             mask_ref, turned_ref, _, keep_ref, give_ref, emit_ref, cells_ref):
     count_x, cells_z = cells_ref.shape[0] - 2, cells_ref.shape[2]
     count_y = cells_ref.shape[1] - 2 * ROWS
     pitch = field_ref.shape[1] // count_x
     pad = ROWS
     lane = lax.broadcasted_iota(jnp.int32, (ROWS, cells_z), 1)
-
-    row = lax.broadcasted_iota(jnp.int32, (ROWS, cells_z), 0)
-    stage = 0
-    for family, (axis, masks) in enumerate(stages):
-        turned = jnp.where(row < PIECE, turn_ref[family, 0], turn_ref[family, 1])
-        for mask in masks:
-            ahead_ref[stage] = jnp.where(turned == jnp.where(is_set(axis, mask), 1, 0), 1.0, 0.0)
-            stage += 1
 
     odd_x, odd_y = is_set("gx", 1), is_set("gy", 1)
     cells_ref[0, pl.ds(pad, count_y), :] = jnp.where(odd_x, face_xb_ref[...], face_xa_ref[...])
@@ -152,7 +159,7 @@
         cells_ref[i + 1, pl.ds(pad - 1, 1), :] = low_y[i:i + 1]
         cells_ref[i + 1, pl.ds(pad + count_y, 1), :] = high_y[i:i + 1]
 
-    turned = [turn_ref[0, v] != 0 for v in range(2)]
+    turned = [turned_ref[v] != 0 for v in range(2)]
     zeros = jnp.zeros((ROWS, cells_z), jnp.float32)
     up, down = (lane + 1) & (cells_z - 1), (lane - 1) & (cells_z - 1)
 
@@ -191,7 +198,7 @@
                 rows = pl.ds(slot + base + g * ROWS, ROWS)
                 fields.append((emit_ref[0, rows, :], emit_ref[1, rows, :], emit_ref[2, rows, :],
                                field_ref[3, rows, :]))
-            return tuple(march(fields, shear_ref[v, i], turned[v], index_ref, mask_ref,
+            return tuple(march(fields, v * count_x + i, turned[v], index_ref, mask_ref,
                                states[v]) for v in range(2))
 
         states = lax.fori_loop(0, count_x, body, (((zeros,) * 4,) * group,) * 2, unroll=UNROLL_X)
@@ -207,13 +214,13 @@
     lax.fori_loop(0, count_y // (ROWS * group), block_of, 0)
 
 
-def y_kernel(group, kept, pitch, turn_ref, shear_ref, emit_ref, field_ref, index_ref, mask_ref,
+def y_kernel(group, kept, count_x, count_y, emit_ref, field_ref, index_ref, mask_ref, turned_ref,
              out_ref):
     cells_z = emit_ref.shape[-1]
-    count_y = shear_ref.shape[1]
+    pitch = emit_ref.shape[1] // count_x
     size = out_ref.shape[0] * PIECE
     first = jnp.where(is_set("gy", 1) == bool(kept), size, 0)
-    turned = [turn_ref[1, v] != 0 for v in range(2)]
+    turned = [turned_ref[2 + v] != 0 for v in range(2)]
     zeros = jnp.zeros((ROWS, cells_z), jnp.float32)
 
     def block_of(block, carry):
@@ -224,7 +231,7 @@
                 rows = pl.ds(start + j, ROWS, stride=pitch)
                 fields.append((emit_ref[0, rows, :], emit_ref[1, rows, :], emit_ref[2, rows, :],
                                field_ref[3, rows, :]))
-            return tuple(march(fields, shear_ref[v, j], turned[v], index_ref, mask_ref,
+            return tuple(march(fields, 2 * count_x + v * count_y + j, turned[v], index_ref, mask_ref,
                                states[v]) for v in range(2))
 
         states = lax.fori_loop(0, count_y, body, (((zeros,) * 4,) * group,) * 2, unroll=UNROLL_Y)
@@ -250,60 +257,66 @@
     return jax.ShapeDtypeStruct(shape, jnp.float32)
 
 
-def load(density):
+def load(density, transfer_table, shear_x, shear_y, direction):
     count_x, count_y, cells_z = density.shape
+    places = 2 * (count_x + count_y)
+    sources = [pltpu.with_memory_space_constraint(a, pltpu.HBM)
+               for a in (density, transfer_table, shear_x, shear_y, direction)]
     return pl.pallas_call(
-        load_kernel,
+        functools.partial(load_kernel, STAGES),
         out_shape=(floats(count_x + 2, count_y + 2 * ROWS, cells_z),
                    floats(count_y, cells_z), floats(count_y, cells_z),
                    floats(count_x, cells_z), floats(count_x, cells_z),
-                   jax.ShapeDtypeStruct((2 * SHEAR, ROWS, cells_z), jnp.int32),
-                   floats(4 * SHEAR, ROWS, cells_z)),
-        in_specs=[HBM],
-        out_specs=(VMEM,) * 7,
-        scratch_shapes=[pltpu.SemaphoreType.DMA],
+                   floats(4, ROWS, cells_z),
+                   jax.ShapeDtypeStruct((places, ROWS, cells_z), jnp.int32),
+                   floats(places, ROWS, cells_z),
+                   jax.ShapeDtypeStruct((4, ROWS, cells_z), jnp.int32),
+                   floats(sum(len(masks) for _, masks in STAGES), ROWS, cells_z)),
+        in_specs=[HBM] * 5,
+        out_specs=(VMEM,) * 10,
+        scratch_shapes=[pltpu.VMEM(transfer_table.shape, jnp.int32),
+                        pltpu.SMEM(shear_x.shape, jnp.int32), pltpu.SMEM(shear_y.shape, jnp.int32),
+                        pltpu.SMEM(direction.shape, jnp.int32), pltpu.SemaphoreType.DMA((5,))],
         name="load",
-        **options(LOAD_COST),
-    )(density)
-
-
-def classify(cells, transfer_table, step_len):
+        **options(2),
+    )(*sources)
+
+
+def classify(cells, lut, step_len):
     count_x, count_y, cells_z = cells.shape[0] - 2, cells.shape[1] - 2 * ROWS, cells.shape[2]
     return pl.pallas_call(
         functools.partial(classify_kernel, step_len),
         out_shape=floats(4, count_x * (count_y + 1), cells_z),
         in_specs=[VMEM, VMEM],
         out_specs=VMEM,
-        scratch_shapes=[pltpu.VMEM((4, ROWS, cells_z), jnp.float32)],
         name="classify",
         **options(3),
-    )(cells, transfer_table)
-
-
-def x_march(cells, halo, field, shifts, shear_x, direction):
+    )(cells, lut)
+
+
+def x_march(cells, halo, field, shifts):
     count_y, cells_z = cells.shape[1] - 2 * ROWS, cells.shape[2]
     part = floats(count_y // (2 * PIECE), 4, 2 * PIECE, cells_z)
-    ahead = floats(sum(len(masks) for _, masks in STAGES), ROWS, cells_z)
     return pl.pallas_call(
-        functools.partial(x_kernel, GROUP_X, STAGES),
-        out_shape=(part, part, floats(3, *field.shape[1:]), ahead, floats(*cells.shape)),
-        in_specs=[SMEM] * 2 + [VMEM] * 8,
-        out_specs=(VMEM,) * 5,
-        input_output_aliases={9: 4},
+        functools.partial(x_kernel, GROUP_X),
+        out_shape=(part, part, floats(3, *field.shape[1:]), floats(*cells.shape)),
+        in_specs=[VMEM] * 9,
+        out_specs=(VMEM,) * 4,
+        input_output_aliases={8: 3},
         name="x_march",
         **options(8),
-    )(direction, shear_x, *halo, field, *shifts, cells)[:4]
-
-
-def y_march(emitted, field, shifts, shear_y, direction, count_x, kept):
+    )(*halo, field, *shifts, cells)[:3]
+
+
+def y_march(emitted, field, shifts, sizes, kept):
     cells_z = field.shape[-1]
     return pl.pallas_call(
-        functools.partial(y_kernel, GROUP_Y, kept, field.shape[1] // count_x),
-        out_shape=floats(count_x // (2 * PIECE), 4, 2 * PIECE, cells_z),
-        in_specs=[SMEM] * 2 + [VMEM] * 4,
+        functools.partial(y_kernel, GROUP_Y, kept, *sizes),
+        out_shape=floats(sizes[0] // (2 * PIECE), 4, 2 * PIECE, cells_z),
+        in_specs=[VMEM] * 5,
         out_specs=VMEM,
         **options(2.5),
-    )(direction, shear_y, emitted, field, *shifts)
+    )(emitted, field, *shifts)
 
 
 def neighbours(axis, offset):
@@ -381,17 +394,17 @@
 def local(density, transfer_table, shear_x, shear_y, direction):
     count_x = density.shape[0]
     step_len = 1.0 / (count_x * lax.axis_size("gx"))
-    cells, *faces, index, mask = load(density)
-    shifts = (index, mask)
+    cells, xa, xb, ya, yb, lut, *shifts, ahead = load(density, transfer_table, shear_x, shear_y,
+                                                      direction)
     halo = [lax.ppermute(face, axis, neighbours(axis, offset)) for face, axis, offset in
-            zip(faces, ("gx", "gx", "gy", "gy"), (1, 0, 1, 0))]
-    field = classify(cells, transfer_table, step_len)
-    keep_x, give_x, emitted, ahead = x_march(cells, halo, field, shifts, shear_x, direction)
+            zip((xa, xb, ya, yb), ("gx", "gx", "gy", "gy"), (1, 0, 1, 0))]
+    field = classify(cells, lut, step_len)
+    keep_x, give_x, emitted = x_march(cells, halo, field, shifts)
 
     x, y = Exchange("gx", 0, ahead), Exchange("gy", len(STAGES[0][1]), ahead)
     x.send(keep_x, give_x, 1)
-    given = y_march(emitted, field, shifts, shear_y, direction, count_x, 0)
-    kept = y_march(emitted, field, shifts, shear_y, direction, count_x, 1)
+    given = y_march(emitted, field, shifts, density.shape[:2], 0)
+    kept = y_march(emitted, field, shifts, density.shape[:2], 1)
     x.send(*x.meet("pair", 2), 2)
     y.send(kept, given, 1)
     x.send(*x.meet("ring_first", 4), 4)

time: 43 us -> 41.7 us (0.970)
  local copies, waits for them, and re-layouts: 1.91 us -> 0 us
  starting transfers between devices: 20.9 us -> 22.4 us
  Pallas kernels: 12.1 us -> 11.5 us
    unnamed x10 -> x0, local copies, waits for them, and re-layouts: 1.91 us -> none
    ppermute x7, starting transfers between devices: 10.5 us -> 12 us  [send(): self.got = lax.ppermute(give, self.axis, swapped(self.axis, mask))]
    pallas_call x4, Pallas kernels: 8.77 us -> 8.2 us  [the longest x1 3.55 us: x_march(): pl.pallas_call(functools.partial(x_kernel, GROUP_X), out_shape=(part, par...]
  transfers between devices with their start and end apart: 11 -> 11, of which waited for: 4 -> 4; matrix products, arithmetic and copies ran while one was open for 0% -> 0% of each run, Pallas kernels for 17% -> 14%
where the time goes in v2:
time: 41.7 us; the launch traced here: 41.6 us
  starting transfers between devices  22.4 us (54%)
  Pallas kernels  11.5 us (28%)
  waiting for transfers between devices  6.91 us (17%)
  between operations  0.75 us (2%)
    ppermute x7, starting transfers between devices, send(): self.got = lax.ppermute(give, self.axis, swapped(self.axis, mask))  12 us
    ppermute x4, starting transfers between devices, local(): lax.ppermute(face, axis, neighbours(axis, offset))  10.5 us
    ppermute x7, waiting for transfers between devices, send(): self.got = lax.ppermute(give, self.axis, swapped(self.axis, mask))  6.9 us
    pallas_call x1, Pallas kernels, x_march(): pl.pallas_call(functools.partial(x_kernel, GROUP_X), out_shape=(part, par...  3.55 us
    pallas_call x2, Pallas kernels, y_march(): pl.pallas_call(functools.partial(y_kernel, GROUP_Y, kept, *sizes), out_sh...  3.2 us
    pallas_call x1, Pallas kernels, classify(): pl.pallas_call(functools.partial(classify_kernel, step_len), out_shape=fl...  1.97 us
    pallas_call x1, Pallas kernels, load(): pl.pallas_call(functools.partial(load_kernel, STAGES), out_shape=(floats(...  1.45 us
    pallas_call x7, Pallas kernels, meet(): pl.pallas_call(functools.partial(stage_kernel, self.axis, mask, self.firs...  1.34 us
  transfers between devices with their start and end apart: 11, of which 4 were waited for; matrix products, arithmetic and copies ran while one was open for 0% of the time, Pallas kernels for 14%

profile of v2, /device:TPU:24, one launch (start us, length us, event | category | flops | bytes accessed | tf_op | source)
XLA Modules:
  0.0 41.6 jit_solution(8522705828727818374)
XLA Ops:
  0.6 1.4 %load.1 = (f32[34,80,128]{2,1,0:T(8,128)S(1)}, f32[64,128]{1,0:T(8,128)S(1)}, f32[64,128]{1,0:T(8,128)S(1)}, f32[32,128]{1,0:T(8,128)S(1)}, f32[32,128]{1,0:T(8,...) custom-call(f32[32,64,128]{2,1,0:T(8,128)} %density_ref.1, ...), custom_call_target="tpu_custom_call" | custom-call | bytes 7000000 | tf_op jit(solution)/shard_map/load/pallas_call | solution.py:265
  2.1 3.4 %collective-permute-start = (f32[64,128]{1,0:T(8,128)S(1)}, f32[64,128]{1,0:T(8,128)S(1)}, u32[]{:S(2)}, u32[]{:S(2)}) collective-permute-start(f32[64,128]{1,0:T(8,128)S(1)} %get-tuple-element.25), channel_id=1, source_target_pairs={{8,16},{24,32},{40,48},{56,64},{72,80},{88,96},{104,112},{16,8},{3... | collective-permute-start | bytes 98312 | tf_op jit(solution)/shard_map/ppermute | solution.py:399
  5.5 0.6 %collective-permute-start.1 = (f32[64,128]{1,0:T(8,128)S(1)}, f32[64,128]{1,0:T(8,128)S(1)}, u32[]{:S(2)}, u32[]{:S(2)}) collective-permute-start(f32[64,128]{1,0:T(8,128)S(1)} %get-tuple-element.26), channel_id=1, source_target_pairs={{0,8},{16,24},{32,40},{48,56},{64,72},{80,88},{96,104},{112,120},{... | collective-permute-start | bytes 98312 | tf_op jit(solution)/shard_map/ppermute | solution.py:399
  6.1 0.7 %collective-permute-start.2 = (f32[32,128]{1,0:T(8,128)S(1)}, f32[32,128]{1,0:T(8,128)S(1)}, u32[]{:S(2)}, u32[]{:S(2)}) collective-permute-start(f32[32,128]{1,0:T(8,128)S(1)} %get-tuple-element.27), channel_id=1, source_target_pairs={{1,2},{3,4},{5,6},{2,1},{4,3},{6,5},{9,10},{11,12},{13,14},{10,9},... | collective-permute-start | bytes 49160 | tf_op jit(solution)/shard_map/ppermute | solution.py:399
  6.8 5.8 %collective-permute-start.3 = (f32[32,128]{1,0:T(8,128)S(1)}, f32[32,128]{1,0:T(8,128)S(1)}, u32[]{:S(2)}, u32[]{:S(2)}) collective-permute-start(f32[32,128]{1,0:T(8,128)S(1)} %get-tuple-element.28), channel_id=1, source_target_pairs={{0,1},{2,3},{4,5},{6,7},{1,0},{3,2},{5,4},{7,6},{8,9},{10,11},{12,... | collective-permute-start | bytes 49160 | tf_op jit(solution)/shard_map/ppermute | solution.py:399
  12.6 2.0 %classify.1.field_ref = f32[4,2080,128]{2,1,0:T(8,128)S(1)} custom-call(f32[34,80,128]{2,1,0:T(8,128)S(1)} %get-tuple-element.29.cells_ref._, f32[4,8,128]{2,1,0:T(8,128)S(1)} %get-tuple-element.30.lut_ref), custom_call_target="tpu_custom_call" | custom-call | bytes 10500000 | tf_op jit(solution)/shard_map/classify/pallas_call | solution.py:287
  14.5 0.0 collective-permute-done.2.face_ya_ref
  14.5 0.0 collective-permute-done.3.face_yb_ref
  14.5 0.0 collective-permute-done.face_xa_ref
  14.6 0.0 collective-permute-done.1.face_xb_ref
  14.6 3.5 %x_march.1 = (f32[8,4,8,128]{3,2,1,0:T(8,128)S(1)}, f32[8,4,8,128]{3,2,1,0:T(8,128)S(1)}, f32[3,2080,128]{2,1,0:T(8,128)S(1)}, f32[34,80,128]{2,1,0:T(8,128)S(1)}) custom-call(f32[64,128]{1,0:T(8,128)S(1)} %collective-permute-done.face_xa_ref, f32[64,128]{1,0:T(8,128)S(1)} %collective-permute-done.1.face_xb_ref, ...), custom_call_target="tpu_custom_call", output_to_operand_aliasing={{3}: (8, {})} | custom-call | bytes 28000000 | tf_op jit(solution)/shard_map/x_march/pallas_call | solution.py:300
  18.1 0.1 collective-permute-start.4
  18.2 1.6 %shard_map.73 = f32[4,4,8,128]{3,2,1,0:T(8,128)S(1)} custom-call(f32[3,2080,128]{2,1,0:T(8,128)S(1)} %get-tuple-element.43.emit_ref, f32[4,2080,128]{2,1,0:T(8,128)S(1)} %classify.1.field_ref, s32[192,8,128]{2,1,0:T(8,128)S(1)} %get-tuple-element.31.index_ref, f32[192,8,128]{2,1,0:T(8,128)S(1)} %get-tuple-element.32.mask_ref, ...), custom_call_target="tpu_custom_call" | custom-call | bytes 8750000 | tf_op jit(solution)/shard_map/pallas_call | solution.py:313
  19.9 3.3 %collective-permute-start.8 = (f32[4,4,8,128]{3,2,1,0:T(8,128)S(1)}, f32[4,4,8,128]{3,2,1,0:T(8,128)S(1)}, u32[]{:S(2)}, u32[]{:S(2)}) collective-permute-start(f32[4,4,8,128]{3,2,1,0:T(8,128)S(1)} %shard_map.73), channel_id=1, source_target_pairs={{0,1},{1,0},{2,3},{3,2},{4,5},{5,4},{6,7},{7,6},{8,9},{9,8},{10,11... | collective-permute-start | bytes 196616 | tf_op jit(solution)/shard_map/ppermute | solution.py:377
  23.2 0.0 collective-permute-done.4.got_ref
  23.2 0.1 collective-permute-start.5
  23.3 1.6 %shard_map.72.keep_ref = f32[4,4,8,128]{3,2,1,0:T(8,128)S(1)} custom-call(f32[3,2080,128]{2,1,0:T(8,128)S(1)} %get-tuple-element.43.emit_ref, f32[4,2080,128]{2,1,0:T(8,128)S(1)} %classify.1.field_ref, s32[192,8,128]{2,1,0:T(8,128)S(1)} %get-tuple-element.31.index_ref, f32[192,8,128]{2,1,0:T(8,128)S(1)} %get-tuple-element.32.mask_ref, ...), custom_call_target="tpu_custom_call" | custom-call | bytes 8750000 | tf_op jit(solution)/shard_map/pallas_call | solution.py:313
  24.9 1.5 %collective-permute-done.8.got_ref = f32[4,4,8,128]{3,2,1,0:T(8,128)S(1)} collective-permute-done((f32[4,4,8,128]{3,2,1,0:T(8,128)S(1)}, f32[4,4,8,128]{3,2,1,0:T(8,128)S(1)}, u32[]{:S(2)}, u32[]{:S(2)}) %collective-permute-start.8) | collective-permute-done | bytes 65568 | tf_op jit(solution)/shard_map/ppermute | solution.py:377
  26.4 3.9 %collective-permute-start.9 = (f32[2,4,8,128]{3,2,1,0:T(8,128)S(1)}, f32[2,4,8,128]{3,2,1,0:T(8,128)S(1)}, u32[]{:S(2)}, u32[]{:S(2)}) collective-permute-start(f32[2,4,8,128]{3,2,1,0:T(8,128)S(1)} %get-tuple-element.45), channel_id=1, source_target_pairs={{0,2},{1,3},{2,0},{3,1},{4,6},{5,7},{6,4},{7,5},{8,10},{9,11},{10,... | collective-permute-start | bytes 98312 | tf_op jit(solution)/shard_map/ppermute | solution.py:377
  30.3 0.0 collective-permute-done.5.got_ref
  30.4 0.8 %collective-permute-start.6 = (f32[2,4,8,128]{3,2,1,0:T(8,128)S(1)}, f32[2,4,8,128]{3,2,1,0:T(8,128)S(1)}, u32[]{:S(2)}, u32[]{:S(2)}) collective-permute-start(f32[2,4,8,128]{3,2,1,0:T(8,128)S(1)} %get-tuple-element.40), channel_id=1, source_target_pairs={{0,32},{8,40},{16,48},{24,56},{32,0},{40,8},{48,16},{56,24},{64,96... | collective-permute-start | bytes 98312 | tf_op jit(solution)/shard_map/ppermute | solution.py:377
  31.2 1.1 %collective-permute-done.9.got_ref = f32[2,4,8,128]{3,2,1,0:T(8,128)S(1)} collective-permute-done((f32[2,4,8,128]{3,2,1,0:T(8,128)S(1)}, f32[2,4,8,128]{3,2,1,0:T(8,128)S(1)}, u32[]{:S(2)}, u32[]{:S(2)}) %collective-permute-start.9) | collective-permute-done | bytes 32800 | tf_op jit(solution)/shard_map/ppermute | solution.py:377
  32.3 3.7 %collective-permute-start.10 = (f32[1,4,8,128]{3,2,1,0:T(8,128)S(1)}, f32[1,4,8,128]{3,2,1,0:T(8,128)S(1)}, u32[]{:S(2)}, u32[]{:S(2)}) collective-permute-start(f32[1,4,8,128]{3,2,1,0:T(8,128)S(1)} %get-tuple-element.47), channel_id=1, source_target_pairs={{0,6},{1,7},{2,4},{3,5},{4,2},{5,3},{6,0},{7,1},{8,14},{9,15},{10,... | collective-permute-start | bytes 49160 | tf_op jit(solution)/shard_map/ppermute | solution.py:377
  35.9 0.0 collective-permute-done.6.got_ref
  35.9 0.1 collective-permute-start.7
  36.0 1.6 %collective-permute-done.10.got_ref = f32[1,4,8,128]{3,2,1,0:T(8,128)S(1)} collective-permute-done((f32[1,4,8,128]{3,2,1,0:T(8,128)S(1)}, f32[1,4,8,128]{3,2,1,0:T(8,128)S(1)}, u32[]{:S(2)}, u32[]{:S(2)}) %collective-permute-start.10) | collective-permute-done | bytes 16416 | tf_op jit(solution)/shard_map/ppermute | solution.py:377
  37.6 0.6 %shard_map.76 = f32[2,4,4,128]{3,2,1,0:T(4,128)} custom-call(f32[1,4,8,128]{3,2,1,0:T(8,128)S(1)} %get-tuple-element.46.keep_ref, f32[1,4,8,128]{3,2,1,0:T(8,128)S(1)} %collective-permute-done.10.got_ref, f32[7,8,128]{2,1,0:T(8,128)S(1)} %get-tuple-element.36.ahead_ref), custom_call_target="tpu_custom_call" | custom-call | bytes 1050000 | tf_op jit(solution)/shard_map/pallas_call | solution.py:385
  38.3 2.7 %collective-permute-done.7.got_ref = f32[1,4,8,128]{3,2,1,0:T(8,128)S(1)} collective-permute-done((f32[1,4,8,128]{3,2,1,0:T(8,128)S(1)}, f32[1,4,8,128]{3,2,1,0:T(8,128)S(1)}, u32[]{:S(2)}, u32[]{:S(2)}) %collective-permute-start.7) | collective-permute-done | bytes 16416 | tf_op jit(solution)/shard_map/ppermute | solution.py:377
  41.0 0.6 %shard_map.71 = f32[2,4,4,128]{3,2,1,0:T(4,128)} custom-call(f32[1,4,8,128]{3,2,1,0:T(8,128)S(1)} %get-tuple-element.41.keep_ref, f32[1,4,8,128]{3,2,1,0:T(8,128)S(1)} %collective-permute-done.7.got_ref, f32[7,8,128]{2,1,0:T(8,128)S(1)} %get-tuple-element.36.ahead_ref), custom_call_target="tpu_custom_call" | custom-call | bytes 1050000 | tf_op jit(solution)/shard_map/pallas_call | solution.py:385
  (5 shorter events, 0.1 us)
Async XLA Ops:
  2.1 12.5 %collective-permute-start = (f32[64,128]{1,0:T(8,128)S(1)}, f32[64,128]{1,0:T(8,128)S(1)}, u32[]{:S(2)}, u32[]{:S(2)}) collective-permute-start(f32[64,128]{1,0:T(8,128)S(1)} %get-tuple-element.25), channel_id=1, source_target_pairs={{8,16},{24,32},{40,48},{56,64},{72,80},{88,96},{104,112},{16,8},{3... | collective-permute-start | bytes 98312 | tf_op jit(solution)/shard_map/ppermute | solution.py:399
  5.5 9.0 %collective-permute-start.1 = (f32[64,128]{1,0:T(8,128)S(1)}, f32[64,128]{1,0:T(8,128)S(1)}, u32[]{:S(2)}, u32[]{:S(2)}) collective-permute-start(f32[64,128]{1,0:T(8,128)S(1)} %get-tuple-element.26), channel_id=1, source_target_pairs={{0,8},{16,24},{32,40},{48,56},{64,72},{80,88},{96,104},{112,120},{... | collective-permute-start | bytes 98312 | tf_op jit(solution)/shard_map/ppermute | solution.py:399
  6.1 8.4 %collective-permute-start.2 = (f32[32,128]{1,0:T(8,128)S(1)}, f32[32,128]{1,0:T(8,128)S(1)}, u32[]{:S(2)}, u32[]{:S(2)}) collective-permute-start(f32[32,128]{1,0:T(8,128)S(1)} %get-tuple-element.27), channel_id=1, source_target_pairs={{1,2},{3,4},{5,6},{2,1},{4,3},{6,5},{9,10},{11,12},{13,14},{10,9},... | collective-permute-start | bytes 49160 | tf_op jit(solution)/shard_map/ppermute | solution.py:399
  6.8 7.8 %collective-permute-start.3 = (f32[32,128]{1,0:T(8,128)S(1)}, f32[32,128]{1,0:T(8,128)S(1)}, u32[]{:S(2)}, u32[]{:S(2)}) collective-permute-start(f32[32,128]{1,0:T(8,128)S(1)} %get-tuple-element.28), channel_id=1, source_target_pairs={{0,1},{2,3},{4,5},{6,7},{1,0},{3,2},{5,4},{7,6},{8,9},{10,11},{12,... | collective-permute-start | bytes 49160 | tf_op jit(solution)/shard_map/ppermute | solution.py:399
  18.1 5.1 %collective-permute-start.4 = (f32[8,4,8,128]{3,2,1,0:T(8,128)S(1)}, f32[8,4,8,128]{3,2,1,0:T(8,128)S(1)}, u32[]{:S(2)}, u32[]{:S(2)}) collective-permute-start(f32[8,4,8,128]{3,2,1,0:T(8,128)S(1)} %get-tuple-element.35), channel_id=1, source_target_pairs={{0,8},{8,0},{16,24},{24,16},{32,40},{40,32},{48,56},{56,48},{64,72... | collective-permute-start | bytes 393224 | tf_op jit(solution)/shard_map/ppermute | solution.py:377
  19.9 6.5 %collective-permute-start.8 = (f32[4,4,8,128]{3,2,1,0:T(8,128)S(1)}, f32[4,4,8,128]{3,2,1,0:T(8,128)S(1)}, u32[]{:S(2)}, u32[]{:S(2)}) collective-permute-start(f32[4,4,8,128]{3,2,1,0:T(8,128)S(1)} %shard_map.73), channel_id=1, source_target_pairs={{0,1},{1,0},{2,3},{3,2},{4,5},{5,4},{6,7},{7,6},{8,9},{9,8},{10,11... | collective-permute-start | bytes 196616 | tf_op jit(solution)/shard_map/ppermute | solution.py:377
  23.2 7.1 %collective-permute-start.5 = (f32[4,4,8,128]{3,2,1,0:T(8,128)S(1)}, f32[4,4,8,128]{3,2,1,0:T(8,128)S(1)}, u32[]{:S(2)}, u32[]{:S(2)}) collective-permute-start(f32[4,4,8,128]{3,2,1,0:T(8,128)S(1)} %get-tuple-element.38), channel_id=1, source_target_pairs={{0,16},{8,24},{16,0},{24,8},{32,48},{40,56},{48,32},{56,40},{64,80... | collective-permute-start | bytes 196616 | tf_op jit(solution)/shard_map/ppermute | solution.py:377
  26.4 5.8 %collective-permute-start.9 = (f32[2,4,8,128]{3,2,1,0:T(8,128)S(1)}, f32[2,4,8,128]{3,2,1,0:T(8,128)S(1)}, u32[]{:S(2)}, u32[]{:S(2)}) collective-permute-start(f32[2,4,8,128]{3,2,1,0:T(8,128)S(1)} %get-tuple-element.45), channel_id=1, source_target_pairs={{0,2},{1,3},{2,0},{3,1},{4,6},{5,7},{6,4},{7,5},{8,10},{9,11},{10,... | collective-permute-start | bytes 98312 | tf_op jit(solution)/shard_map/ppermute | solution.py:377
  30.4 5.5 %collective-permute-start.6 = (f32[2,4,8,128]{3,2,1,0:T(8,128)S(1)}, f32[2,4,8,128]{3,2,1,0:T(8,128)S(1)}, u32[]{:S(2)}, u32[]{:S(2)}) collective-permute-start(f32[2,4,8,128]{3,2,1,0:T(8,128)S(1)} %get-tuple-element.40), channel_id=1, source_target_pairs={{0,32},{8,40},{16,48},{24,56},{32,0},{40,8},{48,16},{56,24},{64,96... | collective-permute-start | bytes 98312 | tf_op jit(solution)/shard_map/ppermute | solution.py:377
  32.3 5.4 %collective-permute-start.10 = (f32[1,4,8,128]{3,2,1,0:T(8,128)S(1)}, f32[1,4,8,128]{3,2,1,0:T(8,128)S(1)}, u32[]{:S(2)}, u32[]{:S(2)}) collective-permute-start(f32[1,4,8,128]{3,2,1,0:T(8,128)S(1)} %get-tuple-element.47), channel_id=1, source_target_pairs={{0,6},{1,7},{2,4},{3,5},{4,2},{5,3},{6,0},{7,1},{8,14},{9,15},{10,... | collective-permute-start | bytes 49160 | tf_op jit(solution)/shard_map/ppermute | solution.py:377
  35.9 5.0 %collective-permute-start.7 = (f32[1,4,8,128]{3,2,1,0:T(8,128)S(1)}, f32[1,4,8,128]{3,2,1,0:T(8,128)S(1)}, u32[]{:S(2)}, u32[]{:S(2)}) collective-permute-start(f32[1,4,8,128]{3,2,1,0:T(8,128)S(1)} %get-tuple-element.42), channel_id=1, source_target_pairs={{0,96},{8,104},{16,112},{24,120},{32,64},{40,72},{48,80},{56,88},{... | collective-permute-start | bytes 49160 | tf_op jit(solution)/shard_map/ppermute | solution.py:377

commit v3 on v2

--- a/solution.py
+++ b/solution.py
@@ -14,7 +14,7 @@
 PACK = 1024.0
 ROUNDER = 12582912.0
 GROUP_X, GROUP_Y = 4, 2
-UNROLL_C, UNROLL_E, UNROLL_X, UNROLL_Y = 32, 32, 32, 64
+UNROLL_C, UNROLL_E, UNROLL_X, UNROLL_Y = 16, 32, 32, 64
 
 VMEM = pl.BlockSpec(memory_space=pltpu.VMEM)
 HBM = pl.BlockSpec(memory_space=pltpu.HBM)
@@ -39,8 +39,8 @@
 
 
 def load_kernel(stages, density_ref, table_ref, shear_x_ref, shear_y_ref, turn_ref, cells_ref,
-                face_xa_ref, face_xb_ref, face_ya_ref, face_yb_ref, lut_ref, index_ref, mask_ref,
-                turned_ref, ahead_ref, levels_ref, shifts_x_ref, shifts_y_ref, turns_ref, sems):
+                face_xa_ref, share_ref, own_ref, lut_ref, index_ref, mask_ref, turned_ref,
+                ahead_ref, levels_ref, shifts_x_ref, shifts_y_ref, turns_ref, sems):
     count_x, count_y, cells_z = density_ref.shape
     inner = cells_ref.at[pl.ds(1, count_x), pl.ds(ROWS, count_y), :]
     copies = [pltpu.make_async_copy(source, target, sems.at[k]) for k, (source, target) in
@@ -88,20 +88,29 @@
     odd_x, odd_y = is_set("gx", 1), is_set("gy", 1)
     first, last = cells_ref[1, pl.ds(ROWS, count_y), :], cells_ref[count_x, pl.ds(ROWS, count_y), :]
     face_xa_ref[...] = jnp.where(odd_x, last, first)
-    face_xb_ref[...] = jnp.where(odd_x, first, last)
+    share_ref[pl.ds(0, count_y), :] = jnp.where(odd_x, first, last)
     first, last = (cells_ref[pl.ds(1, count_x), ROWS, :],
                    cells_ref[pl.ds(1, count_x), ROWS + count_y - 1, :])
-    face_ya_ref[...] = jnp.where(odd_y, last, first)
-    face_yb_ref[...] = jnp.where(odd_y, first, last)
-
-
-def classify_kernel(step_len, cells_ref, lut_ref, field_ref):
+    outward = odd_x == odd_y
+    share_ref[pl.ds(count_y, count_x), :] = jnp.where(outward, first, last)
+    own_ref[...] = jnp.where(outward, last, first)
+
+
+def relay_kernel(own_ref, shared_ref, out_ref):
+    rows = own_ref.shape[0]
+    out_ref[pl.ds(0, rows), :] = own_ref[...]
+    out_ref[pl.ds(rows, rows), :] = shared_ref[pl.ds(shared_ref.shape[0] - rows, rows), :]
+
+
+def classify_kernel(step_len, parity, cells_ref, lut_ref, *refs):
+    field_ref = refs[-1]
     count_x, cells_z = cells_ref.shape[0] - 2, cells_ref.shape[2]
     count_y = cells_ref.shape[1] - 2 * ROWS
     pitch = field_ref.shape[1] // count_x
 
-    def body(i, carry):
-        slot = slot_of(i, count_x) * pitch
+    def body(t, carry):
+        i = (t // PIECE * 2 + parity) * PIECE + t % PIECE
+        slot = (t + parity * (count_x // 2)) * pitch
         for base in range(0, count_y, ROWS):
             scaled = cells_ref[i + 1, pl.ds(ROWS + base, ROWS), :] * (cells_z - 1.0)
             knot = scaled.astype(jnp.int32)
@@ -118,7 +127,7 @@
                 field_ref[c, pl.ds(slot + base, ROWS), :] = values[c]
         return carry
 
-    lax.fori_loop(0, count_x, body, 0, unroll=UNROLL_C)
+    lax.fori_loop(0, count_x // 2, body, 0, unroll=UNROLL_C)
 
 
 def march(fields, place, turned, index_ref, mask_ref, states):
@@ -141,7 +150,7 @@
     return [state[1] * fade, state[2] * fade, state[3] * fade, total]
 
 
-def x_kernel(group, face_xa_ref, face_xb_ref, face_ya_ref, face_yb_ref, field_ref, index_ref,
+def x_kernel(group, face_xa_ref, shared_ref, crossed_ref, returned_ref, field_ref, index_ref,
              mask_ref, turned_ref, _, keep_ref, give_ref, emit_ref, cells_ref):
     count_x, cells_z = cells_ref.shape[0] - 2, cells_ref.shape[2]
     count_y = cells_ref.shape[1] - 2 * ROWS
@@ -150,11 +159,12 @@
     lane = lax.broadcasted_iota(jnp.int32, (ROWS, cells_z), 1)
 
     odd_x, odd_y = is_set("gx", 1), is_set("gy", 1)
-    cells_ref[0, pl.ds(pad, count_y), :] = jnp.where(odd_x, face_xb_ref[...], face_xa_ref[...])
-    cells_ref[count_x + 1, pl.ds(pad, count_y), :] = jnp.where(odd_x, face_xa_ref[...],
-                                                               face_xb_ref[...])
-    low_y = jnp.where(odd_y, face_yb_ref[...], face_ya_ref[...])
-    high_y = jnp.where(odd_y, face_ya_ref[...], face_yb_ref[...])
+    near, far = face_xa_ref[...], shared_ref[pl.ds(0, count_y), :]
+    cells_ref[0, pl.ds(pad, count_y), :] = jnp.where(odd_x, far, near)
+    cells_ref[count_x + 1, pl.ds(pad, count_y), :] = jnp.where(odd_x, near, far)
+    own, other = crossed_ref[pl.ds(0, count_x), :], returned_ref[pl.ds(count_x, count_x), :]
+    outward = odd_x == odd_y
+    low_y, high_y = jnp.where(outward, other, own), jnp.where(outward, own, other)
     for i in range(count_x):
         cells_ref[i + 1, pl.ds(pad - 1, 1), :] = low_y[i:i + 1]
         cells_ref[i + 1, pl.ds(pad + count_y, 1), :] = high_y[i:i + 1]
@@ -265,15 +275,15 @@
     return pl.pallas_call(
         functools.partial(load_kernel, STAGES),
         out_shape=(floats(count_x + 2, count_y + 2 * ROWS, cells_z),
-                   floats(count_y, cells_z), floats(count_y, cells_z),
-                   floats(count_x, cells_z), floats(count_x, cells_z),
+                   floats(count_y, cells_z), floats(count_y + count_x, cells_z),
+                   floats(count_x, cells_z),
                    floats(4, ROWS, cells_z),
                    jax.ShapeDtypeStruct((places, ROWS, cells_z), jnp.int32),
                    floats(places, ROWS, cells_z),
                    jax.ShapeDtypeStruct((4, ROWS, cells_z), jnp.int32),
                    floats(sum(len(masks) for _, masks in STAGES), ROWS, cells_z)),
         in_specs=[HBM] * 5,
-        out_specs=(VMEM,) * 10,
+        out_specs=(VMEM,) * 9,
         scratch_shapes=[pltpu.VMEM(transfer_table.shape, jnp.int32),
                         pltpu.SMEM(shear_x.shape, jnp.int32), pltpu.SMEM(shear_y.shape, jnp.int32),
                         pltpu.SMEM(direction.shape, jnp.int32), pltpu.SemaphoreType.DMA((5,))],
@@ -282,16 +292,27 @@
     )(*sources)
 
 
-def classify(cells, lut, step_len):
+def relay(own, shared):
+    return pl.pallas_call(
+        relay_kernel,
+        out_shape=floats(2 * own.shape[0], own.shape[1]),
+        in_specs=[VMEM, VMEM],
+        out_specs=VMEM,
+        name="relay",
+        **options(0.3),
+    )(own, shared)
+
+
+def classify(cells, lut, step_len, part, *before):
     count_x, count_y, cells_z = cells.shape[0] - 2, cells.shape[1] - 2 * ROWS, cells.shape[2]
     return pl.pallas_call(
-        functools.partial(classify_kernel, step_len),
+        functools.partial(classify_kernel, step_len, part),
         out_shape=floats(4, count_x * (count_y + 1), cells_z),
-        in_specs=[VMEM, VMEM],
+        in_specs=[VMEM] * (2 + len(before)),
         out_specs=VMEM,
-        name="classify",
-        **options(3),
-    )(cells, lut)
+        input_output_aliases={2: 0} if before else {},
+        **options(1.5),
+    )(cells, lut, *before)
 
 
 def x_march(cells, halo, field, shifts):
@@ -323,6 +344,12 @@
     count = lax.axis_size(axis)
     pairs = [(i, i + 1) for i in range(offset, count - 1, 2)]
     return pairs + [(target, source) for source, target in pairs]
+
+
+def crossings():
+    count = lax.axis_size("gy")
+    return [(i * count + source, i * count + target) for i in range(lax.axis_size("gx"))
+            for source, target in neighbours("gy", i % 2)]
 
 
 def swapped(axis, mask):
@@ -394,11 +421,15 @@
 def local(density, transfer_table, shear_x, shear_y, direction):
     count_x = density.shape[0]
     step_len = 1.0 / (count_x * lax.axis_size("gx"))
-    cells, xa, xb, ya, yb, lut, *shifts, ahead = load(density, transfer_table, shear_x, shear_y,
-                                                      direction)
-    halo = [lax.ppermute(face, axis, neighbours(axis, offset)) for face, axis, offset in
-            zip((xa, xb, ya, yb), ("gx", "gx", "gy", "gy"), (1, 0, 1, 0))]
-    field = classify(cells, lut, step_len)
+    cells, face, share, own, lut, *shifts, ahead = load(density, transfer_table, shear_x, shear_y,
+                                                        direction)
+    shared = lax.ppermute(share, "gx", swapped("gx", 1))
+    faced = lax.ppermute(face, "gx", neighbours("gx", 1))
+    crossed = lax.ppermute(relay(own, shared), ("gx", "gy"), crossings())
+    returned = lax.ppermute(crossed, "gx", swapped("gx", 1))
+    field = classify(cells, lut, step_len, 0)
+    field = classify(cells, lut, step_len, 1, field)
+    halo = (faced, shared, crossed, returned)
     keep_x, give_x, emitted = x_march(cells, halo, field, shifts)
 
     x, y = Exchange("gx", 0, ahead), Exchange("gy", len(STAGES[0][1]), ahead)

time: 41.7 us -> 39.9 us (0.957)
  starting transfers between devices: 22.4 us -> 17.3 us
  waiting for transfers between devices: 6.91 us -> 10 us
    ppermute x7, starting transfers between devices: 12 us -> 8.36 us  [send(): self.got = lax.ppermute(give, self.axis, swapped(self.axis, mask))]
    ppermute x4, waiting for transfers between devices: 0.01 us -> 2.16 us  [the longest x1 1.22 us: local(): shared = lax.ppermute(share, 'gx', swapped('gx', 1))]
    ppermute x4, starting transfers between devices: 10.5 us -> 8.98 us  [the longest x1 5.77 us: local(): crossed = lax.ppermute(relay(own, shared), ('gx', 'gy'), crossings())]
    ppermute x7, waiting for transfers between devices: 6.9 us -> 7.89 us  [send(): self.got = lax.ppermute(give, self.axis, swapped(self.axis, mask))]
    pallas_call x1 -> x3, Pallas kernels: 1.97 us -> 2.05 us  [the longest x2 2.05 us: classify(): pl.pallas_call(functools.partial(classify_kernel, step_len, part), out_sh...]
  transfers between devices with their start and end apart: 11 -> 11, of which waited for: 4 -> 6; matrix products, arithmetic and copies ran while one was open for 0% -> 0% of each run, Pallas kernels for 14% -> 15%
where the time goes in v3:
time: 39.9 us; the launch traced here: 39.7 us
  starting transfers between devices  17.3 us (43%)
  Pallas kernels  11.6 us (29%)
  waiting for transfers between devices  10 us (25%)
  between operations  0.73 us (2%)
    ppermute x7, starting transfers between devices, send(): self.got = lax.ppermute(give, self.axis, swapped(self.axis, mask))  8.36 us
    ppermute x7, waiting for transfers between devices, send(): self.got = lax.ppermute(give, self.axis, swapped(self.axis, mask))  7.89 us
    ppermute x1, starting transfers between devices, local(): crossed = lax.ppermute(relay(own, shared), ('gx', 'gy'), crossings())  5.77 us
    pallas_call x1, Pallas kernels, x_march(): pl.pallas_call(functools.partial(x_kernel, GROUP_X), out_shape=(part, par...  3.54 us
    pallas_call x2, Pallas kernels, y_march(): pl.pallas_call(functools.partial(y_kernel, GROUP_Y, kept, *sizes), out_sh...  3.19 us
    pallas_call x2, Pallas kernels, classify(): pl.pallas_call(functools.partial(classify_kernel, step_len, part), out_sh...  2.05 us
    ppermute x1, starting transfers between devices, local(): faced = lax.ppermute(face, 'gx', neighbours('gx', 1))  1.92 us
    pallas_call x1, Pallas kernels, load(): pl.pallas_call(functools.partial(load_kernel, STAGES), out_shape=(floats(...  1.45 us
  transfers between devices with their start and end apart: 11, of which 6 were waited for; matrix products, arithmetic and copies ran while one was open for 0% of the time, Pallas kernels for 15%

profile of v3, /device:TPU:24, one launch (start us, length us, event | category | flops | bytes accessed | tf_op | source)
XLA Modules:
  0.0 39.7 jit_solution(3270532122479860264)
XLA Ops:
  0.6 1.4 %load.1 = (f32[34,80,128]{2,1,0:T(8,128)S(1)}, f32[64,128]{1,0:T(8,128)S(1)}, f32[96,128]{1,0:T(8,128)S(1)}, f32[32,128]{1,0:T(8,128)S(1)}, f32[4,8,128]{2,1,0:T...) custom-call(f32[32,64,128]{2,1,0:T(8,128)} %density_ref.1, ...), custom_call_target="tpu_custom_call" | custom-call | bytes 7000000 | tf_op jit(solution)/shard_map/load/pallas_call | solution.py:275
  2.1 0.1 collective-permute-start.1
  2.2 1.2 %collective-permute-done.1.shared_ref = f32[96,128]{1,0:T(8,128)S(1)} collective-permute-done((f32[96,128]{1,0:T(8,128)S(1)}, f32[96,128]{1,0:T(8,128)S(1)}, u32[]{:S(2)}, u32[]{:S(2)}) %collective-permute-start.1) | collective-permute-done | bytes 49184 | tf_op jit(solution)/shard_map/ppermute | solution.py:426
  3.4 5.8 %collective-permute-start.2 = (f32[64,128]{1,0:T(8,128)S(1)}, f32[64,128]{1,0:T(8,128)S(1)}, u32[]{:S(2)}, u32[]{:S(2)}) collective-permute-start(f32[64,128]{1,0:T(8,128)S(1)} %relay.1), channel_id=1, source_target_pairs={{0,1},{2,3},{4,5},{6,7},{1,0},{3,2},{5,4},{7,6},{9,10},{11,12},{13... | collective-permute-start | bytes 98312 | tf_op jit(solution)/shard_map/ppermute | solution.py:428
  9.2 1.9 %collective-permute-start = (f32[64,128]{1,0:T(8,128)S(1)}, f32[64,128]{1,0:T(8,128)S(1)}, u32[]{:S(2)}, u32[]{:S(2)}) collective-permute-start(f32[64,128]{1,0:T(8,128)S(1)} %get-tuple-element.24), channel_id=1, source_target_pairs={{8,16},{24,32},{40,48},{56,64},{72,80},{88,96},{104,112},{16,8},{3... | collective-permute-start | bytes 98312 | tf_op jit(solution)/shard_map/ppermute | solution.py:427
  11.1 0.0 collective-permute-done.2.crossed_ref
  11.1 1.2 %collective-permute-start.3 = (f32[64,128]{1,0:T(8,128)S(1)}, f32[64,128]{1,0:T(8,128)S(1)}, u32[]{:S(2)}, u32[]{:S(2)}) collective-permute-start(f32[64,128]{1,0:T(8,128)S(1)} %collective-permute-done.2.crossed_ref), channel_id=1, source_target_pairs={{0,8},{8,0},{16,24},{24,16},{32,40},{40,32},{48,56},{56,48},{64,72... | collective-permute-start | bytes 98312 | tf_op jit(solution)/shard_map/ppermute | solution.py:429
  12.3 1.0 %shard_map.68.refs_0_ = f32[4,2080,128]{2,1,0:T(8,128)S(1)} custom-call(f32[34,80,128]{2,1,0:T(8,128)S(1)} %get-tuple-element.27.cells_ref._, f32[4,8,128]{2,1,0:T(8,128)S(1)} %get-tuple-element.28.lut_ref), custom_call_target="tpu_custom_call" | custom-call | bytes 5250000 | tf_op jit(solution)/shard_map/pallas_call | solution.py:308
  13.3 1.0 %shard_map.69.field_ref = f32[4,2080,128]{2,1,0:T(8,128)S(1)} custom-call(f32[34,80,128]{2,1,0:T(8,128)S(1)} %get-tuple-element.27.cells_ref._, f32[4,8,128]{2,1,0:T(8,128)S(1)} %get-tuple-element.28.lut_ref, f32[4,2080,128]{2,1,0:T(8,128)S(1)} %shard_map.68.refs_0_), custom_call_target="tpu_custom_call", output_to_operand_aliasing={{}: (2, {})} | custom-call | bytes 5250000 | tf_op jit(solution)/shard_map/pallas_call | solution.py:308
  14.4 0.9 %collective-permute-done.face_xa_ref = f32[64,128]{1,0:T(8,128)S(1)} collective-permute-done((f32[64,128]{1,0:T(8,128)S(1)}, f32[64,128]{1,0:T(8,128)S(1)}, u32[]{:S(2)}, u32[]{:S(2)}) %collective-permute-start) | collective-permute-done | bytes 32800 | tf_op jit(solution)/shard_map/ppermute | solution.py:427
  15.3 0.0 collective-permute-done.3.returned_ref
  15.3 3.5 %x_march.1 = (f32[8,4,8,128]{3,2,1,0:T(8,128)S(1)}, f32[8,4,8,128]{3,2,1,0:T(8,128)S(1)}, f32[3,2080,128]{2,1,0:T(8,128)S(1)}, f32[34,80,128]{2,1,0:T(8,128)S(1)}) custom-call(f32[64,128]{1,0:T(8,128)S(1)} %collective-permute-done.face_xa_ref, f32[96,128]{1,0:T(8,128)S(1)} %collective-permute-done.1.shared_ref, ...), custom_call_target="tpu_custom_call", output_to_operand_aliasing={{3}: (8, {})} | custom-call | bytes 28000000 | tf_op jit(solution)/shard_map/x_march/pallas_call | solution.py:321
  18.9 0.1 collective-permute-start.4
  19.0 1.6 %shard_map.75 = f32[4,4,8,128]{3,2,1,0:T(8,128)S(1)} custom-call(f32[3,2080,128]{2,1,0:T(8,128)S(1)} %get-tuple-element.41.emit_ref, f32[4,2080,128]{2,1,0:T(8,128)S(1)} %shard_map.69.field_ref, s32[192,8,128]{2,1,0:T(8,128)S(1)} %get-tuple-element.29.index_ref, f32[192,8,128]{2,1,0:T(8,128)S(1)} %get-tuple-element.30.mask_ref, ...), custom_call_target="tpu_custom_call" | custom-call | bytes 8750000 | tf_op jit(solution)/shard_map/pallas_call | solution.py:334
  20.6 2.2 %collective-permute-start.8 = (f32[4,4,8,128]{3,2,1,0:T(8,128)S(1)}, f32[4,4,8,128]{3,2,1,0:T(8,128)S(1)}, u32[]{:S(2)}, u32[]{:S(2)}) collective-permute-start(f32[4,4,8,128]{3,2,1,0:T(8,128)S(1)} %shard_map.75), channel_id=1, source_target_pairs={{0,1},{1,0},{2,3},{3,2},{4,5},{5,4},{6,7},{7,6},{8,9},{9,8},{10,11... | collective-permute-start | bytes 196616 | tf_op jit(solution)/shard_map/ppermute | solution.py:404
  22.8 0.0 collective-permute-done.4.got_ref
  22.8 1.1 %collective-permute-start.5 = (f32[4,4,8,128]{3,2,1,0:T(8,128)S(1)}, f32[4,4,8,128]{3,2,1,0:T(8,128)S(1)}, u32[]{:S(2)}, u32[]{:S(2)}) collective-permute-start(f32[4,4,8,128]{3,2,1,0:T(8,128)S(1)} %get-tuple-element.36), channel_id=1, source_target_pairs={{0,16},{8,24},{16,0},{24,8},{32,48},{40,56},{48,32},{56,40},{64,80... | collective-permute-start | bytes 196616 | tf_op jit(solution)/shard_map/ppermute | solution.py:404
  23.9 1.6 %shard_map.74.keep_ref = f32[4,4,8,128]{3,2,1,0:T(8,128)S(1)} custom-call(f32[3,2080,128]{2,1,0:T(8,128)S(1)} %get-tuple-element.41.emit_ref, f32[4,2080,128]{2,1,0:T(8,128)S(1)} %shard_map.69.field_ref, s32[192,8,128]{2,1,0:T(8,128)S(1)} %get-tuple-element.29.index_ref, f32[192,8,128]{2,1,0:T(8,128)S(1)} %get-tuple-element.30.mask_ref, ...), custom_call_target="tpu_custom_call" | custom-call | bytes 8750000 | tf_op jit(solution)/shard_map/pallas_call | solution.py:334
  25.5 1.7 %collective-permute-done.8.got_ref = f32[4,4,8,128]{3,2,1,0:T(8,128)S(1)} collective-permute-done((f32[4,4,8,128]{3,2,1,0:T(8,128)S(1)}, f32[4,4,8,128]{3,2,1,0:T(8,128)S(1)}, u32[]{:S(2)}, u32[]{:S(2)}) %collective-permute-start.8) | collective-permute-done | bytes 65568 | tf_op jit(solution)/shard_map/ppermute | solution.py:404
  27.2 1.6 %collective-permute-start.9 = (f32[2,4,8,128]{3,2,1,0:T(8,128)S(1)}, f32[2,4,8,128]{3,2,1,0:T(8,128)S(1)}, u32[]{:S(2)}, u32[]{:S(2)}) collective-permute-start(f32[2,4,8,128]{3,2,1,0:T(8,128)S(1)} %get-tuple-element.43), channel_id=1, source_target_pairs={{0,2},{1,3},{2,0},{3,1},{4,6},{5,7},{6,4},{7,5},{8,10},{9,11},{10,... | collective-permute-start | bytes 98312 | tf_op jit(solution)/shard_map/ppermute | solution.py:404
  28.8 0.0 collective-permute-done.5.got_ref
  28.8 0.5 %collective-permute-start.6 = (f32[2,4,8,128]{3,2,1,0:T(8,128)S(1)}, f32[2,4,8,128]{3,2,1,0:T(8,128)S(1)}, u32[]{:S(2)}, u32[]{:S(2)}) collective-permute-start(f32[2,4,8,128]{3,2,1,0:T(8,128)S(1)} %get-tuple-element.38), channel_id=1, source_target_pairs={{0,32},{8,40},{16,48},{24,56},{32,0},{40,8},{48,16},{56,24},{64,96... | collective-permute-start | bytes 98312 | tf_op jit(solution)/shard_map/ppermute | solution.py:404
  29.3 1.9 %collective-permute-done.9.got_ref = f32[2,4,8,128]{3,2,1,0:T(8,128)S(1)} collective-permute-done((f32[2,4,8,128]{3,2,1,0:T(8,128)S(1)}, f32[2,4,8,128]{3,2,1,0:T(8,128)S(1)}, u32[]{:S(2)}, u32[]{:S(2)}) %collective-permute-start.9) | collective-permute-done | bytes 32800 | tf_op jit(solution)/shard_map/ppermute | solution.py:404
  31.2 2.8 %collective-permute-start.10 = (f32[1,4,8,128]{3,2,1,0:T(8,128)S(1)}, f32[1,4,8,128]{3,2,1,0:T(8,128)S(1)}, u32[]{:S(2)}, u32[]{:S(2)}) collective-permute-start(f32[1,4,8,128]{3,2,1,0:T(8,128)S(1)} %get-tuple-element.45), channel_id=1, source_target_pairs={{0,6},{1,7},{2,4},{3,5},{4,2},{5,3},{6,0},{7,1},{8,14},{9,15},{10,... | collective-permute-start | bytes 49160 | tf_op jit(solution)/shard_map/ppermute | solution.py:404
  34.0 0.0 collective-permute-done.6.got_ref
  34.1 0.1 collective-permute-start.7
  34.1 2.1 %collective-permute-done.10.got_ref = f32[1,4,8,128]{3,2,1,0:T(8,128)S(1)} collective-permute-done((f32[1,4,8,128]{3,2,1,0:T(8,128)S(1)}, f32[1,4,8,128]{3,2,1,0:T(8,128)S(1)}, u32[]{:S(2)}, u32[]{:S(2)}) %collective-permute-start.10) | collective-permute-done | bytes 16416 | tf_op jit(solution)/shard_map/ppermute | solution.py:404
  36.2 0.6 %shard_map.78 = f32[2,4,4,128]{3,2,1,0:T(4,128)} custom-call(f32[1,4,8,128]{3,2,1,0:T(8,128)S(1)} %get-tuple-element.44.keep_ref, f32[1,4,8,128]{3,2,1,0:T(8,128)S(1)} %collective-permute-done.10.got_ref, f32[7,8,128]{2,1,0:T(8,128)S(1)} %get-tuple-element.34.ahead_ref), custom_call_target="tpu_custom_call" | custom-call | bytes 1050000 | tf_op jit(solution)/shard_map/pallas_call | solution.py:412
  36.8 2.2 %collective-permute-done.7.got_ref = f32[1,4,8,128]{3,2,1,0:T(8,128)S(1)} collective-permute-done((f32[1,4,8,128]{3,2,1,0:T(8,128)S(1)}, f32[1,4,8,128]{3,2,1,0:T(8,128)S(1)}, u32[]{:S(2)}, u32[]{:S(2)}) %collective-permute-start.7) | collective-permute-done | bytes 16416 | tf_op jit(solution)/shard_map/ppermute | solution.py:404
  39.1 0.6 %shard_map.73 = f32[2,4,4,128]{3,2,1,0:T(4,128)} custom-call(f32[1,4,8,128]{3,2,1,0:T(8,128)S(1)} %get-tuple-element.39.keep_ref, f32[1,4,8,128]{3,2,1,0:T(8,128)S(1)} %collective-permute-done.7.got_ref, f32[7,8,128]{2,1,0:T(8,128)S(1)} %get-tuple-element.34.ahead_ref), custom_call_target="tpu_custom_call" | custom-call | bytes 1050000 | tf_op jit(solution)/shard_map/pallas_call | solution.py:412
  (6 shorter events, 0.1 us)
Async XLA Ops:
  2.1 1.3 %collective-permute-start.1 = (f32[96,128]{1,0:T(8,128)S(1)}, f32[96,128]{1,0:T(8,128)S(1)}, u32[]{:S(2)}, u32[]{:S(2)}) collective-permute-start(f32[96,128]{1,0:T(8,128)S(1)} %get-tuple-element.25), channel_id=1, source_target_pairs={{0,8},{8,0},{16,24},{24,16},{32,40},{40,32},{48,56},{56,48},{64,72... | collective-permute-start | bytes 147464 | tf_op jit(solution)/shard_map/ppermute | solution.py:426
  3.4 7.7 %collective-permute-start.2 = (f32[64,128]{1,0:T(8,128)S(1)}, f32[64,128]{1,0:T(8,128)S(1)}, u32[]{:S(2)}, u32[]{:S(2)}) collective-permute-start(f32[64,128]{1,0:T(8,128)S(1)} %relay.1), channel_id=1, source_target_pairs={{0,1},{2,3},{4,5},{6,7},{1,0},{3,2},{5,4},{7,6},{9,10},{11,12},{13... | collective-permute-start | bytes 98312 | tf_op jit(solution)/shard_map/ppermute | solution.py:428
  9.2 6.1 %collective-permute-start = (f32[64,128]{1,0:T(8,128)S(1)}, f32[64,128]{1,0:T(8,128)S(1)}, u32[]{:S(2)}, u32[]{:S(2)}) collective-permute-start(f32[64,128]{1,0:T(8,128)S(1)} %get-tuple-element.24), channel_id=1, source_target_pairs={{8,16},{24,32},{40,48},{56,64},{72,80},{88,96},{104,112},{16,8},{3... | collective-permute-start | bytes 98312 | tf_op jit(solution)/shard_map/ppermute | solution.py:427
  11.1 4.2 %collective-permute-start.3 = (f32[64,128]{1,0:T(8,128)S(1)}, f32[64,128]{1,0:T(8,128)S(1)}, u32[]{:S(2)}, u32[]{:S(2)}) collective-permute-start(f32[64,128]{1,0:T(8,128)S(1)} %collective-permute-done.2.crossed_ref), channel_id=1, source_target_pairs={{0,8},{8,0},{16,24},{24,16},{32,40},{40,32},{48,56},{56,48},{64,72... | collective-permute-start | bytes 98312 | tf_op jit(solution)/shard_map/ppermute | solution.py:429
  18.9 3.9 %collective-permute-start.4 = (f32[8,4,8,128]{3,2,1,0:T(8,128)S(1)}, f32[8,4,8,128]{3,2,1,0:T(8,128)S(1)}, u32[]{:S(2)}, u32[]{:S(2)}) collective-permute-start(f32[8,4,8,128]{3,2,1,0:T(8,128)S(1)} %get-tuple-element.33), channel_id=1, source_target_pairs={{0,8},{8,0},{16,24},{24,16},{32,40},{40,32},{48,56},{56,48},{64,72... | collective-permute-start | bytes 393224 | tf_op jit(solution)/shard_map/ppermute | solution.py:404
  20.6 6.6 %collective-permute-start.8 = (f32[4,4,8,128]{3,2,1,0:T(8,128)S(1)}, f32[4,4,8,128]{3,2,1,0:T(8,128)S(1)}, u32[]{:S(2)}, u32[]{:S(2)}) collective-permute-start(f32[4,4,8,128]{3,2,1,0:T(8,128)S(1)} %shard_map.75), channel_id=1, source_target_pairs={{0,1},{1,0},{2,3},{3,2},{4,5},{5,4},{6,7},{7,6},{8,9},{9,8},{10,11... | collective-permute-start | bytes 196616 | tf_op jit(solution)/shard_map/ppermute | solution.py:404
  22.8 5.9 %collective-permute-start.5 = (f32[4,4,8,128]{3,2,1,0:T(8,128)S(1)}, f32[4,4,8,128]{3,2,1,0:T(8,128)S(1)}, u32[]{:S(2)}, u32[]{:S(2)}) collective-permute-start(f32[4,4,8,128]{3,2,1,0:T(8,128)S(1)} %get-tuple-element.36), channel_id=1, source_target_pairs={{0,16},{8,24},{16,0},{24,8},{32,48},{40,56},{48,32},{56,40},{64,80... | collective-permute-start | bytes 196616 | tf_op jit(solution)/shard_map/ppermute | solution.py:404
  27.2 4.0 %collective-permute-start.9 = (f32[2,4,8,128]{3,2,1,0:T(8,128)S(1)}, f32[2,4,8,128]{3,2,1,0:T(8,128)S(1)}, u32[]{:S(2)}, u32[]{:S(2)}) collective-permute-start(f32[2,4,8,128]{3,2,1,0:T(8,128)S(1)} %get-tuple-element.43), channel_id=1, source_target_pairs={{0,2},{1,3},{2,0},{3,1},{4,6},{5,7},{6,4},{7,5},{8,10},{9,11},{10,... | collective-permute-start | bytes 98312 | tf_op jit(solution)/shard_map/ppermute | solution.py:404
  28.8 5.2 %collective-permute-start.6 = (f32[2,4,8,128]{3,2,1,0:T(8,128)S(1)}, f32[2,4,8,128]{3,2,1,0:T(8,128)S(1)}, u32[]{:S(2)}, u32[]{:S(2)}) collective-permute-start(f32[2,4,8,128]{3,2,1,0:T(8,128)S(1)} %get-tuple-element.38), channel_id=1, source_target_pairs={{0,32},{8,40},{16,48},{24,56},{32,0},{40,8},{48,16},{56,24},{64,96... | collective-permute-start | bytes 98312 | tf_op jit(solution)/shard_map/ppermute | solution.py:404
  31.2 5.0 %collective-permute-start.10 = (f32[1,4,8,128]{3,2,1,0:T(8,128)S(1)}, f32[1,4,8,128]{3,2,1,0:T(8,128)S(1)}, u32[]{:S(2)}, u32[]{:S(2)}) collective-permute-start(f32[1,4,8,128]{3,2,1,0:T(8,128)S(1)} %get-tuple-element.45), channel_id=1, source_target_pairs={{0,6},{1,7},{2,4},{3,5},{4,2},{5,3},{6,0},{7,1},{8,14},{9,15},{10,... | collective-permute-start | bytes 49160 | tf_op jit(solution)/shard_map/ppermute | solution.py:404
  34.1 5.0 %collective-permute-start.7 = (f32[1,4,8,128]{3,2,1,0:T(8,128)S(1)}, f32[1,4,8,128]{3,2,1,0:T(8,128)S(1)}, u32[]{:S(2)}, u32[]{:S(2)}) collective-permute-start(f32[1,4,8,128]{3,2,1,0:T(8,128)S(1)} %get-tuple-element.40), channel_id=1, source_target_pairs={{0,96},{8,104},{16,112},{24,120},{32,64},{40,72},{48,80},{56,88},{... | collective-permute-start | bytes 49160 | tf_op jit(solution)/shard_map/ppermute | solution.py:404

commit v4 on v3

--- a/solution.py
+++ b/solution.py
@@ -39,7 +39,7 @@
 
 
 def load_kernel(stages, density_ref, table_ref, shear_x_ref, shear_y_ref, turn_ref, cells_ref,
-                face_xa_ref, share_ref, own_ref, lut_ref, index_ref, mask_ref, turned_ref,
+                face_xa_ref, face_xb_ref, hop_ref, own_ref, lut_ref, index_ref, mask_ref, turned_ref,
                 ahead_ref, levels_ref, shifts_x_ref, shifts_y_ref, turns_ref, sems):
     count_x, count_y, cells_z = density_ref.shape
     inner = cells_ref.at[pl.ds(1, count_x), pl.ds(ROWS, count_y), :]
@@ -88,18 +88,17 @@
     odd_x, odd_y = is_set("gx", 1), is_set("gy", 1)
     first, last = cells_ref[1, pl.ds(ROWS, count_y), :], cells_ref[count_x, pl.ds(ROWS, count_y), :]
     face_xa_ref[...] = jnp.where(odd_x, last, first)
-    share_ref[pl.ds(0, count_y), :] = jnp.where(odd_x, first, last)
+    face_xb_ref[...] = jnp.where(odd_x, first, last)
     first, last = (cells_ref[pl.ds(1, count_x), ROWS, :],
                    cells_ref[pl.ds(1, count_x), ROWS + count_y - 1, :])
-    outward = odd_x == odd_y
-    share_ref[pl.ds(count_y, count_x), :] = jnp.where(outward, first, last)
-    own_ref[...] = jnp.where(outward, last, first)
-
-
-def relay_kernel(own_ref, shared_ref, out_ref):
+    hop_ref[...] = jnp.where(odd_y, last, first)
+    own_ref[...] = jnp.where(odd_y, first, last)
+
+
+def relay_kernel(own_ref, hopped_ref, out_ref):
     rows = own_ref.shape[0]
     out_ref[pl.ds(0, rows), :] = own_ref[...]
-    out_ref[pl.ds(rows, rows), :] = shared_ref[pl.ds(shared_ref.shape[0] - rows, rows), :]
+    out_ref[pl.ds(rows, rows), :] = hopped_ref[...]
 
 
 def classify_kernel(step_len, parity, cells_ref, lut_ref, *refs):
@@ -150,7 +149,7 @@
     return [state[1] * fade, state[2] * fade, state[3] * fade, total]
 
 
-def x_kernel(group, face_xa_ref, shared_ref, crossed_ref, returned_ref, field_ref, index_ref,
+def x_kernel(group, face_xa_ref, face_xb_ref, crossed_ref, field_ref, index_ref,
              mask_ref, turned_ref, _, keep_ref, give_ref, emit_ref, cells_ref):
     count_x, cells_z = cells_ref.shape[0] - 2, cells_ref.shape[2]
     count_y = cells_ref.shape[1] - 2 * ROWS
@@ -159,12 +158,11 @@
     lane = lax.broadcasted_iota(jnp.int32, (ROWS, cells_z), 1)
 
     odd_x, odd_y = is_set("gx", 1), is_set("gy", 1)
-    near, far = face_xa_ref[...], shared_ref[pl.ds(0, count_y), :]
+    near, far = face_xa_ref[...], face_xb_ref[...]
     cells_ref[0, pl.ds(pad, count_y), :] = jnp.where(odd_x, far, near)
     cells_ref[count_x + 1, pl.ds(pad, count_y), :] = jnp.where(odd_x, near, far)
-    own, other = crossed_ref[pl.ds(0, count_x), :], returned_ref[pl.ds(count_x, count_x), :]
-    outward = odd_x == odd_y
-    low_y, high_y = jnp.where(outward, other, own), jnp.where(outward, own, other)
+    near, far = crossed_ref[pl.ds(0, count_x), :], crossed_ref[pl.ds(count_x, count_x), :]
+    low_y, high_y = jnp.where(odd_y, near, far), jnp.where(odd_y, far, near)
     for i in range(count_x):
         cells_ref[i + 1, pl.ds(pad - 1, 1), :] = low_y[i:i + 1]
         cells_ref[i + 1, pl.ds(pad + count_y, 1), :] = high_y[i:i + 1]
@@ -275,15 +273,15 @@
     return pl.pallas_call(
         functools.partial(load_kernel, STAGES),
         out_shape=(floats(count_x + 2, count_y + 2 * ROWS, cells_z),
-                   floats(count_y, cells_z), floats(count_y + count_x, cells_z),
-                   floats(count_x, cells_z),
+                   floats(count_y, cells_z), floats(count_y, cells_z),
+                   floats(count_x, cells_z), floats(count_x, cells_z),
                    floats(4, ROWS, cells_z),
                    jax.ShapeDtypeStruct((places, ROWS, cells_z), jnp.int32),
                    floats(places, ROWS, cells_z),
                    jax.ShapeDtypeStruct((4, ROWS, cells_z), jnp.int32),
                    floats(sum(len(masks) for _, masks in STAGES), ROWS, cells_z)),
         in_specs=[HBM] * 5,
-        out_specs=(VMEM,) * 9,
+        out_specs=(VMEM,) * 10,
         scratch_shapes=[pltpu.VMEM(transfer_table.shape, jnp.int32),
                         pltpu.SMEM(shear_x.shape, jnp.int32), pltpu.SMEM(shear_y.shape, jnp.int32),
                         pltpu.SMEM(direction.shape, jnp.int32), pltpu.SemaphoreType.DMA((5,))],
@@ -292,7 +290,7 @@
     )(*sources)
 
 
-def relay(own, shared):
+def relay(own, hopped):
     return pl.pallas_call(
         relay_kernel,
         out_shape=floats(2 * own.shape[0], own.shape[1]),
@@ -300,7 +298,7 @@
         out_specs=VMEM,
         name="relay",
         **options(0.3),
-    )(own, shared)
+    )(own, hopped)
 
 
 def classify(cells, lut, step_len, part, *before):
@@ -321,9 +319,9 @@
     return pl.pallas_call(
         functools.partial(x_kernel, GROUP_X),
         out_shape=(part, part, floats(3, *field.shape[1:]), floats(*cells.shape)),
-        in_specs=[VMEM] * 9,
+        in_specs=[VMEM] * 8,
         out_specs=(VMEM,) * 4,
-        input_output_aliases={8: 3},
+        input_output_aliases={7: 3},
         name="x_march",
         **options(8),
     )(*halo, field, *shifts, cells)[:3]
@@ -346,10 +344,10 @@
     return pairs + [(target, source) for source, target in pairs]
 
 
-def crossings():
-    count = lax.axis_size("gy")
-    return [(i * count + source, i * count + target) for i in range(lax.axis_size("gx"))
-            for source, target in neighbours("gy", i % 2)]
+def hops(axis):
+    count = lax.axis_size(axis)
+    moves = [(i, i + 4 * (i % 2) - 2) for i in range(count)]
+    return [(source, target) for source, target in moves if 0 <= target < count]
 
 
 def swapped(axis, mask):
@@ -421,15 +419,15 @@
 def local(density, transfer_table, shear_x, shear_y, direction):
     count_x = density.shape[0]
     step_len = 1.0 / (count_x * lax.axis_size("gx"))
-    cells, face, share, own, lut, *shifts, ahead = load(density, transfer_table, shear_x, shear_y,
-                                                        direction)
-    shared = lax.ppermute(share, "gx", swapped("gx", 1))
-    faced = lax.ppermute(face, "gx", neighbours("gx", 1))
-    crossed = lax.ppermute(relay(own, shared), ("gx", "gy"), crossings())
-    returned = lax.ppermute(crossed, "gx", swapped("gx", 1))
+    cells, outer, inner, hop, own, lut, *shifts, ahead = load(density, transfer_table, shear_x,
+                                                              shear_y, direction)
+    inner = lax.ppermute(inner, "gx", swapped("gx", 1))
+    hopped = lax.ppermute(hop, "gy", hops("gy"))
+    outer = lax.ppermute(outer, "gx", neighbours("gx", 1))
+    crossed = lax.ppermute(relay(own, hopped), "gy", swapped("gy", 1))
     field = classify(cells, lut, step_len, 0)
     field = classify(cells, lut, step_len, 1, field)
-    halo = (faced, shared, crossed, returned)
+    halo = (outer, inner, crossed)
     keep_x, give_x, emitted = x_march(cells, halo, field, shifts)
 
     x, y = Exchange("gx", 0, ahead), Exchange("gy", len(STAGES[0][1]), ahead)

time: 39.9 us -> 38.8 us (0.972)
  waiting for transfers between devices: 10 us -> 7.67 us
  starting transfers between devices: 17.3 us -> 18.7 us
    ppermute x4, waiting for transfers between devices: 2.16 us -> 0.31 us  [the longest x1 0.3 us: local(): hopped = lax.ppermute(hop, 'gy', hops('gy'))]
    ppermute x4, starting transfers between devices: 8.98 us -> 10.7 us  [the longest x1 5.39 us: local(): crossed = lax.ppermute(relay(own, hopped), 'gy', swapped('gy', 1))]
    ppermute x7, waiting for transfers between devices: 7.89 us -> 7.36 us  [send(): self.got = lax.ppermute(give, self.axis, swapped(self.axis, mask))]
    ppermute x7, starting transfers between devices: 8.36 us -> 7.95 us  [send(): self.got = lax.ppermute(give, self.axis, swapped(self.axis, mask))]
  transfers between devices with their start and end apart: 11 -> 11, of which waited for: 6 -> 5; matrix products, arithmetic and copies ran while one was open for 0% -> 0% of each run, Pallas kernels for 15% -> 15%
where the time goes in v4:
time: 38.8 us; the launch traced here: 38.7 us
  starting transfers between devices  18.7 us (48%)
  Pallas kernels  11.6 us (30%)
  waiting for transfers between devices  7.67 us (20%)
  between operations  0.75 us (2%)
    ppermute x7, starting transfers between devices, send(): self.got = lax.ppermute(give, self.axis, swapped(self.axis, mask))  7.95 us
    ppermute x7, waiting for transfers between devices, send(): self.got = lax.ppermute(give, self.axis, swapped(self.axis, mask))  7.36 us
    ppermute x1, starting transfers between devices, local(): crossed = lax.ppermute(relay(own, hopped), 'gy', swapped('gy', 1))  5.39 us
    pallas_call x1, Pallas kernels, x_march(): pl.pallas_call(functools.partial(x_kernel, GROUP_X), out_shape=(part, par...  3.55 us
    ppermute x1, starting transfers between devices, local(): outer = lax.ppermute(outer, 'gx', neighbours('gx', 1))  3.45 us
    pallas_call x2, Pallas kernels, y_march(): pl.pallas_call(functools.partial(y_kernel, GROUP_Y, kept, *sizes), out_sh...  3.2 us
    pallas_call x2, Pallas kernels, classify(): pl.pallas_call(functools.partial(classify_kernel, step_len, part), out_sh...  2.05 us
    pallas_call x1, Pallas kernels, load(): pl.pallas_call(functools.partial(load_kernel, STAGES), out_shape=(floats(...  1.45 us
  transfers between devices with their start and end apart: 11, of which 5 were waited for; matrix products, arithmetic and copies ran while one was open for 0% of the time, Pallas kernels for 15%

profile of v4, /device:TPU:24, one launch (start us, length us, event | category | flops | bytes accessed | tf_op | source)
XLA Modules:
  0.0 38.7 jit_solution(9435890217539586238)
XLA Ops:
  0.6 1.4 %load.1 = (f32[34,80,128]{2,1,0:T(8,128)S(1)}, f32[64,128]{1,0:T(8,128)S(1)}, f32[64,128]{1,0:T(8,128)S(1)}, f32[32,128]{1,0:T(8,128)S(1)}, f32[32,128]{1,0:T(8,...) custom-call(f32[32,64,128]{2,1,0:T(8,128)} %density_ref.1, ...), custom_call_target="tpu_custom_call" | custom-call | bytes 7000000 | tf_op jit(solution)/shard_map/load/pallas_call | solution.py:273
  2.1 1.3 %collective-permute-start.2 = (f32[32,128]{1,0:T(8,128)S(1)}, f32[32,128]{1,0:T(8,128)S(1)}, u32[]{:S(2)}, u32[]{:S(2)}) collective-permute-start(f32[32,128]{1,0:T(8,128)S(1)} %get-tuple-element.28), channel_id=1, source_target_pairs={{1,3},{2,0},{3,5},{4,2},{5,7},{6,4},{9,11},{10,8},{11,13},{12,10},... | collective-permute-start | bytes 49160 | tf_op jit(solution)/shard_map/ppermute | solution.py:425
  3.4 3.4 %collective-permute-start = (f32[64,128]{1,0:T(8,128)S(1)}, f32[64,128]{1,0:T(8,128)S(1)}, u32[]{:S(2)}, u32[]{:S(2)}) collective-permute-start(f32[64,128]{1,0:T(8,128)S(1)} %get-tuple-element.25), channel_id=1, source_target_pairs={{8,16},{24,32},{40,48},{56,64},{72,80},{88,96},{104,112},{16,8},{3... | collective-permute-start | bytes 98312 | tf_op jit(solution)/shard_map/ppermute | solution.py:426
  6.8 0.6 %collective-permute-start.1 = (f32[64,128]{1,0:T(8,128)S(1)}, f32[64,128]{1,0:T(8,128)S(1)}, u32[]{:S(2)}, u32[]{:S(2)}) collective-permute-start(f32[64,128]{1,0:T(8,128)S(1)} %get-tuple-element.26), channel_id=1, source_target_pairs={{0,8},{8,0},{16,24},{24,16},{32,40},{40,32},{48,56},{56,48},{64,72... | collective-permute-start | bytes 98312 | tf_op jit(solution)/shard_map/ppermute | solution.py:424
  7.4 0.3 collective-permute-done.2.hopped_ref
  7.7 5.4 %collective-permute-start.3 = (f32[64,128]{1,0:T(8,128)S(1)}, f32[64,128]{1,0:T(8,128)S(1)}, u32[]{:S(2)}, u32[]{:S(2)}) collective-permute-start(f32[64,128]{1,0:T(8,128)S(1)} %relay.1), channel_id=1, source_target_pairs={{0,1},{1,0},{2,3},{3,2},{4,5},{5,4},{6,7},{7,6},{8,9},{9,8},{10,11... | collective-permute-start | bytes 98312 | tf_op jit(solution)/shard_map/ppermute | solution.py:427
  13.1 1.0 %shard_map.68.refs_0_ = f32[4,2080,128]{2,1,0:T(8,128)S(1)} custom-call(f32[34,80,128]{2,1,0:T(8,128)S(1)} %get-tuple-element.29.cells_ref._, f32[4,8,128]{2,1,0:T(8,128)S(1)} %get-tuple-element.30.lut_ref), custom_call_target="tpu_custom_call" | custom-call | bytes 5250000 | tf_op jit(solution)/shard_map/pallas_call | solution.py:306
  14.1 1.0 %shard_map.69.field_ref = f32[4,2080,128]{2,1,0:T(8,128)S(1)} custom-call(f32[34,80,128]{2,1,0:T(8,128)S(1)} %get-tuple-element.29.cells_ref._, f32[4,8,128]{2,1,0:T(8,128)S(1)} %get-tuple-element.30.lut_ref, f32[4,2080,128]{2,1,0:T(8,128)S(1)} %shard_map.68.refs_0_), custom_call_target="tpu_custom_call", output_to_operand_aliasing={{}: (2, {})} | custom-call | bytes 5250000 | tf_op jit(solution)/shard_map/pallas_call | solution.py:306
  15.2 0.0 collective-permute-done.face_xa_ref
  15.2 0.0 collective-permute-done.1.face_xb_ref
  15.2 0.0 collective-permute-done.3.crossed_ref
  15.2 3.6 %x_march.1 = (f32[8,4,8,128]{3,2,1,0:T(8,128)S(1)}, f32[8,4,8,128]{3,2,1,0:T(8,128)S(1)}, f32[3,2080,128]{2,1,0:T(8,128)S(1)}, f32[34,80,128]{2,1,0:T(8,128)S(1)}) custom-call(f32[64,128]{1,0:T(8,128)S(1)} %collective-permute-done.face_xa_ref, f32[64,128]{1,0:T(8,128)S(1)} %collective-permute-done.1.face_xb_ref, ...), custom_call_target="tpu_custom_call", output_to_operand_aliasing={{3}: (7, {})} | custom-call | bytes 28000000 | tf_op jit(solution)/shard_map/x_march/pallas_call | solution.py:319
  18.8 0.1 collective-permute-start.4
  18.8 1.6 %shard_map.75 = f32[4,4,8,128]{3,2,1,0:T(8,128)S(1)} custom-call(f32[3,2080,128]{2,1,0:T(8,128)S(1)} %get-tuple-element.43.emit_ref, f32[4,2080,128]{2,1,0:T(8,128)S(1)} %shard_map.69.field_ref, s32[192,8,128]{2,1,0:T(8,128)S(1)} %get-tuple-element.31.index_ref, f32[192,8,128]{2,1,0:T(8,128)S(1)} %get-tuple-element.32.mask_ref, ...), custom_call_target="tpu_custom_call" | custom-call | bytes 8750000 | tf_op jit(solution)/shard_map/pallas_call | solution.py:332
  20.5 3.3 %collective-permute-start.8 = (f32[4,4,8,128]{3,2,1,0:T(8,128)S(1)}, f32[4,4,8,128]{3,2,1,0:T(8,128)S(1)}, u32[]{:S(2)}, u32[]{:S(2)}) collective-permute-start(f32[4,4,8,128]{3,2,1,0:T(8,128)S(1)} %shard_map.75), channel_id=1, source_target_pairs={{0,1},{1,0},{2,3},{3,2},{4,5},{5,4},{6,7},{7,6},{8,9},{9,8},{10,11... | collective-permute-start | bytes 196616 | tf_op jit(solution)/shard_map/ppermute | solution.py:402
  23.8 0.0 collective-permute-done.4.got_ref
  23.9 0.1 collective-permute-start.5
  24.0 1.6 %shard_map.74.keep_ref = f32[4,4,8,128]{3,2,1,0:T(8,128)S(1)} custom-call(f32[3,2080,128]{2,1,0:T(8,128)S(1)} %get-tuple-element.43.emit_ref, f32[4,2080,128]{2,1,0:T(8,128)S(1)} %shard_map.69.field_ref, s32[192,8,128]{2,1,0:T(8,128)S(1)} %get-tuple-element.31.index_ref, f32[192,8,128]{2,1,0:T(8,128)S(1)} %get-tuple-element.32.mask_ref, ...), custom_call_target="tpu_custom_call" | custom-call | bytes 8750000 | tf_op jit(solution)/shard_map/pallas_call | solution.py:332
  25.5 1.5 %collective-permute-done.8.got_ref = f32[4,4,8,128]{3,2,1,0:T(8,128)S(1)} collective-permute-done((f32[4,4,8,128]{3,2,1,0:T(8,128)S(1)}, f32[4,4,8,128]{3,2,1,0:T(8,128)S(1)}, u32[]{:S(2)}, u32[]{:S(2)}) %collective-permute-start.8) | collective-permute-done | bytes 65568 | tf_op jit(solution)/shard_map/ppermute | solution.py:402
  27.1 1.6 %collective-permute-start.9 = (f32[2,4,8,128]{3,2,1,0:T(8,128)S(1)}, f32[2,4,8,128]{3,2,1,0:T(8,128)S(1)}, u32[]{:S(2)}, u32[]{:S(2)}) collective-permute-start(f32[2,4,8,128]{3,2,1,0:T(8,128)S(1)} %get-tuple-element.45), channel_id=1, source_target_pairs={{0,2},{1,3},{2,0},{3,1},{4,6},{5,7},{6,4},{7,5},{8,10},{9,11},{10,... | collective-permute-start | bytes 98312 | tf_op jit(solution)/shard_map/ppermute | solution.py:402
  28.6 0.0 collective-permute-done.5.got_ref
  28.7 0.9 %collective-permute-start.6 = (f32[2,4,8,128]{3,2,1,0:T(8,128)S(1)}, f32[2,4,8,128]{3,2,1,0:T(8,128)S(1)}, u32[]{:S(2)}, u32[]{:S(2)}) collective-permute-start(f32[2,4,8,128]{3,2,1,0:T(8,128)S(1)} %get-tuple-element.40), channel_id=1, source_target_pairs={{0,32},{8,40},{16,48},{24,56},{32,0},{40,8},{48,16},{56,24},{64,96... | collective-permute-start | bytes 98312 | tf_op jit(solution)/shard_map/ppermute | solution.py:402
  29.5 1.5 %collective-permute-done.9.got_ref = f32[2,4,8,128]{3,2,1,0:T(8,128)S(1)} collective-permute-done((f32[2,4,8,128]{3,2,1,0:T(8,128)S(1)}, f32[2,4,8,128]{3,2,1,0:T(8,128)S(1)}, u32[]{:S(2)}, u32[]{:S(2)}) %collective-permute-start.9) | collective-permute-done | bytes 32800 | tf_op jit(solution)/shard_map/ppermute | solution.py:402
  31.1 1.9 %collective-permute-start.10 = (f32[1,4,8,128]{3,2,1,0:T(8,128)S(1)}, f32[1,4,8,128]{3,2,1,0:T(8,128)S(1)}, u32[]{:S(2)}, u32[]{:S(2)}) collective-permute-start(f32[1,4,8,128]{3,2,1,0:T(8,128)S(1)} %get-tuple-element.47), channel_id=1, source_target_pairs={{0,6},{1,7},{2,4},{3,5},{4,2},{5,3},{6,0},{7,1},{8,14},{9,15},{10,... | collective-permute-start | bytes 49160 | tf_op jit(solution)/shard_map/ppermute | solution.py:402
  33.0 0.0 collective-permute-done.6.got_ref
  33.0 0.1 collective-permute-start.7
  33.1 3.0 %collective-permute-done.10.got_ref = f32[1,4,8,128]{3,2,1,0:T(8,128)S(1)} collective-permute-done((f32[1,4,8,128]{3,2,1,0:T(8,128)S(1)}, f32[1,4,8,128]{3,2,1,0:T(8,128)S(1)}, u32[]{:S(2)}, u32[]{:S(2)}) %collective-permute-start.10) | collective-permute-done | bytes 16416 | tf_op jit(solution)/shard_map/ppermute | solution.py:402
  36.1 0.6 %shard_map.78 = f32[2,4,4,128]{3,2,1,0:T(4,128)} custom-call(f32[1,4,8,128]{3,2,1,0:T(8,128)S(1)} %get-tuple-element.46.keep_ref, f32[1,4,8,128]{3,2,1,0:T(8,128)S(1)} %collective-permute-done.10.got_ref, f32[7,8,128]{2,1,0:T(8,128)S(1)} %get-tuple-element.36.ahead_ref), custom_call_target="tpu_custom_call" | custom-call | bytes 1050000 | tf_op jit(solution)/shard_map/pallas_call | solution.py:410
  36.7 1.3 %collective-permute-done.7.got_ref = f32[1,4,8,128]{3,2,1,0:T(8,128)S(1)} collective-permute-done((f32[1,4,8,128]{3,2,1,0:T(8,128)S(1)}, f32[1,4,8,128]{3,2,1,0:T(8,128)S(1)}, u32[]{:S(2)}, u32[]{:S(2)}) %collective-permute-start.7) | collective-permute-done | bytes 16416 | tf_op jit(solution)/shard_map/ppermute | solution.py:402
  38.0 0.6 %shard_map.73 = f32[2,4,4,128]{3,2,1,0:T(4,128)} custom-call(f32[1,4,8,128]{3,2,1,0:T(8,128)S(1)} %get-tuple-element.41.keep_ref, f32[1,4,8,128]{3,2,1,0:T(8,128)S(1)} %collective-permute-done.7.got_ref, f32[7,8,128]{2,1,0:T(8,128)S(1)} %get-tuple-element.36.ahead_ref), custom_call_target="tpu_custom_call" | custom-call | bytes 1050000 | tf_op jit(solution)/shard_map/pallas_call | solution.py:410
  (6 shorter events, 0.1 us)
Async XLA Ops:
  2.1 5.6 %collective-permute-start.2 = (f32[32,128]{1,0:T(8,128)S(1)}, f32[32,128]{1,0:T(8,128)S(1)}, u32[]{:S(2)}, u32[]{:S(2)}) collective-permute-start(f32[32,128]{1,0:T(8,128)S(1)} %get-tuple-element.28), channel_id=1, source_target_pairs={{1,3},{2,0},{3,5},{4,2},{5,7},{6,4},{9,11},{10,8},{11,13},{12,10},... | collective-permute-start | bytes 49160 | tf_op jit(solution)/shard_map/ppermute | solution.py:425
  3.4 11.8 %collective-permute-start = (f32[64,128]{1,0:T(8,128)S(1)}, f32[64,128]{1,0:T(8,128)S(1)}, u32[]{:S(2)}, u32[]{:S(2)}) collective-permute-start(f32[64,128]{1,0:T(8,128)S(1)} %get-tuple-element.25), channel_id=1, source_target_pairs={{8,16},{24,32},{40,48},{56,64},{72,80},{88,96},{104,112},{16,8},{3... | collective-permute-start | bytes 98312 | tf_op jit(solution)/shard_map/ppermute | solution.py:426
  6.8 8.3 %collective-permute-start.1 = (f32[64,128]{1,0:T(8,128)S(1)}, f32[64,128]{1,0:T(8,128)S(1)}, u32[]{:S(2)}, u32[]{:S(2)}) collective-permute-start(f32[64,128]{1,0:T(8,128)S(1)} %get-tuple-element.26), channel_id=1, source_target_pairs={{0,8},{8,0},{16,24},{24,16},{32,40},{40,32},{48,56},{56,48},{64,72... | collective-permute-start | bytes 98312 | tf_op jit(solution)/shard_map/ppermute | solution.py:424
  7.7 7.5 %collective-permute-start.3 = (f32[64,128]{1,0:T(8,128)S(1)}, f32[64,128]{1,0:T(8,128)S(1)}, u32[]{:S(2)}, u32[]{:S(2)}) collective-permute-start(f32[64,128]{1,0:T(8,128)S(1)} %relay.1), channel_id=1, source_target_pairs={{0,1},{1,0},{2,3},{3,2},{4,5},{5,4},{6,7},{7,6},{8,9},{9,8},{10,11... | collective-permute-start | bytes 98312 | tf_op jit(solution)/shard_map/ppermute | solution.py:427
  18.8 5.1 %collective-permute-start.4 = (f32[8,4,8,128]{3,2,1,0:T(8,128)S(1)}, f32[8,4,8,128]{3,2,1,0:T(8,128)S(1)}, u32[]{:S(2)}, u32[]{:S(2)}) collective-permute-start(f32[8,4,8,128]{3,2,1,0:T(8,128)S(1)} %get-tuple-element.35), channel_id=1, source_target_pairs={{0,8},{8,0},{16,24},{24,16},{32,40},{40,32},{48,56},{56,48},{64,72... | collective-permute-start | bytes 393224 | tf_op jit(solution)/shard_map/ppermute | solution.py:402
  20.5 6.5 %collective-permute-start.8 = (f32[4,4,8,128]{3,2,1,0:T(8,128)S(1)}, f32[4,4,8,128]{3,2,1,0:T(8,128)S(1)}, u32[]{:S(2)}, u32[]{:S(2)}) collective-permute-start(f32[4,4,8,128]{3,2,1,0:T(8,128)S(1)} %shard_map.75), channel_id=1, source_target_pairs={{0,1},{1,0},{2,3},{3,2},{4,5},{5,4},{6,7},{7,6},{8,9},{9,8},{10,11... | collective-permute-start | bytes 196616 | tf_op jit(solution)/shard_map/ppermute | solution.py:402
  23.9 4.8 %collective-permute-start.5 = (f32[4,4,8,128]{3,2,1,0:T(8,128)S(1)}, f32[4,4,8,128]{3,2,1,0:T(8,128)S(1)}, u32[]{:S(2)}, u32[]{:S(2)}) collective-permute-start(f32[4,4,8,128]{3,2,1,0:T(8,128)S(1)} %get-tuple-element.38), channel_id=1, source_target_pairs={{0,16},{8,24},{16,0},{24,8},{32,48},{40,56},{48,32},{56,40},{64,80... | collective-permute-start | bytes 196616 | tf_op jit(solution)/shard_map/ppermute | solution.py:402
  27.1 4.0 %collective-permute-start.9 = (f32[2,4,8,128]{3,2,1,0:T(8,128)S(1)}, f32[2,4,8,128]{3,2,1,0:T(8,128)S(1)}, u32[]{:S(2)}, u32[]{:S(2)}) collective-permute-start(f32[2,4,8,128]{3,2,1,0:T(8,128)S(1)} %get-tuple-element.45), channel_id=1, source_target_pairs={{0,2},{1,3},{2,0},{3,1},{4,6},{5,7},{6,4},{7,5},{8,10},{9,11},{10,... | collective-permute-start | bytes 98312 | tf_op jit(solution)/shard_map/ppermute | solution.py:402
  28.7 4.3 %collective-permute-start.6 = (f32[2,4,8,128]{3,2,1,0:T(8,128)S(1)}, f32[2,4,8,128]{3,2,1,0:T(8,128)S(1)}, u32[]{:S(2)}, u32[]{:S(2)}) collective-permute-start(f32[2,4,8,128]{3,2,1,0:T(8,128)S(1)} %get-tuple-element.40), channel_id=1, source_target_pairs={{0,32},{8,40},{16,48},{24,56},{32,0},{40,8},{48,16},{56,24},{64,96... | collective-permute-start | bytes 98312 | tf_op jit(solution)/shard_map/ppermute | solution.py:402
  31.1 5.0 %collective-permute-start.10 = (f32[1,4,8,128]{3,2,1,0:T(8,128)S(1)}, f32[1,4,8,128]{3,2,1,0:T(8,128)S(1)}, u32[]{:S(2)}, u32[]{:S(2)}) collective-permute-start(f32[1,4,8,128]{3,2,1,0:T(8,128)S(1)} %get-tuple-element.47), channel_id=1, source_target_pairs={{0,6},{1,7},{2,4},{3,5},{4,2},{5,3},{6,0},{7,1},{8,14},{9,15},{10,... | collective-permute-start | bytes 49160 | tf_op jit(solution)/shard_map/ppermute | solution.py:402
  33.0 5.0 %collective-permute-start.7 = (f32[1,4,8,128]{3,2,1,0:T(8,128)S(1)}, f32[1,4,8,128]{3,2,1,0:T(8,128)S(1)}, u32[]{:S(2)}, u32[]{:S(2)}) collective-permute-start(f32[1,4,8,128]{3,2,1,0:T(8,128)S(1)} %get-tuple-element.42), channel_id=1, source_target_pairs={{0,96},{8,104},{16,112},{24,120},{32,64},{40,72},{48,80},{56,88},{... | collective-permute-start | bytes 49160 | tf_op jit(solution)/shard_map/ppermute | solution.py:402

commit v5 on v4

--- a/solution.py
+++ b/solution.py
@@ -14,7 +14,7 @@
 PACK = 1024.0
 ROUNDER = 12582912.0
 GROUP_X, GROUP_Y = 4, 2
-UNROLL_C, UNROLL_E, UNROLL_X, UNROLL_Y = 16, 32, 32, 64
+UNROLL_C, UNROLL_E, UNROLL_F, UNROLL_X, UNROLL_Y = 16, 32, 30, 32, 64
 
 VMEM = pl.BlockSpec(memory_space=pltpu.VMEM)
 HBM = pl.BlockSpec(memory_space=pltpu.HBM)
@@ -149,8 +149,40 @@
     return [state[1] * fade, state[2] * fade, state[3] * fade, total]
 
 
+def emission(cells_ref, field_ref, emit_ref, i, base):
+    count_x, cells_z = cells_ref.shape[0] - 2, cells_ref.shape[2]
+    pitch, pad = field_ref.shape[1] // count_x, ROWS
+    lane = lax.broadcasted_iota(jnp.int32, (ROWS, cells_z), 1)
+    here = cells_ref[i + 1, pl.ds(base + pad, ROWS), :]
+    diff_x = (cells_ref[i + 2, pl.ds(base + pad, ROWS), :]
+              - cells_ref[i, pl.ds(base + pad, ROWS), :])
+    diff_y = (cells_ref[i + 1, pl.ds(base + pad + 1, ROWS), :]
+              - cells_ref[i + 1, pl.ds(base + pad - 1, ROWS), :])
+    above = lane_take(here, (lane + 1) & (cells_z - 1))
+    below = lane_take(here, (lane - 1) & (cells_z - 1))
+    diff_z = jnp.where(lane == cells_z - 1, 0.0, above) - jnp.where(lane == 0, 0.0, below)
+    side = diff_y + diff_z
+    facing = jnp.abs(diff_x + (side + side))
+    norm = diff_x * diff_x + diff_y * diff_y + diff_z * diff_z + 0.04
+    shaded = 0.3 + (0.7 / 3.0) * facing * lax.rsqrt(norm)
+    rows = pl.ds(slot_of(i, count_x) * pitch + base, ROWS)
+    for c in range(3):
+        emit_ref[c, rows, :] = field_ref[c, rows, :] * shaded
+
+
+def shade_kernel(cells_ref, field_ref, emit_ref):
+    count_x, count_y = cells_ref.shape[0] - 2, cells_ref.shape[1] - 2 * ROWS
+
+    def body(i, carry):
+        for base in range(0, count_y, ROWS):
+            emission(cells_ref, field_ref, emit_ref, i, base)
+        return carry
+
+    lax.fori_loop(0, count_x, body, 0, unroll=UNROLL_E)
+
+
 def x_kernel(group, face_xa_ref, face_xb_ref, crossed_ref, field_ref, index_ref,
-             mask_ref, turned_ref, _, keep_ref, give_ref, emit_ref, cells_ref):
+             mask_ref, turned_ref, _cells, _emit, keep_ref, give_ref, emit_ref, cells_ref):
     count_x, cells_z = cells_ref.shape[0] - 2, cells_ref.shape[2]
     count_y = cells_ref.shape[1] - 2 * ROWS
     pitch = field_ref.shape[1] // count_x
@@ -169,32 +201,16 @@
 
     turned = [turned_ref[v] != 0 for v in range(2)]
     zeros = jnp.zeros((ROWS, cells_z), jnp.float32)
-    up, down = (lane + 1) & (cells_z - 1), (lane - 1) & (cells_z - 1)
-
-    def shade(i, base):
-        here = cells_ref[i + 1, pl.ds(base + pad, ROWS), :]
-        diff_x = (cells_ref[i + 2, pl.ds(base + pad, ROWS), :]
-                  - cells_ref[i, pl.ds(base + pad, ROWS), :])
-        diff_y = (cells_ref[i + 1, pl.ds(base + pad + 1, ROWS), :]
-                  - cells_ref[i + 1, pl.ds(base + pad - 1, ROWS), :])
-        above = jnp.where(lane == cells_z - 1, 0.0, lane_take(here, up))
-        below = jnp.where(lane == 0, 0.0, lane_take(here, down))
-        diff_z = above - below
-        side = diff_y + diff_z
-        facing = jnp.abs(diff_x + (side + side))
-        norm = diff_x * diff_x + diff_y * diff_y + diff_z * diff_z + 0.04
-        return 0.3 + (0.7 / 3.0) * facing * lax.rsqrt(norm)
-
-    def emission(i, carry):
-        slot = slot_of(i, count_x) * pitch
+    for i in (0, count_x - 1):
         for base in range(0, count_y, ROWS):
-            shaded = shade(i, base)
-            rows = pl.ds(slot + base, ROWS)
-            for c in range(3):
-                emit_ref[c, rows, :] = field_ref[c, rows, :] * shaded
+            emission(cells_ref, field_ref, emit_ref, i, base)
+
+    def edges(i, carry):
+        for base in (0, count_y - ROWS):
+            emission(cells_ref, field_ref, emit_ref, i, base)
         return carry
 
-    lax.fori_loop(0, count_x, emission, 0, unroll=UNROLL_E)
+    lax.fori_loop(1, count_x - 1, edges, 0, unroll=UNROLL_F)
 
     def block_of(block, carry):
         base = pl.multiple_of(block * (ROWS * group), ROWS)
@@ -313,18 +329,29 @@
     )(cells, lut, *before)
 
 
-def x_march(cells, halo, field, shifts):
+def shade(cells, field):
+    return pl.pallas_call(
+        shade_kernel,
+        out_shape=floats(3, *field.shape[1:]),
+        in_specs=[VMEM, VMEM],
+        out_specs=VMEM,
+        name="shade",
+        **options(2),
+    )(cells, field)
+
+
+def x_march(cells, halo, field, shifts, emitted):
     count_y, cells_z = cells.shape[1] - 2 * ROWS, cells.shape[2]
     part = floats(count_y // (2 * PIECE), 4, 2 * PIECE, cells_z)
     return pl.pallas_call(
         functools.partial(x_kernel, GROUP_X),
-        out_shape=(part, part, floats(3, *field.shape[1:]), floats(*cells.shape)),
-        in_specs=[VMEM] * 8,
+        out_shape=(part, part, floats(*emitted.shape), floats(*cells.shape)),
+        in_specs=[VMEM] * 9,
         out_specs=(VMEM,) * 4,
-        input_output_aliases={7: 3},
+        input_output_aliases={7: 3, 8: 2},
         name="x_march",
-        **options(8),
-    )(*halo, field, *shifts, cells)[:3]
+        **options(4),
+    )(*halo, field, *shifts, cells, emitted)[:3]
 
 
 def y_march(emitted, field, shifts, sizes, kept):
@@ -354,22 +381,37 @@
     return [(i, i ^ mask) for i in range(lax.axis_size(axis))]
 
 
-def stage_kernel(axis, mask, order, split, keep_ref, got_ref, ahead_ref, *out_refs):
-    mine_ahead = ahead_ref[order] > 0.5
-
-    def joined(p):
-        mine, theirs = [[ref[p, c] for c in range(4)] for ref in (keep_ref, got_ref)]
-        seen = jnp.exp2(-jnp.where(mine_ahead, mine[3], theirs[3]))
-        near, far = jnp.where(mine_ahead, 1.0, seen), jnp.where(mine_ahead, seen, 1.0)
-        return [mine[c] * near + theirs[c] * far for c in range(3)] + [mine[3] + theirs[3]]
-
-    parts = [joined(p) for p in range(keep_ref.shape[0])]
-    if split == "image":
-        red, green, blue, total = parts[0]
+def joined(keep_ref, got_ref, ahead, p):
+    mine_ahead = ahead > 0.5
+    mine, theirs = [[ref[p, c] for c in range(4)] for ref in (keep_ref, got_ref)]
+    seen = jnp.exp2(-jnp.where(mine_ahead, mine[3], theirs[3]))
+    near, far = jnp.where(mine_ahead, 1.0, seen), jnp.where(mine_ahead, seen, 1.0)
+    return [mine[c] * near + theirs[c] * far for c in range(3)] + [mine[3] + theirs[3]]
+
+
+def image_kernel(orders, keep_x_ref, got_x_ref, keep_y_ref, got_y_ref, ahead_ref, *out_refs):
+    refs = ((keep_x_ref, got_x_ref), (keep_y_ref, got_y_ref))
+    for order, (keep_ref, got_ref), out_ref in zip(orders, refs, out_refs):
+        red, green, blue, total = joined(keep_ref, got_ref, ahead_ref[order], 0)
         for c, value in enumerate((red, green, blue, 1.0 - jnp.exp2(-total))):
             for v in range(2):
-                out_refs[0][v, c] = value[PIECE * v:PIECE * (v + 1)]
-        return
+                out_ref[v, c] = value[PIECE * v:PIECE * (v + 1)]
+
+
+def images(x, y):
+    shape = floats(2, 4, PIECE, x.keep.shape[-1])
+    return pl.pallas_call(
+        functools.partial(image_kernel, (x.order(), y.order())),
+        out_shape=(shape, shape),
+        in_specs=[VMEM] * 5,
+        out_specs=(VMEM, VMEM),
+        name="images",
+        **options(0.3),
+    )(x.keep, x.got, y.keep, y.got, x.ahead)
+
+
+def stage_kernel(axis, mask, order, split, keep_ref, got_ref, ahead_ref, *out_refs):
+    parts = [joined(keep_ref, got_ref, ahead_ref[order], p) for p in range(keep_ref.shape[0])]
     pick = lambda flag, a, b: [jnp.where(flag, one, two) for one, two in zip(a, b)]
     if split == "pair":
         high = is_set(axis, mask)
@@ -401,17 +443,16 @@
         self.keep, self.stage = keep, self.stage + 1
         self.got = lax.ppermute(give, self.axis, swapped(self.axis, mask))
 
+    def order(self):
+        return self.first + self.stage - 1
+
     def meet(self, split, mask=0):
         count, *rest = self.keep.shape
-        if split == "image":
-            shape = floats(2, 4, PIECE, rest[-1])
-        else:
-            shape = (floats(count // 2, *rest),) * 2
         return pl.pallas_call(
-            functools.partial(stage_kernel, self.axis, mask, self.first + self.stage - 1, split),
-            out_shape=shape,
+            functools.partial(stage_kernel, self.axis, mask, self.order(), split),
+            out_shape=(floats(count // 2, *rest),) * 2,
             in_specs=[VMEM] * 3,
-            out_specs=VMEM if split == "image" else (VMEM, VMEM),
+            out_specs=(VMEM, VMEM),
             **options(0.3),
         )(self.keep, self.got, self.ahead)
 
@@ -427,8 +468,9 @@
     crossed = lax.ppermute(relay(own, hopped), "gy", swapped("gy", 1))
     field = classify(cells, lut, step_len, 0)
     field = classify(cells, lut, step_len, 1, field)
+    emitted = shade(cells, field)
     halo = (outer, inner, crossed)
-    keep_x, give_x, emitted = x_march(cells, halo, field, shifts)
+    keep_x, give_x, emitted = x_march(cells, halo, field, shifts, emitted)
 
     x, y = Exchange("gx", 0, ahead), Exchange("gy", len(STAGES[0][1]), ahead)
     x.send(keep_x, give_x, 1)
@@ -439,9 +481,8 @@
     x.send(*x.meet("ring_first", 4), 4)
     x.send(*x.meet("ring_second"), 12)
     y.send(*y.meet("ring_first", 2), 2)
-    image_x = x.meet("image")
     y.send(*y.meet("ring_second"), 6)
-    return image_x, y.meet("image")
+    return images(x, y)
 
 
 def solution(mesh):

time: 38.8 us -> 38.9 us (level)
  waiting for transfers between devices: 7.67 us -> 9.5 us
  starting transfers between devices: 18.7 us -> 17.1 us
    ppermute x7, waiting for transfers between devices: 7.36 us -> 9.19 us  [send(): self.got = lax.ppermute(give, self.axis, swapped(self.axis, mask))]
    ppermute x7, starting transfers between devices: 7.95 us -> 6.4 us  [send(): self.got = lax.ppermute(give, self.axis, swapped(self.axis, mask))]
    pallas_call x1, Pallas kernels: 3.55 us -> 3.03 us  [x_march(): pl.pallas_call(functools.partial(x_kernel, GROUP_X), out_shape=(part, par...]
  transfers between devices with their start and end apart: 11 -> 11, of which waited for: 5 -> 6; matrix products, arithmetic and copies ran while one was open for 0% -> 0% of each run, Pallas kernels for 15% -> 16%
where the time goes in v5:
time: 38.9 us; the launch traced here: 38.7 us
  starting transfers between devices  17.1 us (44%)
  Pallas kernels  11.4 us (29%)
  waiting for transfers between devices  9.5 us (24%)
  between operations  0.75 us (2%)
    ppermute x7, waiting for transfers between devices, send(): self.got = lax.ppermute(give, self.axis, swapped(self.axis, mask))  9.19 us
    ppermute x7, starting transfers between devices, send(): self.got = lax.ppermute(give, self.axis, swapped(self.axis, mask))  6.4 us
    ppermute x1, starting transfers between devices, local(): crossed = lax.ppermute(relay(own, hopped), 'gy', swapped('gy', 1))  5.39 us
    ppermute x1, starting transfers between devices, local(): outer = lax.ppermute(outer, 'gx', neighbours('gx', 1))  3.45 us
    pallas_call x2, Pallas kernels, y_march(): pl.pallas_call(functools.partial(y_kernel, GROUP_Y, kept, *sizes), out_sh...  3.2 us
    pallas_call x1, Pallas kernels, x_march(): pl.pallas_call(functools.partial(x_kernel, GROUP_X), out_shape=(part, par...  3.03 us
    pallas_call x2, Pallas kernels, classify(): pl.pallas_call(functools.partial(classify_kernel, step_len, part), out_sh...  2.06 us
    pallas_call x1, Pallas kernels, load(): pl.pallas_call(functools.partial(load_kernel, STAGES), out_shape=(floats(...  1.45 us
  transfers between devices with their start and end apart: 11, of which 6 were waited for; matrix products, arithmetic and copies ran while one was open for 0% of the time, Pallas kernels for 16%

profile of v5, /device:TPU:24, one launch (start us, length us, event | category | flops | bytes accessed | tf_op | source)
XLA Modules:
  0.0 38.7 jit_solution(499880592291103850)
XLA Ops:
  0.6 1.4 %load.1 = (f32[34,80,128]{2,1,0:T(8,128)S(1)}, f32[64,128]{1,0:T(8,128)S(1)}, f32[64,128]{1,0:T(8,128)S(1)}, f32[32,128]{1,0:T(8,128)S(1)}, f32[32,128]{1,0:T(8,...) custom-call(f32[32,64,128]{2,1,0:T(8,128)} %density_ref.1, ...), custom_call_target="tpu_custom_call" | custom-call | bytes 7000000 | tf_op jit(solution)/shard_map/load/pallas_call | solution.py:289
  2.1 1.3 %collective-permute-start.2 = (f32[32,128]{1,0:T(8,128)S(1)}, f32[32,128]{1,0:T(8,128)S(1)}, u32[]{:S(2)}, u32[]{:S(2)}) collective-permute-start(f32[32,128]{1,0:T(8,128)S(1)} %get-tuple-element.28), channel_id=1, source_target_pairs={{1,3},{2,0},{3,5},{4,2},{5,7},{6,4},{9,11},{10,8},{11,13},{12,10},... | collective-permute-start | bytes 49160 | tf_op jit(solution)/shard_map/ppermute | solution.py:466
  3.4 3.4 %collective-permute-start = (f32[64,128]{1,0:T(8,128)S(1)}, f32[64,128]{1,0:T(8,128)S(1)}, u32[]{:S(2)}, u32[]{:S(2)}) collective-permute-start(f32[64,128]{1,0:T(8,128)S(1)} %get-tuple-element.25), channel_id=1, source_target_pairs={{8,16},{24,32},{40,48},{56,64},{72,80},{88,96},{104,112},{16,8},{3... | collective-permute-start | bytes 98312 | tf_op jit(solution)/shard_map/ppermute | solution.py:467
  6.8 0.6 %collective-permute-start.1 = (f32[64,128]{1,0:T(8,128)S(1)}, f32[64,128]{1,0:T(8,128)S(1)}, u32[]{:S(2)}, u32[]{:S(2)}) collective-permute-start(f32[64,128]{1,0:T(8,128)S(1)} %get-tuple-element.26), channel_id=1, source_target_pairs={{0,8},{8,0},{16,24},{24,16},{32,40},{40,32},{48,56},{56,48},{64,72... | collective-permute-start | bytes 98312 | tf_op jit(solution)/shard_map/ppermute | solution.py:465
  7.4 0.3 collective-permute-done.2.hopped_ref
  7.7 5.4 %collective-permute-start.3 = (f32[64,128]{1,0:T(8,128)S(1)}, f32[64,128]{1,0:T(8,128)S(1)}, u32[]{:S(2)}, u32[]{:S(2)}) collective-permute-start(f32[64,128]{1,0:T(8,128)S(1)} %relay.1), channel_id=1, source_target_pairs={{0,1},{1,0},{2,3},{3,2},{4,5},{5,4},{6,7},{7,6},{8,9},{9,8},{10,11... | collective-permute-start | bytes 98312 | tf_op jit(solution)/shard_map/ppermute | solution.py:468
  13.1 1.0 %shard_map.68.refs_0_ = f32[4,2080,128]{2,1,0:T(8,128)S(1)} custom-call(f32[34,80,128]{2,1,0:T(8,128)S(1)} %get-tuple-element.29.cells_ref._cells, f32[4,8,128]{2,1,0:T(8,128)S(1)} %get-tuple-element.30.lut_ref), custom_call_target="tpu_custom_call" | custom-call | bytes 5250000 | tf_op jit(solution)/shard_map/pallas_call | solution.py:322
  14.1 1.0 %shard_map.69.field_ref = f32[4,2080,128]{2,1,0:T(8,128)S(1)} custom-call(f32[34,80,128]{2,1,0:T(8,128)S(1)} %get-tuple-element.29.cells_ref._cells, f32[4,8,128]{2,1,0:T(8,128)S(1)} %get-tuple-element.30.lut_ref, f32[4,2080,128]{2,1,0:T(8,128)S(1)} %shard_map.68.refs_0_), custom_call_target="tpu_custom_call", output_to_operand_aliasing={{}: (2, {})} | custom-call | bytes 5250000 | tf_op jit(solution)/shard_map/pallas_call | solution.py:322
  15.2 0.9 %shade.1._emit = f32[3,2080,128]{2,1,0:T(8,128)S(1)} custom-call(f32[34,80,128]{2,1,0:T(8,128)S(1)} %get-tuple-element.29.cells_ref._cells, f32[4,2080,128]{2,1,0:T(8,128)S(1)} %shard_map.69.field_ref), custom_call_target="tpu_custom_call" | custom-call | bytes 7000000 | tf_op jit(solution)/shard_map/shade/pallas_call | solution.py:333
  16.1 0.0 collective-permute-done.face_xa_ref
  16.1 0.0 collective-permute-done.1.face_xb_ref
  16.1 0.0 collective-permute-done.3.crossed_ref
  16.1 3.0 %x_march.1 = (f32[8,4,8,128]{3,2,1,0:T(8,128)S(1)}, f32[8,4,8,128]{3,2,1,0:T(8,128)S(1)}, f32[3,2080,128]{2,1,0:T(8,128)S(1)}, f32[34,80,128]{2,1,0:T(8,128)S(1)}) custom-call(f32[64,128]{1,0:T(8,128)S(1)} %collective-permute-done.face_xa_ref, f32[64,128]{1,0:T(8,128)S(1)} %collective-permute-done.1.face_xb_ref, ...), custom_call_target="tpu_custom_call", output_to_operand_aliasing={{3}: (7, {}), {2}: (8, {})} | custom-call | bytes 14000000 | tf_op jit(solution)/shard_map/x_march/pallas_call | solution.py:346
  19.1 0.1 collective-permute-start.4
  19.2 1.6 %shard_map.74 = f32[4,4,8,128]{3,2,1,0:T(8,128)S(1)} custom-call(f32[3,2080,128]{2,1,0:T(8,128)S(1)} %get-tuple-element.43.emit_ref, f32[4,2080,128]{2,1,0:T(8,128)S(1)} %shard_map.69.field_ref, s32[192,8,128]{2,1,0:T(8,128)S(1)} %get-tuple-element.31.index_ref, f32[192,8,128]{2,1,0:T(8,128)S(1)} %get-tuple-element.32.mask_ref, ...), custom_call_target="tpu_custom_call" | custom-call | bytes 8750000 | tf_op jit(solution)/shard_map/pallas_call | solution.py:359
  20.9 2.4 %collective-permute-start.8 = (f32[4,4,8,128]{3,2,1,0:T(8,128)S(1)}, f32[4,4,8,128]{3,2,1,0:T(8,128)S(1)}, u32[]{:S(2)}, u32[]{:S(2)}) collective-permute-start(f32[4,4,8,128]{3,2,1,0:T(8,128)S(1)} %shard_map.74), channel_id=1, source_target_pairs={{0,1},{1,0},{2,3},{3,2},{4,5},{5,4},{6,7},{7,6},{8,9},{9,8},{10,11... | collective-permute-start | bytes 196616 | tf_op jit(solution)/shard_map/ppermute | solution.py:444
  23.3 0.0 collective-permute-done.4.got_ref
  23.3 0.1 collective-permute-start.5
  23.4 1.6 %shard_map.73.keep_ref = f32[4,4,8,128]{3,2,1,0:T(8,128)S(1)} custom-call(f32[3,2080,128]{2,1,0:T(8,128)S(1)} %get-tuple-element.43.emit_ref, f32[4,2080,128]{2,1,0:T(8,128)S(1)} %shard_map.69.field_ref, s32[192,8,128]{2,1,0:T(8,128)S(1)} %get-tuple-element.31.index_ref, f32[192,8,128]{2,1,0:T(8,128)S(1)} %get-tuple-element.32.mask_ref, ...), custom_call_target="tpu_custom_call" | custom-call | bytes 8750000 | tf_op jit(solution)/shard_map/pallas_call | solution.py:359
  25.0 2.4 %collective-permute-done.8.got_ref = f32[4,4,8,128]{3,2,1,0:T(8,128)S(1)} collective-permute-done((f32[4,4,8,128]{3,2,1,0:T(8,128)S(1)}, f32[4,4,8,128]{3,2,1,0:T(8,128)S(1)}, u32[]{:S(2)}, u32[]{:S(2)}) %collective-permute-start.8) | collective-permute-done | bytes 65568 | tf_op jit(solution)/shard_map/ppermute | solution.py:444
  27.5 1.6 %collective-permute-start.9 = (f32[2,4,8,128]{3,2,1,0:T(8,128)S(1)}, f32[2,4,8,128]{3,2,1,0:T(8,128)S(1)}, u32[]{:S(2)}, u32[]{:S(2)}) collective-permute-start(f32[2,4,8,128]{3,2,1,0:T(8,128)S(1)} %get-tuple-element.45), channel_id=1, source_target_pairs={{0,2},{1,3},{2,0},{3,1},{4,6},{5,7},{6,4},{7,5},{8,10},{9,11},{10,... | collective-permute-start | bytes 98312 | tf_op jit(solution)/shard_map/ppermute | solution.py:444
  29.0 0.0 collective-permute-done.5.got_ref
  29.1 0.8 %collective-permute-start.6 = (f32[2,4,8,128]{3,2,1,0:T(8,128)S(1)}, f32[2,4,8,128]{3,2,1,0:T(8,128)S(1)}, u32[]{:S(2)}, u32[]{:S(2)}) collective-permute-start(f32[2,4,8,128]{3,2,1,0:T(8,128)S(1)} %get-tuple-element.40), channel_id=1, source_target_pairs={{0,32},{8,40},{16,48},{24,56},{32,0},{40,8},{48,16},{56,24},{64,96... | collective-permute-start | bytes 98312 | tf_op jit(solution)/shard_map/ppermute | solution.py:444
  29.8 1.6 %collective-permute-done.9.got_ref = f32[2,4,8,128]{3,2,1,0:T(8,128)S(1)} collective-permute-done((f32[2,4,8,128]{3,2,1,0:T(8,128)S(1)}, f32[2,4,8,128]{3,2,1,0:T(8,128)S(1)}, u32[]{:S(2)}, u32[]{:S(2)}) %collective-permute-start.9) | collective-permute-done | bytes 32800 | tf_op jit(solution)/shard_map/ppermute | solution.py:444
  31.5 1.4 %collective-permute-start.10 = (f32[1,4,8,128]{3,2,1,0:T(8,128)S(1)}, f32[1,4,8,128]{3,2,1,0:T(8,128)S(1)}, u32[]{:S(2)}, u32[]{:S(2)}) collective-permute-start(f32[1,4,8,128]{3,2,1,0:T(8,128)S(1)} %get-tuple-element.47), channel_id=1, source_target_pairs={{0,6},{1,7},{2,4},{3,5},{4,2},{5,3},{6,0},{7,1},{8,14},{9,15},{10,... | collective-permute-start | bytes 49160 | tf_op jit(solution)/shard_map/ppermute | solution.py:444
  32.8 0.2 collective-permute-done.6.got_ref
  33.1 0.1 collective-permute-start.7
  33.2 3.3 %collective-permute-done.10.got_y_ref = f32[1,4,8,128]{3,2,1,0:T(8,128)S(1)} collective-permute-done((f32[1,4,8,128]{3,2,1,0:T(8,128)S(1)}, f32[1,4,8,128]{3,2,1,0:T(8,128)S(1)}, u32[]{:S(2)}, u32[]{:S(2)}) %collective-permute-start.10) | collective-permute-done | bytes 16416 | tf_op jit(solution)/shard_map/ppermute | solution.py:444
  36.5 1.6 %collective-permute-done.7.got_x_ref = f32[1,4,8,128]{3,2,1,0:T(8,128)S(1)} collective-permute-done((f32[1,4,8,128]{3,2,1,0:T(8,128)S(1)}, f32[1,4,8,128]{3,2,1,0:T(8,128)S(1)}, u32[]{:S(2)}, u32[]{:S(2)}) %collective-permute-start.7) | collective-permute-done | bytes 16416 | tf_op jit(solution)/shard_map/ppermute | solution.py:444
  38.1 0.6 %images.1 = (f32[2,4,4,128]{3,2,1,0:T(4,128)}, f32[2,4,4,128]{3,2,1,0:T(4,128)}) custom-call(f32[1,4,8,128]{3,2,1,0:T(8,128)S(1)} %get-tuple-element.41.keep_x_ref, f32[1,4,8,128]{3,2,1,0:T(8,128)S(1)} %collective-permute-done.7.got_x_ref, f32[1,4,8,128]{3,2,1,0:T(8,128)S(1)} %get-tuple-element.46.keep_y_ref, ...), custom_call_target="tpu_custom_call" | custom-call | bytes 1050000 | tf_op jit(solution)/shard_map/images/pallas_call | solution.py:403
  (6 shorter events, 0.1 us)
Async XLA Ops:
  2.1 5.6 %collective-permute-start.2 = (f32[32,128]{1,0:T(8,128)S(1)}, f32[32,128]{1,0:T(8,128)S(1)}, u32[]{:S(2)}, u32[]{:S(2)}) collective-permute-start(f32[32,128]{1,0:T(8,128)S(1)} %get-tuple-element.28), channel_id=1, source_target_pairs={{1,3},{2,0},{3,5},{4,2},{5,7},{6,4},{9,11},{10,8},{11,13},{12,10},... | collective-permute-start | bytes 49160 | tf_op jit(solution)/shard_map/ppermute | solution.py:466
  3.4 12.7 %collective-permute-start = (f32[64,128]{1,0:T(8,128)S(1)}, f32[64,128]{1,0:T(8,128)S(1)}, u32[]{:S(2)}, u32[]{:S(2)}) collective-permute-start(f32[64,128]{1,0:T(8,128)S(1)} %get-tuple-element.25), channel_id=1, source_target_pairs={{8,16},{24,32},{40,48},{56,64},{72,80},{88,96},{104,112},{16,8},{3... | collective-permute-start | bytes 98312 | tf_op jit(solution)/shard_map/ppermute | solution.py:467
  6.8 9.2 %collective-permute-start.1 = (f32[64,128]{1,0:T(8,128)S(1)}, f32[64,128]{1,0:T(8,128)S(1)}, u32[]{:S(2)}, u32[]{:S(2)}) collective-permute-start(f32[64,128]{1,0:T(8,128)S(1)} %get-tuple-element.26), channel_id=1, source_target_pairs={{0,8},{8,0},{16,24},{24,16},{32,40},{40,32},{48,56},{56,48},{64,72... | collective-permute-start | bytes 98312 | tf_op jit(solution)/shard_map/ppermute | solution.py:465
  7.7 8.4 %collective-permute-start.3 = (f32[64,128]{1,0:T(8,128)S(1)}, f32[64,128]{1,0:T(8,128)S(1)}, u32[]{:S(2)}, u32[]{:S(2)}) collective-permute-start(f32[64,128]{1,0:T(8,128)S(1)} %relay.1), channel_id=1, source_target_pairs={{0,1},{1,0},{2,3},{3,2},{4,5},{5,4},{6,7},{7,6},{8,9},{9,8},{10,11... | collective-permute-start | bytes 98312 | tf_op jit(solution)/shard_map/ppermute | solution.py:468
  19.1 4.2 %collective-permute-start.4 = (f32[8,4,8,128]{3,2,1,0:T(8,128)S(1)}, f32[8,4,8,128]{3,2,1,0:T(8,128)S(1)}, u32[]{:S(2)}, u32[]{:S(2)}) collective-permute-start(f32[8,4,8,128]{3,2,1,0:T(8,128)S(1)} %get-tuple-element.35), channel_id=1, source_target_pairs={{0,8},{8,0},{16,24},{24,16},{32,40},{40,32},{48,56},{56,48},{64,72... | collective-permute-start | bytes 393224 | tf_op jit(solution)/shard_map/ppermute | solution.py:444
  20.9 6.6 %collective-permute-start.8 = (f32[4,4,8,128]{3,2,1,0:T(8,128)S(1)}, f32[4,4,8,128]{3,2,1,0:T(8,128)S(1)}, u32[]{:S(2)}, u32[]{:S(2)}) collective-permute-start(f32[4,4,8,128]{3,2,1,0:T(8,128)S(1)} %shard_map.74), channel_id=1, source_target_pairs={{0,1},{1,0},{2,3},{3,2},{4,5},{5,4},{6,7},{7,6},{8,9},{9,8},{10,11... | collective-permute-start | bytes 196616 | tf_op jit(solution)/shard_map/ppermute | solution.py:444
  23.3 5.7 %collective-permute-start.5 = (f32[4,4,8,128]{3,2,1,0:T(8,128)S(1)}, f32[4,4,8,128]{3,2,1,0:T(8,128)S(1)}, u32[]{:S(2)}, u32[]{:S(2)}) collective-permute-start(f32[4,4,8,128]{3,2,1,0:T(8,128)S(1)} %get-tuple-element.38), channel_id=1, source_target_pairs={{0,16},{8,24},{16,0},{24,8},{32,48},{40,56},{48,32},{56,40},{64,80... | collective-permute-start | bytes 196616 | tf_op jit(solution)/shard_map/ppermute | solution.py:444
  27.5 4.0 %collective-permute-start.9 = (f32[2,4,8,128]{3,2,1,0:T(8,128)S(1)}, f32[2,4,8,128]{3,2,1,0:T(8,128)S(1)}, u32[]{:S(2)}, u32[]{:S(2)}) collective-permute-start(f32[2,4,8,128]{3,2,1,0:T(8,128)S(1)} %get-tuple-element.45), channel_id=1, source_target_pairs={{0,2},{1,3},{2,0},{3,1},{4,6},{5,7},{6,4},{7,5},{8,10},{9,11},{10,... | collective-permute-start | bytes 98312 | tf_op jit(solution)/shard_map/ppermute | solution.py:444
  29.1 4.0 %collective-permute-start.6 = (f32[2,4,8,128]{3,2,1,0:T(8,128)S(1)}, f32[2,4,8,128]{3,2,1,0:T(8,128)S(1)}, u32[]{:S(2)}, u32[]{:S(2)}) collective-permute-start(f32[2,4,8,128]{3,2,1,0:T(8,128)S(1)} %get-tuple-element.40), channel_id=1, source_target_pairs={{0,32},{8,40},{16,48},{24,56},{32,0},{40,8},{48,16},{56,24},{64,96... | collective-permute-start | bytes 98312 | tf_op jit(solution)/shard_map/ppermute | solution.py:444
  31.5 5.0 %collective-permute-start.10 = (f32[1,4,8,128]{3,2,1,0:T(8,128)S(1)}, f32[1,4,8,128]{3,2,1,0:T(8,128)S(1)}, u32[]{:S(2)}, u32[]{:S(2)}) collective-permute-start(f32[1,4,8,128]{3,2,1,0:T(8,128)S(1)} %get-tuple-element.47), channel_id=1, source_target_pairs={{0,6},{1,7},{2,4},{3,5},{4,2},{5,3},{6,0},{7,1},{8,14},{9,15},{10,... | collective-permute-start | bytes 49160 | tf_op jit(solution)/shard_map/ppermute | solution.py:444
  33.1 5.0 %collective-permute-start.7 = (f32[1,4,8,128]{3,2,1,0:T(8,128)S(1)}, f32[1,4,8,128]{3,2,1,0:T(8,128)S(1)}, u32[]{:S(2)}, u32[]{:S(2)}) collective-permute-start(f32[1,4,8,128]{3,2,1,0:T(8,128)S(1)} %get-tuple-element.42), channel_id=1, source_target_pairs={{0,96},{8,104},{16,112},{24,120},{32,64},{40,72},{48,80},{56,88},{... | collective-permute-start | bytes 49160 | tf_op jit(solution)/shard_map/ppermute | solution.py:444

commit v6 on v5

--- a/solution.py
+++ b/solution.py
@@ -99,6 +99,11 @@
     rows = own_ref.shape[0]
     out_ref[pl.ds(0, rows), :] = own_ref[...]
     out_ref[pl.ds(rows, rows), :] = hopped_ref[...]
+
+
+def turn_kernel(own_ref, hopped_ref, out_ref):
+    middle = is_set("gx", 1) != is_set("gx", 2)
+    out_ref[...] = jnp.where(middle, own_ref[...], hopped_ref[...])
 
 
 def classify_kernel(step_len, parity, cells_ref, lut_ref, *refs):
@@ -317,6 +322,17 @@
     )(own, hopped)
 
 
+def turn(own, hopped):
+    return pl.pallas_call(
+        turn_kernel,
+        out_shape=floats(*own.shape),
+        in_specs=[VMEM, VMEM],
+        out_specs=VMEM,
+        name="turn",
+        **options(0.3),
+    )(own, hopped)
+
+
 def classify(cells, lut, step_len, part, *before):
     count_x, count_y, cells_z = cells.shape[0] - 2, cells.shape[1] - 2 * ROWS, cells.shape[2]
     return pl.pallas_call(
@@ -365,10 +381,9 @@
     )(emitted, field, *shifts)
 
 
-def neighbours(axis, offset):
+def ends(axis):
     count = lax.axis_size(axis)
-    pairs = [(i, i + 1) for i in range(offset, count - 1, 2)]
-    return pairs + [(target, source) for source, target in pairs]
+    return ([(i, i + 4) for i in range(3, count - 4, 4)] + [(i, i - 4) for i in range(4, count, 4)])
 
 
 def hops(axis):
@@ -464,8 +479,9 @@
                                                               shear_y, direction)
     inner = lax.ppermute(inner, "gx", swapped("gx", 1))
     hopped = lax.ppermute(hop, "gy", hops("gy"))
-    outer = lax.ppermute(outer, "gx", neighbours("gx", 1))
+    along = lax.ppermute(outer, "gx", ends("gx"))
     crossed = lax.ppermute(relay(own, hopped), "gy", swapped("gy", 1))
+    outer = lax.ppermute(turn(outer, along), "gx", swapped("gx", 3))
     field = classify(cells, lut, step_len, 0)
     field = classify(cells, lut, step_len, 1, field)
     emitted = shade(cells, field)

time: 38.9 us -> 41.3 us (1.062)
  the two profiles are of different devices: /device:TPU:24 before, /device:TPU:56 now
where the time goes in v6:
time: 41.3 us; the launch traced here: 41.2 us
  starting transfers between devices  16.6 us (40%)
  waiting for transfers between devices  12.4 us (30%)
  Pallas kernels  11.4 us (28%)
  between operations  0.76 us (2%)
    ppermute x7, starting transfers between devices, send(): self.got = lax.ppermute(give, self.axis, swapped(self.axis, mask))  10.4 us
    ppermute x7, waiting for transfers between devices, send(): self.got = lax.ppermute(give, self.axis, swapped(self.axis, mask))  8.65 us
    ppermute x1, waiting for transfers between devices, local(): hopped = lax.ppermute(hop, 'gy', hops('gy'))  3.79 us
    pallas_call x2, Pallas kernels, y_march(): pl.pallas_call(functools.partial(y_kernel, GROUP_Y, kept, *sizes), out_sh...  3.18 us
    pallas_call x1, Pallas kernels, x_march(): pl.pallas_call(functools.partial(x_kernel, GROUP_X), out_shape=(part, par...  3.03 us
    ppermute x1, starting transfers between devices, local(): crossed = lax.ppermute(relay(own, hopped), 'gy', swapped('gy', 1))  2.17 us
    pallas_call x2, Pallas kernels, classify(): pl.pallas_call(functools.partial(classify_kernel, step_len, part), out_sh...  2.06 us
    ppermute x1, starting transfers between devices, local(): outer = lax.ppermute(turn(outer, along), 'gx', swapped('gx', 3))  1.57 us
  transfers between devices with their start and end apart: 12, of which 5 were waited for; matrix products, arithmetic and copies ran while one was open for 0% of the time, Pallas kernels for 15%

profile of v6, /device:TPU:56, one launch (start us, length us, event | category | flops | bytes accessed | tf_op | source)
XLA Modules:
  0.0 41.2 jit_solution(5263078205040176371)
XLA Ops:
  0.6 1.4 %load.1 = (f32[34,80,128]{2,1,0:T(8,128)S(1)}, f32[64,128]{1,0:T(8,128)S(1)}, f32[64,128]{1,0:T(8,128)S(1)}, f32[32,128]{1,0:T(8,128)S(1)}, f32[32,128]{1,0:T(8,...) custom-call(f32[32,64,128]{2,1,0:T(8,128)} %density_ref.1, ...), custom_call_target="tpu_custom_call" | custom-call | bytes 7000000 | tf_op jit(solution)/shard_map/load/pallas_call | solution.py:294
  2.1 0.7 %collective-permute-start = (f32[64,128]{1,0:T(8,128)S(1)}, f32[64,128]{1,0:T(8,128)S(1)}, u32[]{:S(2)}, u32[]{:S(2)}) collective-permute-start(f32[64,128]{1,0:T(8,128)S(1)} %get-tuple-element.25.own_ref), channel_id=1, source_target_pairs={{24,56},{56,88},{88,120},{32,0},{64,32},{96,64},{25,57},{57,89},{8... | collective-permute-start | bytes 98312 | tf_op jit(solution)/shard_map/ppermute | solution.py:482
  2.8 1.3 %collective-permute-start.3 = (f32[32,128]{1,0:T(8,128)S(1)}, f32[32,128]{1,0:T(8,128)S(1)}, u32[]{:S(2)}, u32[]{:S(2)}) collective-permute-start(f32[32,128]{1,0:T(8,128)S(1)} %get-tuple-element.28), channel_id=1, source_target_pairs={{1,3},{2,0},{3,5},{4,2},{5,7},{6,4},{9,11},{10,8},{11,13},{12,10},... | collective-permute-start | bytes 49160 | tf_op jit(solution)/shard_map/ppermute | solution.py:481
  4.1 0.5 %collective-permute-start.2 = (f32[64,128]{1,0:T(8,128)S(1)}, f32[64,128]{1,0:T(8,128)S(1)}, u32[]{:S(2)}, u32[]{:S(2)}) collective-permute-start(f32[64,128]{1,0:T(8,128)S(1)} %get-tuple-element.26), channel_id=1, source_target_pairs={{0,8},{8,0},{16,24},{24,16},{32,40},{40,32},{48,56},{56,48},{64,72... | collective-permute-start | bytes 98312 | tf_op jit(solution)/shard_map/ppermute | solution.py:480
  4.6 3.8 %collective-permute-done.3.hopped_ref = f32[32,128]{1,0:T(8,128)S(1)} collective-permute-done((f32[32,128]{1,0:T(8,128)S(1)}, f32[32,128]{1,0:T(8,128)S(1)}, u32[]{:S(2)}, u32[]{:S(2)}) %collective-permute-start.3) | collective-permute-done | bytes 16416 | tf_op jit(solution)/shard_map/ppermute | solution.py:481
  8.4 2.2 %collective-permute-start.4 = (f32[64,128]{1,0:T(8,128)S(1)}, f32[64,128]{1,0:T(8,128)S(1)}, u32[]{:S(2)}, u32[]{:S(2)}) collective-permute-start(f32[64,128]{1,0:T(8,128)S(1)} %relay.1), channel_id=1, source_target_pairs={{0,1},{1,0},{2,3},{3,2},{4,5},{5,4},{6,7},{7,6},{8,9},{9,8},{10,11... | collective-permute-start | bytes 98312 | tf_op jit(solution)/shard_map/ppermute | solution.py:483
  10.6 0.0 collective-permute-done.hopped_ref
  10.6 1.6 %collective-permute-start.1 = (f32[64,128]{1,0:T(8,128)S(1)}, f32[64,128]{1,0:T(8,128)S(1)}, u32[]{:S(2)}, u32[]{:S(2)}) collective-permute-start(f32[64,128]{1,0:T(8,128)S(1)} %turn.1), channel_id=1, source_target_pairs={{0,24},{8,16},{16,8},{24,0},{32,56},{40,48},{48,40},{56,32},{64,88... | collective-permute-start | bytes 98312 | tf_op jit(solution)/shard_map/ppermute | solution.py:484
  12.2 1.0 %shard_map.68.refs_0_ = f32[4,2080,128]{2,1,0:T(8,128)S(1)} custom-call(f32[34,80,128]{2,1,0:T(8,128)S(1)} %get-tuple-element.29.cells_ref._cells, f32[4,8,128]{2,1,0:T(8,128)S(1)} %get-tuple-element.30.lut_ref), custom_call_target="tpu_custom_call" | custom-call | bytes 5250000 | tf_op jit(solution)/shard_map/pallas_call | solution.py:338
  13.2 1.0 %shard_map.69.field_ref = f32[4,2080,128]{2,1,0:T(8,128)S(1)} custom-call(f32[34,80,128]{2,1,0:T(8,128)S(1)} %get-tuple-element.29.cells_ref._cells, f32[4,8,128]{2,1,0:T(8,128)S(1)} %get-tuple-element.30.lut_ref, f32[4,2080,128]{2,1,0:T(8,128)S(1)} %shard_map.68.refs_0_), custom_call_target="tpu_custom_call", output_to_operand_aliasing={{}: (2, {})} | custom-call | bytes 5250000 | tf_op jit(solution)/shard_map/pallas_call | solution.py:338
  14.2 0.9 %shade.1._emit = f32[3,2080,128]{2,1,0:T(8,128)S(1)} custom-call(f32[34,80,128]{2,1,0:T(8,128)S(1)} %get-tuple-element.29.cells_ref._cells, f32[4,2080,128]{2,1,0:T(8,128)S(1)} %shard_map.69.field_ref), custom_call_target="tpu_custom_call" | custom-call | bytes 7000000 | tf_op jit(solution)/shard_map/shade/pallas_call | solution.py:349
  15.1 0.0 collective-permute-done.2.face_xb_ref
  15.1 0.0 collective-permute-done.4.crossed_ref
  15.1 0.0 collective-permute-done.1.face_xa_ref
  15.1 3.0 %x_march.1 = (f32[8,4,8,128]{3,2,1,0:T(8,128)S(1)}, f32[8,4,8,128]{3,2,1,0:T(8,128)S(1)}, f32[3,2080,128]{2,1,0:T(8,128)S(1)}, f32[34,80,128]{2,1,0:T(8,128)S(1)}) custom-call(f32[64,128]{1,0:T(8,128)S(1)} %collective-permute-done.1.face_xa_ref, f32[64,128]{1,0:T(8,128)S(1)} %collective-permute-done.2.face_xb_ref, ...), custom_call_target="tpu_custom_call", output_to_operand_aliasing={{3}: (7, {}), {2}: (8, {})} | custom-call | bytes 14000000 | tf_op jit(solution)/shard_map/x_march/pallas_call | solution.py:362
  18.2 1.7 %collective-permute-start.5 = (f32[8,4,8,128]{3,2,1,0:T(8,128)S(1)}, f32[8,4,8,128]{3,2,1,0:T(8,128)S(1)}, u32[]{:S(2)}, u32[]{:S(2)}) collective-permute-start(f32[8,4,8,128]{3,2,1,0:T(8,128)S(1)} %get-tuple-element.35), channel_id=1, source_target_pairs={{0,8},{8,0},{16,24},{24,16},{32,40},{40,32},{48,56},{56,48},{64,72... | collective-permute-start | bytes 393224 | tf_op jit(solution)/shard_map/ppermute | solution.py:459
  19.9 1.6 %shard_map.74 = f32[4,4,8,128]{3,2,1,0:T(8,128)S(1)} custom-call(f32[3,2080,128]{2,1,0:T(8,128)S(1)} %get-tuple-element.43.emit_ref, f32[4,2080,128]{2,1,0:T(8,128)S(1)} %shard_map.69.field_ref, s32[192,8,128]{2,1,0:T(8,128)S(1)} %get-tuple-element.31.index_ref, f32[192,8,128]{2,1,0:T(8,128)S(1)} %get-tuple-element.32.mask_ref, ...), custom_call_target="tpu_custom_call" | custom-call | bytes 8750000 | tf_op jit(solution)/shard_map/pallas_call | solution.py:375
  21.5 0.1 collective-permute-start.9
  21.6 0.0 collective-permute-done.5.got_ref
  21.7 2.2 %collective-permute-start.6 = (f32[4,4,8,128]{3,2,1,0:T(8,128)S(1)}, f32[4,4,8,128]{3,2,1,0:T(8,128)S(1)}, u32[]{:S(2)}, u32[]{:S(2)}) collective-permute-start(f32[4,4,8,128]{3,2,1,0:T(8,128)S(1)} %get-tuple-element.38), channel_id=1, source_target_pairs={{0,16},{8,24},{16,0},{24,8},{32,48},{40,56},{48,32},{56,40},{64,80... | collective-permute-start | bytes 196616 | tf_op jit(solution)/shard_map/ppermute | solution.py:459
  23.9 1.6 %shard_map.73.keep_ref = f32[4,4,8,128]{3,2,1,0:T(8,128)S(1)} custom-call(f32[3,2080,128]{2,1,0:T(8,128)S(1)} %get-tuple-element.43.emit_ref, f32[4,2080,128]{2,1,0:T(8,128)S(1)} %shard_map.69.field_ref, s32[192,8,128]{2,1,0:T(8,128)S(1)} %get-tuple-element.31.index_ref, f32[192,8,128]{2,1,0:T(8,128)S(1)} %get-tuple-element.32.mask_ref, ...), custom_call_target="tpu_custom_call" | custom-call | bytes 8750000 | tf_op jit(solution)/shard_map/pallas_call | solution.py:375
  25.4 2.4 %collective-permute-done.9.got_ref = f32[4,4,8,128]{3,2,1,0:T(8,128)S(1)} collective-permute-done((f32[4,4,8,128]{3,2,1,0:T(8,128)S(1)}, f32[4,4,8,128]{3,2,1,0:T(8,128)S(1)}, u32[]{:S(2)}, u32[]{:S(2)}) %collective-permute-start.9) | collective-permute-done | bytes 65568 | tf_op jit(solution)/shard_map/ppermute | solution.py:459
  27.9 2.4 %collective-permute-start.10 = (f32[2,4,8,128]{3,2,1,0:T(8,128)S(1)}, f32[2,4,8,128]{3,2,1,0:T(8,128)S(1)}, u32[]{:S(2)}, u32[]{:S(2)}) collective-permute-start(f32[2,4,8,128]{3,2,1,0:T(8,128)S(1)} %get-tuple-element.45), channel_id=1, source_target_pairs={{0,2},{1,3},{2,0},{3,1},{4,6},{5,7},{6,4},{7,5},{8,10},{9,11},{10,... | collective-permute-start | bytes 98312 | tf_op jit(solution)/shard_map/ppermute | solution.py:459
  30.2 0.0 collective-permute-done.6.got_ref
  30.3 0.5 %collective-permute-start.7 = (f32[2,4,8,128]{3,2,1,0:T(8,128)S(1)}, f32[2,4,8,128]{3,2,1,0:T(8,128)S(1)}, u32[]{:S(2)}, u32[]{:S(2)}) collective-permute-start(f32[2,4,8,128]{3,2,1,0:T(8,128)S(1)} %get-tuple-element.40), channel_id=1, source_target_pairs={{0,32},{8,40},{16,48},{24,56},{32,0},{40,8},{48,16},{56,24},{64,96... | collective-permute-start | bytes 98312 | tf_op jit(solution)/shard_map/ppermute | solution.py:459
  30.8 1.3 %collective-permute-done.10.got_ref = f32[2,4,8,128]{3,2,1,0:T(8,128)S(1)} collective-permute-done((f32[2,4,8,128]{3,2,1,0:T(8,128)S(1)}, f32[2,4,8,128]{3,2,1,0:T(8,128)S(1)}, u32[]{:S(2)}, u32[]{:S(2)}) %collective-permute-start.10) | collective-permute-done | bytes 32800 | tf_op jit(solution)/shard_map/ppermute | solution.py:459
  32.1 3.4 %collective-permute-start.11 = (f32[1,4,8,128]{3,2,1,0:T(8,128)S(1)}, f32[1,4,8,128]{3,2,1,0:T(8,128)S(1)}, u32[]{:S(2)}, u32[]{:S(2)}) collective-permute-start(f32[1,4,8,128]{3,2,1,0:T(8,128)S(1)} %get-tuple-element.47), channel_id=1, source_target_pairs={{0,6},{1,7},{2,4},{3,5},{4,2},{5,3},{6,0},{7,1},{8,14},{9,15},{10,... | collective-permute-start | bytes 49160 | tf_op jit(solution)/shard_map/ppermute | solution.py:459
  35.5 0.0 collective-permute-done.7.got_ref
  35.5 0.1 collective-permute-start.8
  35.6 1.6 %collective-permute-done.11.got_y_ref = f32[1,4,8,128]{3,2,1,0:T(8,128)S(1)} collective-permute-done((f32[1,4,8,128]{3,2,1,0:T(8,128)S(1)}, f32[1,4,8,128]{3,2,1,0:T(8,128)S(1)}, u32[]{:S(2)}, u32[]{:S(2)}) %collective-permute-start.11) | collective-permute-done | bytes 16416 | tf_op jit(solution)/shard_map/ppermute | solution.py:459
  37.2 3.3 %collective-permute-done.8.got_x_ref = f32[1,4,8,128]{3,2,1,0:T(8,128)S(1)} collective-permute-done((f32[1,4,8,128]{3,2,1,0:T(8,128)S(1)}, f32[1,4,8,128]{3,2,1,0:T(8,128)S(1)}, u32[]{:S(2)}, u32[]{:S(2)}) %collective-permute-start.8) | collective-permute-done | bytes 16416 | tf_op jit(solution)/shard_map/ppermute | solution.py:459
  40.6 0.6 %images.1 = (f32[2,4,4,128]{3,2,1,0:T(4,128)}, f32[2,4,4,128]{3,2,1,0:T(4,128)}) custom-call(f32[1,4,8,128]{3,2,1,0:T(8,128)S(1)} %get-tuple-element.41.keep_x_ref, f32[1,4,8,128]{3,2,1,0:T(8,128)S(1)} %collective-permute-done.8.got_x_ref, f32[1,4,8,128]{3,2,1,0:T(8,128)S(1)} %get-tuple-element.46.keep_y_ref, ...), custom_call_target="tpu_custom_call" | custom-call | bytes 1050000 | tf_op jit(solution)/shard_map/images/pallas_call | solution.py:418
  (7 shorter events, 0.1 us)
Async XLA Ops:
  2.1 8.5 %collective-permute-start = (f32[64,128]{1,0:T(8,128)S(1)}, f32[64,128]{1,0:T(8,128)S(1)}, u32[]{:S(2)}, u32[]{:S(2)}) collective-permute-start(f32[64,128]{1,0:T(8,128)S(1)} %get-tuple-element.25.own_ref), channel_id=1, source_target_pairs={{24,56},{56,88},{88,120},{32,0},{64,32},{96,64},{25,57},{57,89},{8... | collective-permute-start | bytes 98312 | tf_op jit(solution)/shard_map/ppermute | solution.py:482
  2.8 5.6 %collective-permute-start.3 = (f32[32,128]{1,0:T(8,128)S(1)}, f32[32,128]{1,0:T(8,128)S(1)}, u32[]{:S(2)}, u32[]{:S(2)}) collective-permute-start(f32[32,128]{1,0:T(8,128)S(1)} %get-tuple-element.28), channel_id=1, source_target_pairs={{1,3},{2,0},{3,5},{4,2},{5,7},{6,4},{9,11},{10,8},{11,13},{12,10},... | collective-permute-start | bytes 49160 | tf_op jit(solution)/shard_map/ppermute | solution.py:481
  4.1 11.1 %collective-permute-start.2 = (f32[64,128]{1,0:T(8,128)S(1)}, f32[64,128]{1,0:T(8,128)S(1)}, u32[]{:S(2)}, u32[]{:S(2)}) collective-permute-start(f32[64,128]{1,0:T(8,128)S(1)} %get-tuple-element.26), channel_id=1, source_target_pairs={{0,8},{8,0},{16,24},{24,16},{32,40},{40,32},{48,56},{56,48},{64,72... | collective-permute-start | bytes 98312 | tf_op jit(solution)/shard_map/ppermute | solution.py:480
  8.4 6.7 %collective-permute-start.4 = (f32[64,128]{1,0:T(8,128)S(1)}, f32[64,128]{1,0:T(8,128)S(1)}, u32[]{:S(2)}, u32[]{:S(2)}) collective-permute-start(f32[64,128]{1,0:T(8,128)S(1)} %relay.1), channel_id=1, source_target_pairs={{0,1},{1,0},{2,3},{3,2},{4,5},{5,4},{6,7},{7,6},{8,9},{9,8},{10,11... | collective-permute-start | bytes 98312 | tf_op jit(solution)/shard_map/ppermute | solution.py:483
  10.6 4.6 %collective-permute-start.1 = (f32[64,128]{1,0:T(8,128)S(1)}, f32[64,128]{1,0:T(8,128)S(1)}, u32[]{:S(2)}, u32[]{:S(2)}) collective-permute-start(f32[64,128]{1,0:T(8,128)S(1)} %turn.1), channel_id=1, source_target_pairs={{0,24},{8,16},{16,8},{24,0},{32,56},{40,48},{48,40},{56,32},{64,88... | collective-permute-start | bytes 98312 | tf_op jit(solution)/shard_map/ppermute | solution.py:484
  18.2 3.4 %collective-permute-start.5 = (f32[8,4,8,128]{3,2,1,0:T(8,128)S(1)}, f32[8,4,8,128]{3,2,1,0:T(8,128)S(1)}, u32[]{:S(2)}, u32[]{:S(2)}) collective-permute-start(f32[8,4,8,128]{3,2,1,0:T(8,128)S(1)} %get-tuple-element.35), channel_id=1, source_target_pairs={{0,8},{8,0},{16,24},{24,16},{32,40},{40,32},{48,56},{56,48},{64,72... | collective-permute-start | bytes 393224 | tf_op jit(solution)/shard_map/ppermute | solution.py:459
  21.5 6.3 %collective-permute-start.9 = (f32[4,4,8,128]{3,2,1,0:T(8,128)S(1)}, f32[4,4,8,128]{3,2,1,0:T(8,128)S(1)}, u32[]{:S(2)}, u32[]{:S(2)}) collective-permute-start(f32[4,4,8,128]{3,2,1,0:T(8,128)S(1)} %shard_map.74), channel_id=1, source_target_pairs={{0,1},{1,0},{2,3},{3,2},{4,5},{5,4},{6,7},{7,6},{8,9},{9,8},{10,11... | collective-permute-start | bytes 196616 | tf_op jit(solution)/shard_map/ppermute | solution.py:459
  21.7 8.6 %collective-permute-start.6 = (f32[4,4,8,128]{3,2,1,0:T(8,128)S(1)}, f32[4,4,8,128]{3,2,1,0:T(8,128)S(1)}, u32[]{:S(2)}, u32[]{:S(2)}) collective-permute-start(f32[4,4,8,128]{3,2,1,0:T(8,128)S(1)} %get-tuple-element.38), channel_id=1, source_target_pairs={{0,16},{8,24},{16,0},{24,8},{32,48},{40,56},{48,32},{56,40},{64,80... | collective-permute-start | bytes 196616 | tf_op jit(solution)/shard_map/ppermute | solution.py:459
  27.9 4.3 %collective-permute-start.10 = (f32[2,4,8,128]{3,2,1,0:T(8,128)S(1)}, f32[2,4,8,128]{3,2,1,0:T(8,128)S(1)}, u32[]{:S(2)}, u32[]{:S(2)}) collective-permute-start(f32[2,4,8,128]{3,2,1,0:T(8,128)S(1)} %get-tuple-element.45), channel_id=1, source_target_pairs={{0,2},{1,3},{2,0},{3,1},{4,6},{5,7},{6,4},{7,5},{8,10},{9,11},{10,... | collective-permute-start | bytes 98312 | tf_op jit(solution)/shard_map/ppermute | solution.py:459
  30.3 5.2 %collective-permute-start.7 = (f32[2,4,8,128]{3,2,1,0:T(8,128)S(1)}, f32[2,4,8,128]{3,2,1,0:T(8,128)S(1)}, u32[]{:S(2)}, u32[]{:S(2)}) collective-permute-start(f32[2,4,8,128]{3,2,1,0:T(8,128)S(1)} %get-tuple-element.40), channel_id=1, source_target_pairs={{0,32},{8,40},{16,48},{24,56},{32,0},{40,8},{48,16},{56,24},{64,96... | collective-permute-start | bytes 98312 | tf_op jit(solution)/shard_map/ppermute | solution.py:459
  32.1 5.1 %collective-permute-start.11 = (f32[1,4,8,128]{3,2,1,0:T(8,128)S(1)}, f32[1,4,8,128]{3,2,1,0:T(8,128)S(1)}, u32[]{:S(2)}, u32[]{:S(2)}) collective-permute-start(f32[1,4,8,128]{3,2,1,0:T(8,128)S(1)} %get-tuple-element.47), channel_id=1, source_target_pairs={{0,6},{1,7},{2,4},{3,5},{4,2},{5,3},{6,0},{7,1},{8,14},{9,15},{10,... | collective-permute-start | bytes 49160 | tf_op jit(solution)/shard_map/ppermute | solution.py:459
  35.5 5.0 %collective-permute-start.8 = (f32[1,4,8,128]{3,2,1,0:T(8,128)S(1)}, f32[1,4,8,128]{3,2,1,0:T(8,128)S(1)}, u32[]{:S(2)}, u32[]{:S(2)}) collective-permute-start(f32[1,4,8,128]{3,2,1,0:T(8,128)S(1)} %get-tuple-element.42), channel_id=1, source_target_pairs={{0,96},{8,104},{16,112},{24,120},{32,64},{40,72},{48,80},{56,88},{... | collective-permute-start | bytes 49160 | tf_op jit(solution)/shard_map/ppermute | solution.py:459

commit v7 on v5

--- a/solution.py
+++ b/solution.py
@@ -14,7 +14,7 @@
 PACK = 1024.0
 ROUNDER = 12582912.0
 GROUP_X, GROUP_Y = 4, 2
-UNROLL_C, UNROLL_E, UNROLL_F, UNROLL_X, UNROLL_Y = 16, 32, 30, 32, 64
+UNROLL_C, UNROLL_E, UNROLL_X, UNROLL_Y = 16, 32, 32, 64
 
 VMEM = pl.BlockSpec(memory_space=pltpu.VMEM)
 HBM = pl.BlockSpec(memory_space=pltpu.HBM)
@@ -170,19 +170,8 @@
         emit_ref[c, rows, :] = field_ref[c, rows, :] * shaded
 
 
-def shade_kernel(cells_ref, field_ref, emit_ref):
-    count_x, count_y = cells_ref.shape[0] - 2, cells_ref.shape[1] - 2 * ROWS
-
-    def body(i, carry):
-        for base in range(0, count_y, ROWS):
-            emission(cells_ref, field_ref, emit_ref, i, base)
-        return carry
-
-    lax.fori_loop(0, count_x, body, 0, unroll=UNROLL_E)
-
-
 def x_kernel(group, face_xa_ref, face_xb_ref, crossed_ref, field_ref, index_ref,
-             mask_ref, turned_ref, _cells, _emit, keep_ref, give_ref, emit_ref, cells_ref):
+             mask_ref, turned_ref, _cells, keep_ref, give_ref, emit_ref, cells_ref):
     count_x, cells_z = cells_ref.shape[0] - 2, cells_ref.shape[2]
     count_y = cells_ref.shape[1] - 2 * ROWS
     pitch = field_ref.shape[1] // count_x
@@ -201,16 +190,13 @@
 
     turned = [turned_ref[v] != 0 for v in range(2)]
     zeros = jnp.zeros((ROWS, cells_z), jnp.float32)
-    for i in (0, count_x - 1):
+
+    def shade(i, carry):
         for base in range(0, count_y, ROWS):
             emission(cells_ref, field_ref, emit_ref, i, base)
-
-    def edges(i, carry):
-        for base in (0, count_y - ROWS):
-            emission(cells_ref, field_ref, emit_ref, i, base)
         return carry
 
-    lax.fori_loop(1, count_x - 1, edges, 0, unroll=UNROLL_F)
+    lax.fori_loop(0, count_x, shade, 0, unroll=UNROLL_E)
 
     def block_of(block, carry):
         base = pl.multiple_of(block * (ROWS * group), ROWS)
@@ -329,29 +315,18 @@
     )(cells, lut, *before)
 
 
-def shade(cells, field):
-    return pl.pallas_call(
-        shade_kernel,
-        out_shape=floats(3, *field.shape[1:]),
-        in_specs=[VMEM, VMEM],
-        out_specs=VMEM,
-        name="shade",
-        **options(2),
-    )(cells, field)
-
-
-def x_march(cells, halo, field, shifts, emitted):
+def x_march(cells, halo, field, shifts):
     count_y, cells_z = cells.shape[1] - 2 * ROWS, cells.shape[2]
     part = floats(count_y // (2 * PIECE), 4, 2 * PIECE, cells_z)
     return pl.pallas_call(
         functools.partial(x_kernel, GROUP_X),
-        out_shape=(part, part, floats(*emitted.shape), floats(*cells.shape)),
-        in_specs=[VMEM] * 9,
+        out_shape=(part, part, floats(3, *field.shape[1:]), floats(*cells.shape)),
+        in_specs=[VMEM] * 8,
         out_specs=(VMEM,) * 4,
-        input_output_aliases={7: 3, 8: 2},
+        input_output_aliases={7: 3},
         name="x_march",
         **options(4),
-    )(*halo, field, *shifts, cells, emitted)[:3]
+    )(*halo, field, *shifts, cells)[:3]
 
 
 def y_march(emitted, field, shifts, sizes, kept):
@@ -468,9 +443,8 @@
     crossed = lax.ppermute(relay(own, hopped), "gy", swapped("gy", 1))
     field = classify(cells, lut, step_len, 0)
     field = classify(cells, lut, step_len, 1, field)
-    emitted = shade(cells, field)
     halo = (outer, inner, crossed)
-    keep_x, give_x, emitted = x_march(cells, halo, field, shifts, emitted)
+    keep_x, give_x, emitted = x_march(cells, halo, field, shifts)
 
     x, y = Exchange("gx", 0, ahead), Exchange("gy", len(STAGES[0][1]), ahead)
     x.send(keep_x, give_x, 1)

time: 38.9 us -> 38.8 us (level)
  starting transfers between devices: 17.1 us -> 18.7 us
  waiting for transfers between devices: 9.5 us -> 8.29 us
  Pallas kernels: 11.4 us -> 11 us
    ppermute x7, starting transfers between devices: 6.4 us -> 7.95 us  [send(): self.got = lax.ppermute(give, self.axis, swapped(self.axis, mask))]
    ppermute x7, waiting for transfers between devices: 9.19 us -> 7.98 us  [send(): self.got = lax.ppermute(give, self.axis, swapped(self.axis, mask))]
    pallas_call x1 -> x0, Pallas kernels: 0.89 us -> none  [shade(): pl.pallas_call(shade_kernel, out_shape=floats(3, *field.shape[1:]), in_sp...]
    pallas_call x1, Pallas kernels: 3.03 us -> 3.55 us  [x_march(): pl.pallas_call(functools.partial(x_kernel, GROUP_X), out_shape=(part, par...]
  transfers between devices with their start and end apart: 11 -> 11, of which waited for: 6 -> 5; matrix products, arithmetic and copies ran while one was open for 0% -> 0% of each run, Pallas kernels for 16% -> 14%
where the time goes in v7:
time: 38.8 us; the launch traced here: 38.7 us
  starting transfers between devices  18.7 us (48%)
  Pallas kernels  11 us (28%)
  waiting for transfers between devices  8.29 us (21%)
  between operations  0.75 us (2%)
    ppermute x7, waiting for transfers between devices, send(): self.got = lax.ppermute(give, self.axis, swapped(self.axis, mask))  7.98 us
    ppermute x7, starting transfers between devices, send(): self.got = lax.ppermute(give, self.axis, swapped(self.axis, mask))  7.95 us
    ppermute x1, starting transfers between devices, local(): crossed = lax.ppermute(relay(own, hopped), 'gy', swapped('gy', 1))  5.39 us
    pallas_call x1, Pallas kernels, x_march(): pl.pallas_call(functools.partial(x_kernel, GROUP_X), out_shape=(part, par...  3.55 us
    ppermute x1, starting transfers between devices, local(): outer = lax.ppermute(outer, 'gx', neighbours('gx', 1))  3.45 us
    pallas_call x2, Pallas kernels, y_march(): pl.pallas_call(functools.partial(y_kernel, GROUP_Y, kept, *sizes), out_sh...  3.2 us
    pallas_call x2, Pallas kernels, classify(): pl.pallas_call(functools.partial(classify_kernel, step_len, part), out_sh...  2.05 us
    pallas_call x1, Pallas kernels, load(): pl.pallas_call(functools.partial(load_kernel, STAGES), out_shape=(floats(...  1.45 us
  transfers between devices with their start and end apart: 11, of which 5 were waited for; matrix products, arithmetic and copies ran while one was open for 0% of the time, Pallas kernels for 14%

profile of v7, /device:TPU:24, one launch (start us, length us, event | category | flops | bytes accessed | tf_op | source)
XLA Modules:
  0.0 38.7 jit_solution(17430285582903689957)
XLA Ops:
  0.6 1.4 %load.1 = (f32[34,80,128]{2,1,0:T(8,128)S(1)}, f32[64,128]{1,0:T(8,128)S(1)}, f32[64,128]{1,0:T(8,128)S(1)}, f32[32,128]{1,0:T(8,128)S(1)}, f32[32,128]{1,0:T(8,...) custom-call(f32[32,64,128]{2,1,0:T(8,128)} %density_ref.1, ...), custom_call_target="tpu_custom_call" | custom-call | bytes 7000000 | tf_op jit(solution)/shard_map/load/pallas_call | solution.py:275
  2.1 1.3 %collective-permute-start.2 = (f32[32,128]{1,0:T(8,128)S(1)}, f32[32,128]{1,0:T(8,128)S(1)}, u32[]{:S(2)}, u32[]{:S(2)}) collective-permute-start(f32[32,128]{1,0:T(8,128)S(1)} %get-tuple-element.28), channel_id=1, source_target_pairs={{1,3},{2,0},{3,5},{4,2},{5,7},{6,4},{9,11},{10,8},{11,13},{12,10},... | collective-permute-start | bytes 49160 | tf_op jit(solution)/shard_map/ppermute | solution.py:441
  3.4 3.4 %collective-permute-start = (f32[64,128]{1,0:T(8,128)S(1)}, f32[64,128]{1,0:T(8,128)S(1)}, u32[]{:S(2)}, u32[]{:S(2)}) collective-permute-start(f32[64,128]{1,0:T(8,128)S(1)} %get-tuple-element.25), channel_id=1, source_target_pairs={{8,16},{24,32},{40,48},{56,64},{72,80},{88,96},{104,112},{16,8},{3... | collective-permute-start | bytes 98312 | tf_op jit(solution)/shard_map/ppermute | solution.py:442
  6.8 0.6 %collective-permute-start.1 = (f32[64,128]{1,0:T(8,128)S(1)}, f32[64,128]{1,0:T(8,128)S(1)}, u32[]{:S(2)}, u32[]{:S(2)}) collective-permute-start(f32[64,128]{1,0:T(8,128)S(1)} %get-tuple-element.26), channel_id=1, source_target_pairs={{0,8},{8,0},{16,24},{24,16},{32,40},{40,32},{48,56},{56,48},{64,72... | collective-permute-start | bytes 98312 | tf_op jit(solution)/shard_map/ppermute | solution.py:440
  7.4 0.3 collective-permute-done.2.hopped_ref
  7.7 5.4 %collective-permute-start.3 = (f32[64,128]{1,0:T(8,128)S(1)}, f32[64,128]{1,0:T(8,128)S(1)}, u32[]{:S(2)}, u32[]{:S(2)}) collective-permute-start(f32[64,128]{1,0:T(8,128)S(1)} %relay.1), channel_id=1, source_target_pairs={{0,1},{1,0},{2,3},{3,2},{4,5},{5,4},{6,7},{7,6},{8,9},{9,8},{10,11... | collective-permute-start | bytes 98312 | tf_op jit(solution)/shard_map/ppermute | solution.py:443
  13.1 1.0 %shard_map.68.refs_0_ = f32[4,2080,128]{2,1,0:T(8,128)S(1)} custom-call(f32[34,80,128]{2,1,0:T(8,128)S(1)} %get-tuple-element.29.cells_ref._cells, f32[4,8,128]{2,1,0:T(8,128)S(1)} %get-tuple-element.30.lut_ref), custom_call_target="tpu_custom_call" | custom-call | bytes 5250000 | tf_op jit(solution)/shard_map/pallas_call | solution.py:308
  14.1 1.0 %shard_map.69.field_ref = f32[4,2080,128]{2,1,0:T(8,128)S(1)} custom-call(f32[34,80,128]{2,1,0:T(8,128)S(1)} %get-tuple-element.29.cells_ref._cells, f32[4,8,128]{2,1,0:T(8,128)S(1)} %get-tuple-element.30.lut_ref, f32[4,2080,128]{2,1,0:T(8,128)S(1)} %shard_map.68.refs_0_), custom_call_target="tpu_custom_call", output_to_operand_aliasing={{}: (2, {})} | custom-call | bytes 5250000 | tf_op jit(solution)/shard_map/pallas_call | solution.py:308
  15.2 0.0 collective-permute-done.face_xa_ref
  15.2 0.0 collective-permute-done.1.face_xb_ref
  15.2 0.0 collective-permute-done.3.crossed_ref
  15.2 3.6 %x_march.1 = (f32[8,4,8,128]{3,2,1,0:T(8,128)S(1)}, f32[8,4,8,128]{3,2,1,0:T(8,128)S(1)}, f32[3,2080,128]{2,1,0:T(8,128)S(1)}, f32[34,80,128]{2,1,0:T(8,128)S(1)}) custom-call(f32[64,128]{1,0:T(8,128)S(1)} %collective-permute-done.face_xa_ref, f32[64,128]{1,0:T(8,128)S(1)} %collective-permute-done.1.face_xb_ref, ...), custom_call_target="tpu_custom_call", output_to_operand_aliasing={{3}: (7, {})} | custom-call | bytes 14000000 | tf_op jit(solution)/shard_map/x_march/pallas_call | solution.py:321
  18.8 0.1 collective-permute-start.4
  18.8 1.6 %shard_map.74 = f32[4,4,8,128]{3,2,1,0:T(8,128)S(1)} custom-call(f32[3,2080,128]{2,1,0:T(8,128)S(1)} %get-tuple-element.43.emit_ref, f32[4,2080,128]{2,1,0:T(8,128)S(1)} %shard_map.69.field_ref, s32[192,8,128]{2,1,0:T(8,128)S(1)} %get-tuple-element.31.index_ref, f32[192,8,128]{2,1,0:T(8,128)S(1)} %get-tuple-element.32.mask_ref, ...), custom_call_target="tpu_custom_call" | custom-call | bytes 8750000 | tf_op jit(solution)/shard_map/pallas_call | solution.py:334
  20.5 3.3 %collective-permute-start.8 = (f32[4,4,8,128]{3,2,1,0:T(8,128)S(1)}, f32[4,4,8,128]{3,2,1,0:T(8,128)S(1)}, u32[]{:S(2)}, u32[]{:S(2)}) collective-permute-start(f32[4,4,8,128]{3,2,1,0:T(8,128)S(1)} %shard_map.74), channel_id=1, source_target_pairs={{0,1},{1,0},{2,3},{3,2},{4,5},{5,4},{6,7},{7,6},{8,9},{9,8},{10,11... | collective-permute-start | bytes 196616 | tf_op jit(solution)/shard_map/ppermute | solution.py:419
  23.8 0.0 collective-permute-done.4.got_ref
  23.9 0.1 collective-permute-start.5
  24.0 1.6 %shard_map.73.keep_ref = f32[4,4,8,128]{3,2,1,0:T(8,128)S(1)} custom-call(f32[3,2080,128]{2,1,0:T(8,128)S(1)} %get-tuple-element.43.emit_ref, f32[4,2080,128]{2,1,0:T(8,128)S(1)} %shard_map.69.field_ref, s32[192,8,128]{2,1,0:T(8,128)S(1)} %get-tuple-element.31.index_ref, f32[192,8,128]{2,1,0:T(8,128)S(1)} %get-tuple-element.32.mask_ref, ...), custom_call_target="tpu_custom_call" | custom-call | bytes 8750000 | tf_op jit(solution)/shard_map/pallas_call | solution.py:334
  25.5 1.5 %collective-permute-done.8.got_ref = f32[4,4,8,128]{3,2,1,0:T(8,128)S(1)} collective-permute-done((f32[4,4,8,128]{3,2,1,0:T(8,128)S(1)}, f32[4,4,8,128]{3,2,1,0:T(8,128)S(1)}, u32[]{:S(2)}, u32[]{:S(2)}) %collective-permute-start.8) | collective-permute-done | bytes 65568 | tf_op jit(solution)/shard_map/ppermute | solution.py:419
  27.1 1.6 %collective-permute-start.9 = (f32[2,4,8,128]{3,2,1,0:T(8,128)S(1)}, f32[2,4,8,128]{3,2,1,0:T(8,128)S(1)}, u32[]{:S(2)}, u32[]{:S(2)}) collective-permute-start(f32[2,4,8,128]{3,2,1,0:T(8,128)S(1)} %get-tuple-element.45), channel_id=1, source_target_pairs={{0,2},{1,3},{2,0},{3,1},{4,6},{5,7},{6,4},{7,5},{8,10},{9,11},{10,... | collective-permute-start | bytes 98312 | tf_op jit(solution)/shard_map/ppermute | solution.py:419
  28.6 0.0 collective-permute-done.5.got_ref
  28.7 0.9 %collective-permute-start.6 = (f32[2,4,8,128]{3,2,1,0:T(8,128)S(1)}, f32[2,4,8,128]{3,2,1,0:T(8,128)S(1)}, u32[]{:S(2)}, u32[]{:S(2)}) collective-permute-start(f32[2,4,8,128]{3,2,1,0:T(8,128)S(1)} %get-tuple-element.40), channel_id=1, source_target_pairs={{0,32},{8,40},{16,48},{24,56},{32,0},{40,8},{48,16},{56,24},{64,96... | collective-permute-start | bytes 98312 | tf_op jit(solution)/shard_map/ppermute | solution.py:419
  29.5 1.5 %collective-permute-done.9.got_ref = f32[2,4,8,128]{3,2,1,0:T(8,128)S(1)} collective-permute-done((f32[2,4,8,128]{3,2,1,0:T(8,128)S(1)}, f32[2,4,8,128]{3,2,1,0:T(8,128)S(1)}, u32[]{:S(2)}, u32[]{:S(2)}) %collective-permute-start.9) | collective-permute-done | bytes 32800 | tf_op jit(solution)/shard_map/ppermute | solution.py:419
  31.1 1.9 %collective-permute-start.10 = (f32[1,4,8,128]{3,2,1,0:T(8,128)S(1)}, f32[1,4,8,128]{3,2,1,0:T(8,128)S(1)}, u32[]{:S(2)}, u32[]{:S(2)}) collective-permute-start(f32[1,4,8,128]{3,2,1,0:T(8,128)S(1)} %get-tuple-element.47), channel_id=1, source_target_pairs={{0,6},{1,7},{2,4},{3,5},{4,2},{5,3},{6,0},{7,1},{8,14},{9,15},{10,... | collective-permute-start | bytes 49160 | tf_op jit(solution)/shard_map/ppermute | solution.py:419
  33.0 0.0 collective-permute-done.6.got_ref
  33.0 0.1 collective-permute-start.7
  33.1 3.0 %collective-permute-done.10.got_y_ref = f32[1,4,8,128]{3,2,1,0:T(8,128)S(1)} collective-permute-done((f32[1,4,8,128]{3,2,1,0:T(8,128)S(1)}, f32[1,4,8,128]{3,2,1,0:T(8,128)S(1)}, u32[]{:S(2)}, u32[]{:S(2)}) %collective-permute-start.10) | collective-permute-done | bytes 16416 | tf_op jit(solution)/shard_map/ppermute | solution.py:419
  36.1 1.9 %collective-permute-done.7.got_x_ref = f32[1,4,8,128]{3,2,1,0:T(8,128)S(1)} collective-permute-done((f32[1,4,8,128]{3,2,1,0:T(8,128)S(1)}, f32[1,4,8,128]{3,2,1,0:T(8,128)S(1)}, u32[]{:S(2)}, u32[]{:S(2)}) %collective-permute-start.7) | collective-permute-done | bytes 16416 | tf_op jit(solution)/shard_map/ppermute | solution.py:419
  38.0 0.6 %images.1 = (f32[2,4,4,128]{3,2,1,0:T(4,128)}, f32[2,4,4,128]{3,2,1,0:T(4,128)}) custom-call(f32[1,4,8,128]{3,2,1,0:T(8,128)S(1)} %get-tuple-element.41.keep_x_ref, f32[1,4,8,128]{3,2,1,0:T(8,128)S(1)} %collective-permute-done.7.got_x_ref, f32[1,4,8,128]{3,2,1,0:T(8,128)S(1)} %get-tuple-element.46.keep_y_ref, ...), custom_call_target="tpu_custom_call" | custom-call | bytes 1050000 | tf_op jit(solution)/shard_map/images/pallas_call | solution.py:378
  (6 shorter events, 0.1 us)
Async XLA Ops:
  2.1 5.6 %collective-permute-start.2 = (f32[32,128]{1,0:T(8,128)S(1)}, f32[32,128]{1,0:T(8,128)S(1)}, u32[]{:S(2)}, u32[]{:S(2)}) collective-permute-start(f32[32,128]{1,0:T(8,128)S(1)} %get-tuple-element.28), channel_id=1, source_target_pairs={{1,3},{2,0},{3,5},{4,2},{5,7},{6,4},{9,11},{10,8},{11,13},{12,10},... | collective-permute-start | bytes 49160 | tf_op jit(solution)/shard_map/ppermute | solution.py:441
  3.4 11.8 %collective-permute-start = (f32[64,128]{1,0:T(8,128)S(1)}, f32[64,128]{1,0:T(8,128)S(1)}, u32[]{:S(2)}, u32[]{:S(2)}) collective-permute-start(f32[64,128]{1,0:T(8,128)S(1)} %get-tuple-element.25), channel_id=1, source_target_pairs={{8,16},{24,32},{40,48},{56,64},{72,80},{88,96},{104,112},{16,8},{3... | collective-permute-start | bytes 98312 | tf_op jit(solution)/shard_map/ppermute | solution.py:442
  6.8 8.3 %collective-permute-start.1 = (f32[64,128]{1,0:T(8,128)S(1)}, f32[64,128]{1,0:T(8,128)S(1)}, u32[]{:S(2)}, u32[]{:S(2)}) collective-permute-start(f32[64,128]{1,0:T(8,128)S(1)} %get-tuple-element.26), channel_id=1, source_target_pairs={{0,8},{8,0},{16,24},{24,16},{32,40},{40,32},{48,56},{56,48},{64,72... | collective-permute-start | bytes 98312 | tf_op jit(solution)/shard_map/ppermute | solution.py:440
  7.7 7.5 %collective-permute-start.3 = (f32[64,128]{1,0:T(8,128)S(1)}, f32[64,128]{1,0:T(8,128)S(1)}, u32[]{:S(2)}, u32[]{:S(2)}) collective-permute-start(f32[64,128]{1,0:T(8,128)S(1)} %relay.1), channel_id=1, source_target_pairs={{0,1},{1,0},{2,3},{3,2},{4,5},{5,4},{6,7},{7,6},{8,9},{9,8},{10,11... | collective-permute-start | bytes 98312 | tf_op jit(solution)/shard_map/ppermute | solution.py:443
  18.8 5.1 %collective-permute-start.4 = (f32[8,4,8,128]{3,2,1,0:T(8,128)S(1)}, f32[8,4,8,128]{3,2,1,0:T(8,128)S(1)}, u32[]{:S(2)}, u32[]{:S(2)}) collective-permute-start(f32[8,4,8,128]{3,2,1,0:T(8,128)S(1)} %get-tuple-element.35), channel_id=1, source_target_pairs={{0,8},{8,0},{16,24},{24,16},{32,40},{40,32},{48,56},{56,48},{64,72... | collective-permute-start | bytes 393224 | tf_op jit(solution)/shard_map/ppermute | solution.py:419
  20.5 6.5 %collective-permute-start.8 = (f32[4,4,8,128]{3,2,1,0:T(8,128)S(1)}, f32[4,4,8,128]{3,2,1,0:T(8,128)S(1)}, u32[]{:S(2)}, u32[]{:S(2)}) collective-permute-start(f32[4,4,8,128]{3,2,1,0:T(8,128)S(1)} %shard_map.74), channel_id=1, source_target_pairs={{0,1},{1,0},{2,3},{3,2},{4,5},{5,4},{6,7},{7,6},{8,9},{9,8},{10,11... | collective-permute-start | bytes 196616 | tf_op jit(solution)/shard_map/ppermute | solution.py:419
  23.9 4.8 %collective-permute-start.5 = (f32[4,4,8,128]{3,2,1,0:T(8,128)S(1)}, f32[4,4,8,128]{3,2,1,0:T(8,128)S(1)}, u32[]{:S(2)}, u32[]{:S(2)}) collective-permute-start(f32[4,4,8,128]{3,2,1,0:T(8,128)S(1)} %get-tuple-element.38), channel_id=1, source_target_pairs={{0,16},{8,24},{16,0},{24,8},{32,48},{40,56},{48,32},{56,40},{64,80... | collective-permute-start | bytes 196616 | tf_op jit(solution)/shard_map/ppermute | solution.py:419
  27.1 4.0 %collective-permute-start.9 = (f32[2,4,8,128]{3,2,1,0:T(8,128)S(1)}, f32[2,4,8,128]{3,2,1,0:T(8,128)S(1)}, u32[]{:S(2)}, u32[]{:S(2)}) collective-permute-start(f32[2,4,8,128]{3,2,1,0:T(8,128)S(1)} %get-tuple-element.45), channel_id=1, source_target_pairs={{0,2},{1,3},{2,0},{3,1},{4,6},{5,7},{6,4},{7,5},{8,10},{9,11},{10,... | collective-permute-start | bytes 98312 | tf_op jit(solution)/shard_map/ppermute | solution.py:419
  28.7 4.3 %collective-permute-start.6 = (f32[2,4,8,128]{3,2,1,0:T(8,128)S(1)}, f32[2,4,8,128]{3,2,1,0:T(8,128)S(1)}, u32[]{:S(2)}, u32[]{:S(2)}) collective-permute-start(f32[2,4,8,128]{3,2,1,0:T(8,128)S(1)} %get-tuple-element.40), channel_id=1, source_target_pairs={{0,32},{8,40},{16,48},{24,56},{32,0},{40,8},{48,16},{56,24},{64,96... | collective-permute-start | bytes 98312 | tf_op jit(solution)/shard_map/ppermute | solution.py:419
  31.1 5.0 %collective-permute-start.10 = (f32[1,4,8,128]{3,2,1,0:T(8,128)S(1)}, f32[1,4,8,128]{3,2,1,0:T(8,128)S(1)}, u32[]{:S(2)}, u32[]{:S(2)}) collective-permute-start(f32[1,4,8,128]{3,2,1,0:T(8,128)S(1)} %get-tuple-element.47), channel_id=1, source_target_pairs={{0,6},{1,7},{2,4},{3,5},{4,2},{5,3},{6,0},{7,1},{8,14},{9,15},{10,... | collective-permute-start | bytes 49160 | tf_op jit(solution)/shard_map/ppermute | solution.py:419
  33.0 5.0 %collective-permute-start.7 = (f32[1,4,8,128]{3,2,1,0:T(8,128)S(1)}, f32[1,4,8,128]{3,2,1,0:T(8,128)S(1)}, u32[]{:S(2)}, u32[]{:S(2)}) collective-permute-start(f32[1,4,8,128]{3,2,1,0:T(8,128)S(1)} %get-tuple-element.42), channel_id=1, source_target_pairs={{0,96},{8,104},{16,112},{24,120},{32,64},{40,72},{48,80},{56,88},{... | collective-permute-start | bytes 49160 | tf_op jit(solution)/shard_map/ppermute | solution.py:419
